TPU v7x, 32 devices: a whole 2x2x4 slice. The times are simulated.
32 devices in a mesh: grp: 4 (over z), grid: 8 (over y, x, core).
Axes of the slice: x: 2, y: 2, z: 4, core: 2. Of those that a mesh axis runs over, the one named last changes fastest.
Arguments:
- vectors: float32 [4, 3, 2, 32, 256, 256], P('grp', None, None, 'grid'), may hold values from -6 to 6
- potential: float32 [32, 256, 256], P('grid'), may hold values from 0.1 to 2
- added_field: float32 [4, 32, 256, 256], P('grp', 'grid'), may hold values from -3 to 3
- qp_states: bfloat16 [32, 32, 256, 256], P(None, 'grid'), may hold values from -0.00390625 to 0.00390625
Outputs:
- elements: float32 [4, 32, 6], P('grp', 'grid')
All inputs are finite; a program needn't handle non-finite values.
Results may differ from a plain program's by a relative error of at most 0.0033.
Values sent between devices are 32-bit elements; how exact they have to be, the bound alone decides.
No kernel may reach another device: no remote copies, remote signals or barrier semaphores. Data moves between devices by JAX's collectives and lax.ppermute only.
A program may use at most 256 MiB of HBM per device.

v0:
```python
import functools

import jax
import jax.numpy as jnp
from jax import lax
from jax.experimental import pallas as pl
from jax.experimental.pallas import tpu as pltpu
from jax.sharding import PartitionSpec as P


ORDER = 4
LANES = 128
SUBS = 8
SHARES = (6, 10, 10, 6)

time_step = 0.2
four_pi = 12.566370614359172
highest = lax.Precision.HIGHEST


def sine_table(length):
    indices = jnp.arange(length, dtype=jnp.int32) + 1
    products = indices[:, None] * indices[None, :] % (2 * (length + 1))
    return jnp.sqrt(2.0 / (length + 1)) * jnp.sin(
        jnp.pi * products.astype(jnp.float32) / (length + 1)
    )


def edge_rows(first, last):
    sub = lax.broadcasted_iota(jnp.int32, first.shape, 0)
    before = jnp.where(sub == 0, 0.0, pltpu.roll(last, 1, 0))
    after = jnp.where(sub == SUBS - 1, 0.0, pltpu.roll(first, SUBS - 1, 0))
    return before, after


def across_lanes(tiles):
    shape = tiles[0].shape
    lane = lax.broadcasted_iota(jnp.int32, shape, len(shape) - 1)
    up = [pltpu.roll(t, 1, len(shape) - 1) for t in tiles]
    down = [pltpu.roll(t, LANES - 1, len(shape) - 1) for t in tiles]
    sums = []
    for m in range(len(tiles)):
        low = up[m - 1] if m > 0 else 0.0
        high = down[m + 1] if m < len(tiles) - 1 else 0.0
        sums.append(
            jnp.where(lane == 0, low, up[m]) + jnp.where(lane == LANES - 1, high, down[m])
        )
    return sums


def neighbour_sum(ref, lead, p, r0, n):
    block = ref[lead + (p, pl.ds(r0, n + 2))]
    x_low = ref[lead + (p - 1, pl.ds(r0 + 1, n))]
    x_high = ref[lead + (p + 1, pl.ds(r0 + 1, n))]
    centre = block[1:-1]
    plain = (block[2:] + block[:-2]) + (x_low + x_high)
    tiles = block.shape[-1] // LANES
    cut = lambda a, m: a[..., m * LANES : (m + 1) * LANES]
    z_sums = across_lanes([cut(centre, m) for m in range(tiles)])
    total = jnp.concatenate([cut(plain, m) + z_sums[m] for m in range(tiles)], axis=-1)
    return centre, total


def spans(size_y, shares):
    edges = [0]
    for share in shares:
        edges.append(edges[-1] + share * size_y // sum(shares))
    found, low = [], 0
    for o0, o1 in zip(edges[:-1], edges[1:]):
        high = min(o1 + SUBS, size_y)
        found.append(((o0, o1), (low, high), (max(o0 - SUBS, 0), high)))
        low = high
    return found


def pieces(rows):
    count = -(-rows // 5)
    sizes = [rows // count + (1 if j < rows % count else 0) for j in range(count)]
    starts = [sum(sizes[:j]) for j in range(count)]
    return list(zip(starts, sizes))


def taylor_kernel(
    span, sources, planes, first_call, flag_ref, mask_ref, own_ref, pot_ref, add_ref, mate_ref,
    mate_pot, mate_add, *refs
):
    out_rows, _, window = span
    msgs, refs = refs[: 2 * len(sources)], refs[2 * len(sources) :]
    if not first_call:
        refs = refs[1:]
    b_ref, rho_out, x_in, f_in, b_out, r_out, u0, u1, u2, u3, w, acc, f_sems, x_sems, o_sems = refs
    s = 0.5 * time_step
    halo = ORDER
    tiles, n_fields = x_in.shape[:2]
    n_vectors = n_fields // 2
    height = window[1] - window[0]
    rows = height // SUBS
    reach = [planes + 2 * (halo - k) for k in range(ORDER + 1)]
    lanes = lambda m: pl.ds(m * LANES, LANES)

    def own_copies(source, target, sem):
        at = pl.ds(window[0], height)
        return [
            (pltpu.make_async_copy(source.at[:, at, lanes(m)], target(m, pl.ds(0, height)), sem()), None, None)
            for m in range(tiles)
        ]

    def halo_copies(side, p0, n, mate, target, sem):
        found = []
        for j, ((start, size), to) in enumerate(sources):
            ref, p = msgs[2 * j], p0
            if not isinstance(p0, int):
                ref, p = msgs[2 * j + 1], 0
            elif p0 >= ref.shape[0]:
                ref, p = msgs[2 * j + 1], p0 - ref.shape[0]
            first = mate.shape[0] - n if side == "low" else 0
            for m in range(tiles):
                goal, done = target(m, pl.ds(to, size)), sem()
                near = pltpu.make_async_copy(
                    mate.at[pl.ds(first, n), pl.ds(window[0] + to, size), lanes(m)], goal, done
                )
                far = pltpu.make_async_copy(
                    ref.at[pl.ds(p, n), pl.ds(start, size), lanes(m)], goal, done
                )
                found.append((near, far, flag_ref[0 if side == "low" else 1]))
        return found

    def counter(sems, first=0):
        used = [0]

        def sem():
            used[0] += 1
            return sems.at[first + used[0] - 1]

        return sem

    def field_copies():
        sem, found = counter(f_sems), []
        for which, (ref, mate) in enumerate(((pot_ref, mate_pot), (add_ref, mate_add))):
            p0 = n_fields * planes + which * (halo - 1)
            for side, to in (("low", 0), ("high", halo - 1 + planes)):
                goal = lambda m, at, to=to: f_in.at[m, which, pl.ds(to, halo - 1), at]
                found += halo_copies(side, p0, halo - 1, mate, goal, sem)
            goal = lambda m, at: f_in.at[m, which, pl.ds(halo - 1, planes), at]
            found += own_copies(ref, goal, sem)
        return found

    per_vector = x_sems.shape[0] // n_vectors

    def vector_copies(i):
        sem, found = counter(x_sems, i * per_vector), []
        for part in range(2):
            j = 2 * i + part
            for side, to in (("low", 0), ("high", halo + planes)):
                goal = lambda m, at, to=to: x_in.at[m, j, pl.ds(to, halo), at]
                found += halo_copies(side, j * planes, halo, mate_ref.at[j], goal, sem)
            goal = lambda m, at: x_in.at[m, j, pl.ds(halo, planes), at]
            found += own_copies(own_ref.at[j], goal, sem)
        return found

    def start(copies):
        for near, far, flag in copies:
            if far is None:
                near.start()
            else:
                pl.when(flag == 0)(near.start)
                pl.when(flag == 1)(far.start)

    def wait(copies):
        for near, _, _ in copies:
            near.wait()

    start(field_copies())
    for i in range(n_vectors):
        start(vector_copies(i))

    def gather(ref, lead, r):
        at = pl.ds(r, SUBS, stride=rows)
        return jnp.concatenate([ref[(m,) + lead + (at, slice(None))] for m in range(tiles)], axis=1)

    def scatter(ref, lead, r, value):
        at = pl.ds(r, SUBS, stride=rows)
        for m in range(tiles):
            ref[(m,) + lead + (at, slice(None))] = value[:, m * LANES : (m + 1) * LANES]

    wait(field_copies())

    def load_w(q, carry):
        for r in range(rows):
            pot = 2.0 * gather(f_in, (0, q), r) + 6.0
            w[0, q, r] = pot
            w[1, q, r] = pot + 2.0 * gather(f_in, (1, q), r)
        return carry

    lax.fori_loop(0, reach[1], load_w, 0)
    acc[...] = jnp.zeros_like(acc)

    def finish(ref, lead):
        before, after = edge_rows(ref[lead + (1,)], ref[lead + (rows,)])
        ref[lead + (0,)] = before
        ref[lead + (rows + 1,)] = after

    def inside(p, k):
        side = halo - k
        low = jnp.where(p < side, mask_ref[0], 1.0)
        return jnp.where(p >= side + planes, mask_ref[1], low)

    out_count = out_rows[1] - out_rows[0]
    inner = pl.ds(out_rows[0] - window[0], out_count)

    def b_copies(i):
        return [
            pltpu.make_async_copy(
                b_out.at[m, pl.ds(2 * i, 2), :, inner],
                b_ref.at[pl.ds(2 * i, 2), :, pl.ds(out_rows[0], out_count), lanes(m)],
                o_sems.at[i * tiles + m],
            )
            for m in range(tiles)
        ]

    def vector(i, carry):
        wait(vector_copies(i))

        def load_field(q, carry):
            for part in range(2):
                for r in range(rows):
                    u0[part, q, r + 1] = gather(x_in, (2 * i + part, q), r)
                finish(u0, (part, q))
            return carry

        lax.fori_loop(0, reach[0], load_field, 0)

        def order_1(p, carry):
            keep = inside(p, 1)
            for part in range(2):
                for r0, n in pieces(rows):
                    centre, total = neighbour_sum(u0, (part,), p + 1, r0, n)
                    for stack in range(2):
                        u1[2 * stack + part, p, pl.ds(r0 + 1, n)] = keep * (
                            total - w[stack, p, pl.ds(r0, n)] * centre
                        )
            for chain in range(4):
                finish(u1, (chain, p))
            return carry

        lax.fori_loop(0, reach[1], order_1, 0)
        for k, source, target in ((2, u1, u2), (3, u2, u3)):

            def order_k(p, carry, k=k, source=source, target=target):
                keep = inside(p, k)
                for chain in range(4):
                    for r0, n in pieces(rows):
                        centre, total = neighbour_sum(source, (chain,), p + 1, r0, n)
                        target[chain, p, pl.ds(r0 + 1, n)] = keep * (
                            total - w[chain // 2, p + k - 1, pl.ds(r0, n)] * centre
                        )
                    finish(target, (chain, p))
                return carry

            lax.fori_loop(0, reach[k], order_k, 0)

        def last(p, carry):
            for r0, n in pieces(rows):
                at = pl.ds(r0 + 1, n)
                plain = pl.ds(r0, n)
                rho = acc[p, plain]
                for stack in range(2):
                    ev, od = [], []
                    for part in range(2):
                        chain = 2 * stack + part
                        centre, total = neighbour_sum(u3, (chain,), p + 1, r0, n)
                        fourth = total - w[stack, p + 3, plain] * centre
                        ev.append(
                            u0[part, p + 4, at]
                            - (s**2 / 2) * u2[chain, p + 2, at]
                            + (s**4 / 24) * fourth
                        )
                        od.append(s * u1[chain, p + 3, at] - (s**3 / 6) * centre)
                    real, imag = ev[0] - od[1], od[0] + ev[1]
                    size = real * real + imag * imag
                    rho = rho + size if stack else rho - size
                acc[p, plain] = rho
                for j in range(n):
                    scatter(b_out, (2 * i, p), r0 + j, real[j])
                    scatter(b_out, (2 * i + 1, p), r0 + j, imag[j])
            return carry

        lax.fori_loop(0, planes, last, 0)
        for copy in b_copies(i):
            copy.start()
        return carry

    lax.fori_loop(0, n_vectors, vector, 0)

    def spread(p, carry):
        for r in range(rows):
            scatter(r_out, (p,), r, acc[p, r])
        return carry

    lax.fori_loop(0, planes, spread, 0)
    out = [
        pltpu.make_async_copy(
            r_out.at[m, :, inner], rho_out.at[:, :, lanes(m)], o_sems.at[n_vectors * tiles + m]
        )
        for m in range(tiles)
    ]
    for copy in out:
        copy.start()
    for i in range(n_vectors):
        out += b_copies(i)
    for copy in out:
        copy.wait()


def taylor(span, flags, mask, own, potential, added, mates, sources, b):
    n_fields, planes, _, size_z = own.shape
    out_rows, _, window = span
    height = window[1] - window[0]
    rows = height // SUBS
    tiles = size_z // LANES
    held = lambda *lead: pltpu.VMEM(lead + (rows + 2, SUBS, size_z), jnp.float32)
    plain = lambda *lead: pltpu.VMEM(lead + (rows, SUBS, size_z), jnp.float32)
    natural = lambda *lead: pltpu.VMEM((tiles,) + lead + (height, LANES), jnp.float32)
    hbm = pl.BlockSpec(memory_space=pl.ANY)
    smem = pl.BlockSpec(memory_space=pltpu.SMEM)
    shape = [(piece, to) for _, piece, to in sources]
    operands = [own, potential, added, *mates] + [m for msgs, _, _ in sources for m in msgs]
    aliases = {}
    if b is not None:
        operands.append(b)
        aliases = {2 + len(operands) - 1: 0}
    return pl.pallas_call(
        functools.partial(taylor_kernel, span, shape, planes, b is None),
        out_shape=(
            jax.ShapeDtypeStruct(own.shape, jnp.float32),
            jax.ShapeDtypeStruct((planes, out_rows[1] - out_rows[0], size_z), jnp.float32),
        ),
        in_specs=[smem, smem] + [hbm] * len(operands),
        out_specs=(hbm, hbm),
        input_output_aliases=aliases,
        scratch_shapes=[
            natural(n_fields, planes + 8),
            natural(2, planes + 6),
            natural(n_fields, planes),
            natural(planes),
            held(2, planes + 8),
            held(4, planes + 6),
            held(4, planes + 4),
            held(4, planes + 2),
            plain(2, planes + 6),
            plain(planes),
            pltpu.SemaphoreType.DMA((tiles * (2 + 4 * len(sources)),)),
            pltpu.SemaphoreType.DMA((tiles * n_fields * (1 + 2 * len(sources)),)),
            pltpu.SemaphoreType.DMA((tiles * (n_fields // 2 + 1),)),
        ],
        cost_estimate=pl.CostEstimate(
            flops=rows * SUBS * size_z * planes * 120000, transcendentals=0, bytes_accessed=20 << 20
        ),
        name="taylor",
    )(flags, mask, *operands)


def elements_kernel(n_states, parts, last_step, rec_ref, add_ref, b_ref, q_ref, out_ref, acc):
    step = pl.program_id(0) * pl.num_programs(1) + pl.program_id(1)

    @pl.when(step == 0)
    def _():
        acc[...] = jnp.zeros_like(acc)

    field = rec_ref[0] + add_ref[0]
    group = 16
    total = acc[...]
    for g in range(field.shape[0] // group):
        at = slice(g * group, (g + 1) * group)
        weighted = [field[at] * b_ref[j, 0, at] for j in range(parts)]
        weighted = jnp.concatenate(weighted, axis=0).astype(jnp.bfloat16)
        states = q_ref[:, 0, at].reshape(n_states * group, field.shape[-1])
        total += lax.dot_general(
            states, weighted, (((1,), (1,)), ((), ())), preferred_element_type=jnp.float32
        )
    acc[...] = total

    @pl.when(step == last_step)
    def _():
        found = acc[...].reshape(n_states, group, parts * group)
        row = lax.broadcasted_iota(jnp.int32, found.shape, 1)
        col = lax.broadcasted_iota(jnp.int32, found.shape, 2)
        own = jnp.sum(jnp.where(row == col % group, found, 0.0), axis=1)
        fold_r = lax.broadcasted_iota(jnp.int32, (parts * group, parts), 0)
        fold_c = lax.broadcasted_iota(jnp.int32, (parts * group, parts), 1)
        fold = jnp.where(fold_r // group == fold_c, 1.0, 0.0)
        out_ref[...] = jnp.dot(own, fold, precision=highest, preferred_element_type=jnp.float32)


def elements(received, added, b, states):
    n_states, planes, size_y, size_z = states.shape
    block = 64
    parts = b.shape[0]
    grid = (planes, size_y // block)
    field = pl.BlockSpec((1, block, size_z), lambda p, y: (p, y, 0))
    vec = pl.BlockSpec((parts, 1, block, size_z), lambda p, y: (0, p, y, 0))
    return pl.pallas_call(
        functools.partial(elements_kernel, n_states, parts, planes * (size_y // block) - 1),
        grid=grid,
        out_shape=jax.ShapeDtypeStruct((n_states, parts), jnp.float32),
        in_specs=[field, field]
        + [vec]
        + [pl.BlockSpec((n_states, 1, block, size_z), lambda p, y: (0, p, y, 0))],
        out_specs=pl.BlockSpec((n_states, parts), lambda p, y: (0, 0)),
        scratch_shapes=[pltpu.VMEM((n_states * 16, parts * 16), jnp.float32)],
        name="elements",
    )(received, added, b, states)


def moments_kernel(f_ref, low_ref, high_ref, r_ref, to_right, to_left):
    planes = f_ref.shape[0]

    def step(q, carry):
        at = pl.ds(pl.multiple_of(q * SUBS, SUBS), SUBS)
        r = r_ref[at, :]
        up = low_ref[0, at, :] * f_ref[0, at, :]
        for j in range(1, planes):
            up = r * up + low_ref[j, at, :] * f_ref[j, at, :]
        down = high_ref[planes - 1, at, :] * f_ref[planes - 1, at, :]
        for j in range(planes - 2, -1, -1):
            down = r * down + high_ref[j, at, :] * f_ref[j, at, :]
        to_right[at, :] = up
        to_left[at, :] = down
        return carry

    lax.fori_loop(0, f_ref.shape[1] // SUBS, step, 0, unroll=4)


def solve_kernel(n_far, side_ref, f_ref, low_ref, high_ref, r_ref, scale_ref, *refs):
    far, decay, out = refs[:n_far], refs[n_far : 2 * n_far], refs[2 * n_far]
    planes = f_ref.shape[0]

    def step(q, carry):
        at = pl.ds(pl.multiple_of(q * SUBS, SUBS), SUBS)
        r = r_ref[at, :]
        up, down = jnp.zeros_like(r), jnp.zeros_like(r)
        for k in range(n_far):
            value = decay[k][at, :] * far[k][at, :]
            up = up + side_ref[k] * value
            down = down + (1.0 - side_ref[k]) * value
        below = []
        for j in range(planes):
            up = r * up + low_ref[j, at, :] * f_ref[j, at, :]
            below.append(up)
        for j in range(planes - 1, -1, -1):
            down = r * down
            out[j, at, :] = scale_ref[at, :] * (
                high_ref[j, at, :] * below[j] + low_ref[j, at, :] * down
            )
            down = down + high_ref[j, at, :] * f_ref[j, at, :]
        return carry

    lax.fori_loop(0, f_ref.shape[1] // SUBS, step, 0, unroll=2)


class Poisson:
    def __init__(self, planes, size_y, size_z):
        self.count = lax.axis_size("grid")
        self.place = lax.axis_index("grid")
        self.chip, self.core = self.place // 2, self.place % 2
        self.first = self.core == 0
        self.planes, self.half = planes, size_z // 2
        self.table_y, self.table_z = sine_table(size_y), sine_table(size_z)
        full_x = planes * self.count
        sine_half = lambda n: jnp.sin(
            (0.5 * jnp.pi / (n + 1)) * (jnp.arange(n, dtype=jnp.int32) + 1).astype(jnp.float32)
        )
        of_y = 4.0 * sine_half(size_y) ** 2
        of_z = self.pick(4.0 * sine_half(size_z) ** 2, True)
        mu = of_y[:, None] + of_z[None, :]
        root = jnp.sqrt(mu + 0.25 * mu * mu)
        theta = jnp.log1p(0.5 * mu + root)
        self.r = jnp.exp(-theta)
        x = (2 * planes * self.chip + jnp.arange(2 * planes)).astype(jnp.float32)[:, None, None]
        self.low = -jnp.expm1(-2.0 * theta * (x + 1.0))
        self.high = -jnp.expm1(-2.0 * theta * (full_x - x))
        self.scale = four_pi / (-2.0 * root * jnp.expm1(-2.0 * (full_x + 1) * theta))
        self.hops = list(range(1, self.count // 2))
        other = [self.chip ^ k for k in self.hops]
        self.side = jnp.stack([o < self.chip for o in other]).astype(jnp.float32)
        self.decay = [
            jnp.exp(-(2.0 * planes) * theta * (jnp.abs(o - self.chip) - 1).astype(jnp.float32))
            for o in other
        ]
        self.total = 0.0

    def pick(self, array, mine):
        take = self.first if mine else jnp.logical_not(self.first)
        return jnp.where(take, array[..., : self.half], array[..., self.half :])

    def swap(self, array):
        return lax.ppermute(array, "grid", [(i, i ^ 1) for i in range(self.count)])

    def transform_z(self, density):
        return jnp.einsum("xyz,zl->xyl", density, self.table_z, precision=highest)

    def add(self, piece, at):
        mine, got = self.pick(piece, True), self.swap(self.pick(piece, False))
        both = jnp.where(
            self.first, jnp.concatenate([mine, got]), jnp.concatenate([got, mine])
        )
        rows = self.table_y[at : at + piece.shape[1]]
        self.total += jnp.einsum("xyl,yk->xkl", both, rows, precision=highest)

    def solve(self):
        shape = jax.ShapeDtypeStruct(self.r.shape, jnp.float32)
        vmem = pl.BlockSpec(memory_space=pltpu.VMEM)
        to_right, to_left = pl.pallas_call(
            moments_kernel,
            out_shape=(shape, shape),
            in_specs=[vmem] * 4,
            out_specs=(vmem, vmem),
            name="moments",
        )(self.total, self.low, self.high, self.r)
        far = []
        for k in self.hops:
            sent = jnp.where((self.chip ^ k) > self.chip, to_right, to_left)
            far.append(
                lax.ppermute(sent, "grid", [(i, i ^ (2 * k)) for i in range(self.count)])
            )
        field = pl.pallas_call(
            functools.partial(solve_kernel, len(far)),
            out_shape=jax.ShapeDtypeStruct(self.total.shape, jnp.float32),
            in_specs=[pl.BlockSpec(memory_space=pltpu.SMEM)] + [vmem] * (5 + 2 * len(far)),
            out_specs=vmem,
            name="solve",
        )(self.side, self.total, self.low, self.high, self.r, self.scale, *far, *self.decay)
        field = jnp.einsum("xkl,ky->xyl", field, self.table_y, precision=highest)
        lower, upper = field[: self.planes], field[self.planes :]
        mine = jnp.where(self.first, lower, upper)
        got = self.swap(jnp.where(self.first, upper, lower))
        flip = lambda mine: self.pick(self.table_z.T, mine).T
        back = lambda part, table: jnp.einsum("xyl,lz->xyz", part, table, precision=highest)
        return back(mine, flip(True)) + back(got, flip(False))


def scatter_sum(value, axis):
    count = lax.axis_size(axis)
    place = lax.axis_index(axis)
    step = count // 2
    while step:
        half = value.shape[0] // 2
        upper = (place // step) % 2 == 1
        low, high = value[:half], value[half:]
        pairs = [(i, i ^ step) for i in range(count)]
        sent = lax.ppermute(jnp.where(upper, low, high), axis, pairs)
        value = jnp.where(upper, high, low) + sent
        step //= 2
    return value


def on_device(vectors, potential, added_field, qp_states):
    own = vectors.reshape((-1,) + vectors.shape[3:])
    added = added_field[0]
    count = lax.axis_size("grid")
    groups = lax.axis_size("grp")
    place = lax.axis_index("grid")
    n_fields, planes, size_y, size_z = own.shape
    assert planes == ORDER and n_fields == 6
    assert count % 2 == 0
    mask = jnp.stack([place > 0, place < count - 1]).astype(jnp.float32)
    even = place % 2 == 0
    flags = jnp.stack([even, jnp.logical_not(even)]).astype(jnp.int32)
    mate_pairs = [(i, i ^ 1) for i in range(count)]
    chip_pairs = []
    for i in range(1, count - 1, 2):
        chip_pairs += [(i, i + 1), (i + 1, i)]
    relayed = count == 8
    left, right = count // 2 - 1, count // 2
    first_leg = [(left, count - 1), (right, 0)]
    second_leg = [(count - 1, right), (0, left)]
    layout = spans(size_y, SHARES)
    split = 4

    def message(lo, hi):
        edge = lambda f: jnp.where(even, f[:-1, lo:hi], f[1:, lo:hi])
        parts = [own[split:, :, lo:hi].reshape(-1, hi - lo, size_z), edge(potential), edge(added)]
        return jnp.concatenate(parts)

    cut = layout[0][1][1]
    hops = [None] * len(layout)
    if relayed:
        hops[0] = lax.ppermute(message(0, cut), "grid", first_leg)
    messages = []
    mates = None
    for c, (_, (lo, hi), _) in enumerate(layout):
        block = own[:split, :, lo:hi].reshape(-1, hi - lo, size_z)
        direct = lax.ppermute(block, "grid", chip_pairs)
        rest, pairs = message(lo, hi), chip_pairs
        if mates is None:
            mates = [lax.ppermute(f, "grid", mate_pairs) for f in (own, potential, added)]
        if relayed:
            if c == 1:
                late = lax.ppermute(message(cut, size_y), "grid", first_leg)
                hops[1:] = [late[:, l - cut : h - cut] for _, (l, h), _ in layout[1:]]
            ends = jnp.logical_or(place == 0, place == count - 1)
            rest = jnp.where(ends, hops[c], rest)
            pairs = [p for p in chip_pairs if set(p) != {left, right}] + second_leg
        messages.append((direct, lax.ppermute(rest, "grid", pairs)))

    poisson = Poisson(planes, size_y, size_z)
    group_pairs = [(g, g + groups // 2) for g in range(groups // 2)]
    b, arrived = None, []
    for c, span in enumerate(layout):
        _, (lo, hi), window = span
        sources = []
        if c:
            before = layout[c - 1][1]
            sources.append((messages[c - 1], (window[0] - before[0], lo - window[0]), 0))
        sources.append((messages[c], (0, hi - lo), lo - window[0]))
        if c >= 2:
            b, arrived[c - 2] = lax.optimization_barrier((b, arrived[c - 2]))
        if c == len(layout) - 1:
            b, arrived[c - 1] = lax.optimization_barrier((b, arrived[c - 1]))
        b, rho = taylor(span, flags, mask, own, potential, added, mates, sources, b)
        arrived.append(lax.ppermute(poisson.transform_z(rho), "grp", group_pairs))
    for c, ((o0, _), _, _) in enumerate(layout):
        poisson.add(arrived[c], o0)
    received = poisson.solve()
    partial = elements(received, added, b, qp_states)
    return scatter_sum(partial, "grid")[None]


def solution(mesh):
    in_specs = (
        P("grp", None, None, "grid", None, None),
        P("grid", None, None),
        P("grp", "grid", None, None),
        P(None, "grid", None, None),
    )
    out_specs = P("grp", "grid", None)
    return jax.shard_map(
        on_device, mesh=mesh, in_specs=in_specs, out_specs=out_specs, check_vma=False
    )
```

profile of v0, /device:TPU:28, one launch (start us, length us, event | category | flops | bytes accessed | tf_op | source)
XLA Modules:
  0.0 294.4 jit_solution(15814965829553440077)
XLA Ops:
  0.5 2.9 slice.249
  3.5 1.2 copy-done
  5.2 1.8 pad_maximum_fusion
  7.0 4.0 %collective-permute-start.7 = (f32[14,200,256]{2,1,0:T(8,128)}, f32[14,200,256]{2,1,0:T(8,128)}, u32[]{:S(2)}, u32[]{:S(2)}) collective-permute-start(f32[14,200,256]{2,1,0:T(8,128)} %pad_maximum_fusion), channel_id=1, source_target_pairs={{3,7},{4,0},{11,15},{12,8},{19,23},{20,16},{27,31},{28,24}} | collective-permute-start | bytes 8601608 | tf_op jit(solution)/shard_map/ppermute | solution.py:599
  11.1 2.3 slice.244
  13.3 3.7 %collective-permute-start.3 = (f32[16,56,256]{2,1,0:T(8,128)}, f32[16,56,256]{2,1,0:T(8,128)}, u32[]{:S(2)}, u32[]{:S(2)}) collective-permute-start(f32[16,56,256]{2,1,0:T(8,128)} %bitcast.11), channel_id=1, source_target_pairs={{1,2},{2,1},{3,4},{4,3},{5,6},{6,5},{9,10},{10,9},{11,12},{12,11},... | collective-permute-start | bytes 2752520 | tf_op jit(solution)/shard_map/ppermute | solution.py:593
  17.0 1.1 slice.245
  19.7 2.2 collective-permute-start.4
  22.8 1.1 multiply_exponential_fusion
  24.0 2.2 fusion.96
  26.2 2.1 exponential-minus-one_negate_fusion
  28.3 1.1 fusion.22
  30.0 3.4 %fusion.97 = (f32[4,4,80,256]{3,2,1,0:T(8,128)}, f32[4,4,80,256]{3,2,1,0:T(8,128)}) fusion(f32[6,4,256,256]{3,2,1,0:T(8,128)} %bitcast.65), kind=kLoop, calls=%fused_computation.159 | loop fusion | bytes 5242880 | tf_op jit(solution)/shard_map/slice | solution.py:592
  33.5 16.7 %collective-permute-done.4 = f32[14,56,256]{2,1,0:T(8,128)} collective-permute-done((f32[14,56,256]{2,1,0:T(8,128)}, f32[14,56,256]{2,1,0:T(8,128)}, u32[]{:S(2)}, u32[]{:S(2)}) %collective-permute-start.4) | collective-permute-done | bytes 802848 | tf_op jit(solution)/shard_map/ppermute | solution.py:588
  50.2 1.0 broadcast_select_fusion
  51.2 1.3 collective-permute-start.5
  53.1 3.1 %collective-permute-start.6 = (f32[16,80,256]{2,1,0:T(8,128)}, f32[16,80,256]{2,1,0:T(8,128)}, u32[]{:S(2)}, u32[]{:S(2)}) collective-permute-start(f32[16,80,256]{2,1,0:T(8,128)} %bitcast.13), channel_id=1, source_target_pairs={{1,2},{2,1},{3,4},{4,3},{5,6},{6,5},{9,10},{10,9},{11,12},{12,11},... | collective-permute-start | bytes 3932168 | tf_op jit(solution)/shard_map/ppermute | solution.py:593
  56.3 3.3 %slice_select_fusion.1 = (f32[14,80,256]{2,1,0:T(8,128)}, f32[14,80,256]{2,1,0:T(8,128)}) fusion(f32[14,200,256]{2,1,0:T(8,128)} %collective-permute-done.7, f32[3,80,256]{2,1,0:T(8,128)S(1)} %copy-done.10, f32[3,80,256]{2,1,0:T(8,128)S(1)} %get-tuple-element.43, f32[8,80,256]{2,1,0:T(8,128)S(1)} %bitcast.85, pred[]{:T(512)S(6)} %or.2, ...), kind=kLoop, calls=%fused_computation.8 | loop fusion | flops 1720320 | bytes 6881281 | tf_op jit(solution)/shard_map/jit(_where)/select_n | solution.py:602
  59.6 1.4 collective-permute-start.8
  61.7 2.0 slice.264
  63.6 1.1 slice.266
  64.8 1.9 slice_select_fusion.4
  66.7 3.3 %collective-permute-start.11 = (f32[16,80,256]{2,1,0:T(8,128)S(1)}, f32[16,80,256]{2,1,0:T(8,128)S(1)}, u32[]{:S(2)}, u32[]{:S(2)}) collective-permute-start(f32[16,80,256]{2,1,0:T(8,128)S(1)} %bitcast.87), channel_id=1, source_target_pairs={{1,2},{2,1},{3,4},{4,3},{5,6},{6,5},{9,10},{10,9},{11,12},{12,11},... | collective-permute-start | bytes 3932168 | tf_op jit(solution)/shard_map/ppermute | solution.py:593
  70.1 4.0 %collective-permute-done.5.refs_1_ = f32[14,56,256]{2,1,0:T(8,128)} collective-permute-done((f32[14,56,256]{2,1,0:T(8,128)}, f32[14,56,256]{2,1,0:T(8,128)}, u32[]{:S(2)}, u32[]{:S(2)}) %collective-permute-start.5) | collective-permute-done | bytes 802848 | tf_op jit(solution)/shard_map/ppermute | solution.py:604
  74.1 4.1 %collective-permute-start.17 = (f32[16,40,256]{2,1,0:T(8,128)}, f32[16,40,256]{2,1,0:T(8,128)S(1)}, u32[]{:S(2)}, u32[]{:S(2)}) collective-permute-start(f32[16,40,256]{2,1,0:T(8,128)} %bitcast.22), channel_id=1, source_target_pairs={{1,2},{2,1},{3,4},{4,3},{5,6},{6,5},{9,10},{10,9},{11,12},{12,11},... | collective-permute-start | bytes 1966088 | tf_op jit(solution)/shard_map/ppermute | solution.py:593
  78.2 1.3 collective-permute-start.12
  79.5 19.1 %taylor.4 = (f32[6,4,256,256]{3,2,1,0:T(8,128)}, f32[4,48,256]{2,1,0:T(8,128)}) custom-call(s32[2]{0:T(128)} %get-tuple-element.66.flag_ref, f32[2]{0:T(128)} %get-tuple-element.67.mask_ref, f32[6,4,256,256]{3,2,1,0:T(8,128)} %bitcast.68, f32[4,256,256]{2,1,0:T(8,128)} %pot_ref.7, f32[4,256,256]{2,1,0:T(8,128)} %bitcast.72, ...), custom_call_target="tpu_custom_call" | custom-call | flops 6881280000 | bytes 20971520 | tf_op jit(solution)/shard_map/taylor/pallas_call | solution.py:332
  98.7 3.0 %fusion.29 = f32[4,48,256]{2,1,0:T(8,128)} fusion(f32[4,48,256]{2,1,0:T(8,128)} %get-tuple-element.23, s32[256]{0:T(256)S(1)} %iota_add_fusion), kind=kOutput, calls=%fused_computation.50 | convolution fusion | flops 151650304 | bytes 394240 | tf_op jit(solution)/shard_map/xyz,zl->xyl/dot_general | solution.py:500
  101.7 1.3 collective-permute-start.18
  103.0 1.5 collective-permute-start.9
  104.5 26.4 %taylor.5 = (f32[6,4,256,256]{3,2,1,0:T(8,128)}, f32[4,80,256]{2,1,0:T(8,128)}) custom-call(s32[2]{0:T(128)} %get-tuple-element.66.flag_ref, f32[2]{0:T(128)} %get-tuple-element.67.mask_ref, f32[6,4,256,256]{3,2,1,0:T(8,128)} %bitcast.69, f32[4,256,256]{2,1,0:T(8,128)} %pot_ref.7, f32[4,256,256]{2,1,0:T(8,128)} %bitcast.73, ...), custom_call_target="tpu_custom_call", output_to_operand_aliasing={{0}: (12, {})} | custom-call | flops 11796480000 | bytes 20971520 | tf_op jit(solution)/shard_map/taylor/pallas_call | solution.py:332
  130.9 3.2 %fusion.27 = f32[4,80,256]{2,1,0:T(8,128)} fusion(f32[4,80,256]{2,1,0:T(8,128)} %get-tuple-element.27, s32[256]{0:T(256)S(1)} %iota_add_fusion), kind=kOutput, calls=%fused_computation.48 | convolution fusion | flops 252313600 | bytes 656384 | tf_op jit(solution)/shard_map/xyz,zl->xyl/dot_general | solution.py:500
  134.1 1.3 collective-permute-start.13
  135.4 1.1 copy-done.8
  136.5 26.4 %taylor.6 = (f32[6,4,256,256]{3,2,1,0:T(8,128)}, f32[4,80,256]{2,1,0:T(8,128)}) custom-call(s32[2]{0:T(128)} %get-tuple-element.66.flag_ref, f32[2]{0:T(128)} %get-tuple-element.67.mask_ref, f32[6,4,256,256]{3,2,1,0:T(8,128)} %bitcast.70, f32[4,256,256]{2,1,0:T(8,128)} %pot_ref.7, f32[4,256,256]{2,1,0:T(8,128)} %bitcast.74, ...), custom_call_target="tpu_custom_call", output_to_operand_aliasing={{0}: (12, {})} | custom-call | flops 11796480000 | bytes 20971520 | tf_op jit(solution)/shard_map/taylor/pallas_call | solution.py:332
  162.9 2.5 fusion.25
  165.4 1.3 collective-permute-start.15
  166.7 1.0 slice_select_fusion.15
  167.7 28.1 %collective-permute-start.14 = (f32[4,80,128]{2,1,0:T(8,128)S(1)}, f32[4,80,128]{2,1,0:T(8,128)S(1)}, u32[]{:S(2)}, u32[]{:S(2)}) collective-permute-start(f32[4,80,128]{2,1,0:T(8,128)S(1)} %get-tuple-element.48), channel_id=1, source_target_pairs={{0,1},{1,0},{2,3},{3,2},{4,5},{5,4},{6,7},{7,6},{8,9},{9,8},{10,11... | collective-permute-start | bytes 491528 | tf_op jit(solution)/shard_map/ppermute | solution.py:497
  196.8 1.0 fusion.7
  198.7 19.5 %taylor.7 = (f32[6,4,256,256]{3,2,1,0:T(8,128)}, f32[4,48,256]{2,1,0:T(8,128)}) custom-call(s32[2]{0:T(128)} %get-tuple-element.66.flag_ref, f32[2]{0:T(128)} %get-tuple-element.67.mask_ref, f32[6,4,256,256]{3,2,1,0:T(8,128)} %bitcast.71, f32[4,256,256]{2,1,0:T(8,128)} %pot_ref.7, f32[4,256,256]{2,1,0:T(8,128)} %bitcast.75, ...), custom_call_target="tpu_custom_call", output_to_operand_aliasing={{0}: (12, {})} | custom-call | flops 6881280000 | bytes 20971520 | tf_op jit(solution)/shard_map/taylor/pallas_call | solution.py:332
  218.3 2.3 fusion.23
  220.6 1.5 collective-permute-start.19
  222.2 7.7 %collective-permute-start.16 = (f32[4,80,128]{2,1,0:T(8,128)S(1)}, f32[4,80,128]{2,1,0:T(8,128)S(1)}, u32[]{:S(2)}, u32[]{:S(2)}) collective-permute-start(f32[4,80,128]{2,1,0:T(8,128)S(1)} %get-tuple-element.50), channel_id=1, source_target_pairs={{0,1},{1,0},{2,3},{3,2},{4,5},{5,4},{6,7},{7,6},{8,9},{9,8},{10,11... | collective-permute-start | bytes 491528 | tf_op jit(solution)/shard_map/ppermute | solution.py:497
  229.8 3.3 %collective-permute-done.19 = f32[4,48,256]{2,1,0:T(8,128)S(1)} collective-permute-done((f32[4,48,256]{2,1,0:T(8,128)S(1)}, f32[4,48,256]{2,1,0:T(8,128)S(1)}, u32[]{:S(2)}, u32[]{:S(2)}) %collective-permute-start.19) | collective-permute-done | bytes 196640 | tf_op jit(solution)/shard_map/ppermute | solution.py:621
  233.2 2.4 collective-permute-start.20
  235.6 1.0 fusion.13
  236.7 1.0 fusion.41
  237.7 2.1 fusion.2.f_ref
  239.8 2.9 moments.1
  242.7 1.0 broadcast_select_fusion.1
  243.7 2.4 collective-permute-start.21
  246.1 2.6 collective-permute-start.22
  250.0 5.2 %collective-permute-done.22.refs_1_ = f32[256,128]{1,0:T(8,128)S(1)} collective-permute-done((f32[256,128]{1,0:T(8,128)S(1)}, f32[256,128]{1,0:T(8,128)S(1)}, u32[]{:S(2)}, u32[]{:S(2)}) %collective-permute-start.22) | collective-permute-done | bytes 131104 | tf_op jit(solution)/shard_map/ppermute | solution.py:524
  255.9 3.7 %solve.1 = f32[8,256,128]{2,1,0:T(8,128)} custom-call(f32[3]{0:T(128)} %add_convert_fusion.side_ref, f32[8,256,128]{2,1,0:T(8,128)} %fusion.2.f_ref, f32[8,256,128]{2,1,0:T(8,128)} %get-tuple-element.59.low_ref, f32[8,256,128]{2,1,0:T(8,128)} %get-tuple-element.58.high_ref, f32[256,128]{1,0:T(8,128)} %get-tuple-element.61.r_ref, ...), custom_call_target="tpu_custom_call" | custom-call | tf_op jit(solution)/shard_map/solve/pallas_call | solution.py:526
  259.6 3.3 %convolution_bitcast_fusion = f32[8,256,128]{2,1,0:T(8,128)S(1)} fusion(f32[8,256,128]{2,1,0:T(8,128)} %solve.1, s32[256]{0:T(256)S(1)} %iota_add_fusion), kind=kOutput, calls=%fused_computation.2 | convolution fusion | flops 805961728 | bytes 2098176 | tf_op jit(solution)/shard_map/xkl,ky->xyl/dot_general | solution.py:533
  263.2 1.0 fusion.3
  265.0 2.0 convolution_add_fusion.rec_ref
  267.0 16.8 %elements.1 = f32[32,6]{1,0:T(8,128)} custom-call(f32[4,256,256]{2,1,0:T(8,128)} %convolution_add_fusion.rec_ref, f32[4,256,256]{2,1,0:T(8,128)} %bitcast.76, f32[6,4,256,256]{3,2,1,0:T(8,128)} %get-tuple-element.36.b_ref, bf16[32,4,256,256]{3,2,1,0:T(8,128)(2,1)} %q_ref.1), custom_call_target="tpu_custom_call" | custom-call | tf_op jit(solution)/shard_map/elements/pallas_call | solution.py:402
  284.6 1.7 collective-permute-start.25
  286.3 1.9 collective-permute-done.25
  289.0 1.5 collective-permute-start.26
  290.4 2.2 collective-permute-done.26
  292.7 1.1 collective-permute-done.27
  (87 shorter events, 12.7 us)
Async XLA Ops:
  0.0 78.2 %collective-permute-start = (f32[6,4,256,256]{3,2,1,0:T(8,128)}, f32[6,4,256,256]{3,2,1,0:T(8,128)}, u32[]{:S(2)}, u32[]{:S(2)}) collective-permute-start(f32[6,4,256,256]{3,2,1,0:T(8,128)} %bitcast.60), channel_id=1, source_target_pairs={{0,1},{1,0},{2,3},{3,2},{4,5},{5,4},{6,7},{7,6},{8,9},{9,8},{10,11... | collective-permute-start | bytes 18874376 | tf_op jit(solution)/shard_map/ppermute | solution.py:596
  0.0 59.6 %collective-permute-start.1 = (f32[4,256,256]{2,1,0:T(8,128)}, f32[4,256,256]{2,1,0:T(8,128)}, u32[]{:S(2)}, u32[]{:S(2)}) collective-permute-start(f32[4,256,256]{2,1,0:T(8,128)} %pot_ref.7), channel_id=1, source_target_pairs={{0,1},{1,0},{2,3},{3,2},{4,5},{5,4},{6,7},{7,6},{8,9},{9,8},{10,11... | collective-permute-start | bytes 3145736 | tf_op jit(solution)/shard_map/ppermute | solution.py:596
  0.5 2.9 copy-start.1
  3.4 1.2 copy-start
  3.5 1.7 copy-start.2
  7.0 46.1 %collective-permute-start.7 = (f32[14,200,256]{2,1,0:T(8,128)}, f32[14,200,256]{2,1,0:T(8,128)}, u32[]{:S(2)}, u32[]{:S(2)}) collective-permute-start(f32[14,200,256]{2,1,0:T(8,128)} %pad_maximum_fusion), channel_id=1, source_target_pairs={{3,7},{4,0},{11,15},{12,8},{19,23},{20,16},{27,31},{28,24}} | collective-permute-start | bytes 8601608 | tf_op jit(solution)/shard_map/ppermute | solution.py:599
  13.3 37.9 %collective-permute-start.3 = (f32[16,56,256]{2,1,0:T(8,128)}, f32[16,56,256]{2,1,0:T(8,128)}, u32[]{:S(2)}, u32[]{:S(2)}) collective-permute-start(f32[16,56,256]{2,1,0:T(8,128)} %bitcast.11), channel_id=1, source_target_pairs={{1,2},{2,1},{3,4},{4,3},{5,6},{6,5},{9,10},{10,9},{11,12},{12,11},... | collective-permute-start | bytes 2752520 | tf_op jit(solution)/shard_map/ppermute | solution.py:593
  18.1 0.7 copy-start.4
  18.1 1.6 copy-start.6
  19.7 30.4 %collective-permute-start.4 = (f32[14,56,256]{2,1,0:T(8,128)}, f32[14,56,256]{2,1,0:T(8,128)}, u32[]{:S(2)}, u32[]{:S(2)}) collective-permute-start(f32[14,56,256]{2,1,0:T(8,128)} %pad_maximum_fusion.1), channel_id=1, source_target_pairs={{3,7},{4,0},{11,15},{12,8},{19,23},{20,16},{27,31},{28,24}} | collective-permute-start | bytes 2408456 | tf_op jit(solution)/shard_map/ppermute | solution.py:588
  33.4 16.7 %copy-start.5 = (f32[3,56,256]{2,1,0:T(8,128)S(1)}, f32[3,56,256]{2,1,0:T(8,128)}, u32[]{:S(2)}) copy-start(f32[3,56,256]{2,1,0:T(8,128)} %copy-done.4) | copy-start | bytes 516100
  33.4 16.7 %copy-start.7 = (f32[3,56,256]{2,1,0:T(8,128)S(1)}, f32[3,56,256]{2,1,0:T(8,128)}, u32[]{:S(2)}) copy-start(f32[3,56,256]{2,1,0:T(8,128)} %copy-done.6) | copy-start | bytes 516100
  33.5 22.8 %copy-start.3 = (f32[2,4,80,256]{3,2,1,0:T(8,128)S(1)}, f32[2,4,80,256]{3,2,1,0:T(8,128)}, u32[]{:S(2)}) copy-start(f32[2,4,80,256]{3,2,1,0:T(8,128)} %get-tuple-element.38) | copy-start | bytes 1966084
  33.5 22.8 %copy-start.10 = (f32[3,80,256]{2,1,0:T(8,128)S(1)}, f32[3,80,256]{2,1,0:T(8,128)}, u32[]{:S(2)}) copy-start(f32[3,80,256]{2,1,0:T(8,128)} %get-tuple-element.45) | copy-start | bytes 737284
  33.5 22.8 %copy-start.11 = (f32[3,80,256]{2,1,0:T(8,128)S(1)}, f32[3,80,256]{2,1,0:T(8,128)}, u32[]{:S(2)}) copy-start(f32[3,80,256]{2,1,0:T(8,128)} %get-tuple-element.46) | copy-start | bytes 737284
  50.1 16.6 %collective-permute-start.2 = (f32[4,256,256]{2,1,0:T(8,128)S(1)}, f32[4,256,256]{2,1,0:T(8,128)}, u32[]{:S(2)}, u32[]{:S(2)}) collective-permute-start(f32[4,256,256]{2,1,0:T(8,128)S(1)} %bitcast.81), channel_id=1, source_target_pairs={{0,1},{1,0},{2,3},{3,2},{4,5},{5,4},{6,7},{7,6},{8,9},{9,8},{10,11... | collective-permute-start | bytes 3145736 | tf_op jit(solution)/shard_map/ppermute | solution.py:596
  51.2 22.9 %collective-permute-start.5 = (f32[14,56,256]{2,1,0:T(8,128)}, f32[14,56,256]{2,1,0:T(8,128)}, u32[]{:S(2)}, u32[]{:S(2)}) collective-permute-start(f32[14,56,256]{2,1,0:T(8,128)} %broadcast_select_fusion), channel_id=1, source_target_pairs={{1,2},{2,1},{5,6},{6,5},{7,4},{0,3},{9,10},{10,9},{13,14},{14,13},... | collective-permute-start | bytes 2408456 | tf_op jit(solution)/shard_map/ppermute | solution.py:604
  53.1 48.5 %collective-permute-start.6 = (f32[16,80,256]{2,1,0:T(8,128)}, f32[16,80,256]{2,1,0:T(8,128)}, u32[]{:S(2)}, u32[]{:S(2)}) collective-permute-start(f32[16,80,256]{2,1,0:T(8,128)} %bitcast.13), channel_id=1, source_target_pairs={{1,2},{2,1},{3,4},{4,3},{5,6},{6,5},{9,10},{10,9},{11,12},{12,11},... | collective-permute-start | bytes 3932168 | tf_op jit(solution)/shard_map/ppermute | solution.py:593
  59.6 5.2 %copy-start.13 = (f32[3,40,256]{2,1,0:T(8,128)S(1)}, f32[3,40,256]{2,1,0:T(8,128)}, u32[]{:S(2)}) copy-start(f32[3,40,256]{2,1,0:T(8,128)} %slice_select_fusion.16) | copy-start | bytes 368644
  59.6 5.2 %copy-start.14 = (f32[3,40,256]{2,1,0:T(8,128)S(1)}, f32[3,40,256]{2,1,0:T(8,128)}, u32[]{:S(2)}) copy-start(f32[3,40,256]{2,1,0:T(8,128)} %slice_select_fusion.17) | copy-start | bytes 368644
  59.6 43.4 %collective-permute-start.8 = (f32[14,80,256]{2,1,0:T(8,128)}, f32[14,80,256]{2,1,0:T(8,128)}, u32[]{:S(2)}, u32[]{:S(2)}) collective-permute-start(f32[14,80,256]{2,1,0:T(8,128)} %get-tuple-element.41), channel_id=1, source_target_pairs={{1,2},{2,1},{5,6},{6,5},{7,4},{0,3},{9,10},{10,9},{13,14},{14,13},... | collective-permute-start | bytes 3440648 | tf_op jit(solution)/shard_map/ppermute | solution.py:604
  63.6 3.1 %copy-start.9 = (f32[4,4,80,256]{3,2,1,0:T(8,128)S(1)}, f32[4,4,80,256]{3,2,1,0:T(8,128)}, u32[]{:S(2)}) copy-start(f32[4,4,80,256]{3,2,1,0:T(8,128)} %get-tuple-element.40) | copy-start | bytes 3932164
  66.7 68.6 %collective-permute-start.11 = (f32[16,80,256]{2,1,0:T(8,128)S(1)}, f32[16,80,256]{2,1,0:T(8,128)S(1)}, u32[]{:S(2)}, u32[]{:S(2)}) collective-permute-start(f32[16,80,256]{2,1,0:T(8,128)S(1)} %bitcast.87), channel_id=1, source_target_pairs={{1,2},{2,1},{3,4},{4,3},{5,6},{6,5},{9,10},{10,9},{11,12},{12,11},... | collective-permute-start | bytes 3932168 | tf_op jit(solution)/shard_map/ppermute | solution.py:593
  74.1 123.8 %collective-permute-start.17 = (f32[16,40,256]{2,1,0:T(8,128)}, f32[16,40,256]{2,1,0:T(8,128)S(1)}, u32[]{:S(2)}, u32[]{:S(2)}) collective-permute-start(f32[16,40,256]{2,1,0:T(8,128)} %bitcast.22), channel_id=1, source_target_pairs={{1,2},{2,1},{3,4},{4,3},{5,6},{6,5},{9,10},{10,9},{11,12},{12,11},... | collective-permute-start | bytes 1966088 | tf_op jit(solution)/shard_map/ppermute | solution.py:593
  78.2 57.2 %collective-permute-start.12 = (f32[14,80,256]{2,1,0:T(8,128)}, f32[14,80,256]{2,1,0:T(8,128)}, u32[]{:S(2)}, u32[]{:S(2)}) collective-permute-start(f32[14,80,256]{2,1,0:T(8,128)} %get-tuple-element.42), channel_id=1, source_target_pairs={{1,2},{2,1},{5,6},{6,5},{7,4},{0,3},{9,10},{10,9},{13,14},{14,13},... | collective-permute-start | bytes 3440648 | tf_op jit(solution)/shard_map/ppermute | solution.py:604
  101.7 96.2 %collective-permute-start.18 = (f32[14,40,256]{2,1,0:T(8,128)}, f32[14,40,256]{2,1,0:T(8,128)}, u32[]{:S(2)}, u32[]{:S(2)}) collective-permute-start(f32[14,40,256]{2,1,0:T(8,128)} %slice_select_fusion.4), channel_id=1, source_target_pairs={{1,2},{2,1},{5,6},{6,5},{7,4},{0,3},{9,10},{10,9},{13,14},{14,13},... | collective-permute-start | bytes 1720328 | tf_op jit(solution)/shard_map/ppermute | solution.py:604
  103.0 31.1 %collective-permute-start.9 = (f32[4,48,256]{2,1,0:T(8,128)}, f32[4,48,256]{2,1,0:T(8,128)}, u32[]{:S(2)}, u32[]{:S(2)}) collective-permute-start(f32[4,48,256]{2,1,0:T(8,128)} %fusion.29), channel_id=1, source_target_pairs={{0,16},{8,24},{1,17},{9,25},{2,18},{10,26},{3,19},{11,27},{4,20},{... | collective-permute-start | bytes 589832 | tf_op jit(solution)/shard_map/ppermute | solution.py:621
  134.1 32.6 %collective-permute-start.13 = (f32[4,80,256]{2,1,0:T(8,128)}, f32[4,80,256]{2,1,0:T(8,128)}, u32[]{:S(2)}, u32[]{:S(2)}) collective-permute-start(f32[4,80,256]{2,1,0:T(8,128)} %fusion.27), channel_id=1, source_target_pairs={{0,16},{8,24},{1,17},{9,25},{2,18},{10,26},{3,19},{11,27},{4,20},{... | collective-permute-start | bytes 983048 | tf_op jit(solution)/shard_map/ppermute | solution.py:621
  135.4 1.1 copy-start.8
  165.4 32.5 %collective-permute-start.15 = (f32[4,80,256]{2,1,0:T(8,128)S(1)}, f32[4,80,256]{2,1,0:T(8,128)S(1)}, u32[]{:S(2)}, u32[]{:S(2)}) collective-permute-start(f32[4,80,256]{2,1,0:T(8,128)S(1)} %fusion.25), channel_id=1, source_target_pairs={{0,16},{8,24},{1,17},{9,25},{2,18},{10,26},{3,19},{11,27},{4,20},{... | collective-permute-start | bytes 983048 | tf_op jit(solution)/shard_map/ppermute | solution.py:621
  167.7 29.1 %collective-permute-start.14 = (f32[4,80,128]{2,1,0:T(8,128)S(1)}, f32[4,80,128]{2,1,0:T(8,128)S(1)}, u32[]{:S(2)}, u32[]{:S(2)}) collective-permute-start(f32[4,80,128]{2,1,0:T(8,128)S(1)} %get-tuple-element.48), channel_id=1, source_target_pairs={{0,1},{1,0},{2,3},{3,2},{4,5},{5,4},{6,7},{7,6},{8,9},{9,8},{10,11... | collective-permute-start | bytes 491528 | tf_op jit(solution)/shard_map/ppermute | solution.py:497
  196.7 41.0 %collective-permute-start.10 = (f32[4,48,128]{2,1,0:T(8,128)S(1)}, f32[4,48,128]{2,1,0:T(8,128)S(1)}, u32[]{:S(2)}, u32[]{:S(2)}) collective-permute-start(f32[4,48,128]{2,1,0:T(8,128)S(1)} %get-tuple-element.55), channel_id=1, source_target_pairs={{0,1},{1,0},{2,3},{3,2},{4,5},{5,4},{6,7},{7,6},{8,9},{9,8},{10,11... | collective-permute-start | bytes 294920 | tf_op jit(solution)/shard_map/ppermute | solution.py:497
  197.9 0.8 copy-start.12
  220.6 12.6 %collective-permute-start.19 = (f32[4,48,256]{2,1,0:T(8,128)S(1)}, f32[4,48,256]{2,1,0:T(8,128)S(1)}, u32[]{:S(2)}, u32[]{:S(2)}) collective-permute-start(f32[4,48,256]{2,1,0:T(8,128)S(1)} %fusion.23), channel_id=1, source_target_pairs={{0,16},{8,24},{1,17},{9,25},{2,18},{10,26},{3,19},{11,27},{4,20},{... | collective-permute-start | bytes 589832 | tf_op jit(solution)/shard_map/ppermute | solution.py:621
  222.2 13.4 %collective-permute-start.16 = (f32[4,80,128]{2,1,0:T(8,128)S(1)}, f32[4,80,128]{2,1,0:T(8,128)S(1)}, u32[]{:S(2)}, u32[]{:S(2)}) collective-permute-start(f32[4,80,128]{2,1,0:T(8,128)S(1)} %get-tuple-element.50), channel_id=1, source_target_pairs={{0,1},{1,0},{2,3},{3,2},{4,5},{5,4},{6,7},{7,6},{8,9},{9,8},{10,11... | collective-permute-start | bytes 491528 | tf_op jit(solution)/shard_map/ppermute | solution.py:497
  233.2 3.5 %collective-permute-start.20 = (f32[4,48,128]{2,1,0:T(8,128)S(1)}, f32[4,48,128]{2,1,0:T(8,128)S(1)}, u32[]{:S(2)}, u32[]{:S(2)}) collective-permute-start(f32[4,48,128]{2,1,0:T(8,128)S(1)} %get-tuple-element.57), channel_id=1, source_target_pairs={{0,1},{1,0},{2,3},{3,2},{4,5},{5,4},{6,7},{7,6},{8,9},{9,8},{10,11... | collective-permute-start | bytes 294920 | tf_op jit(solution)/shard_map/ppermute | solution.py:497
  243.7 6.3 %collective-permute-start.21 = (f32[256,128]{1,0:T(8,128)S(1)}, f32[256,128]{1,0:T(8,128)S(1)}, u32[]{:S(2)}, u32[]{:S(2)}) collective-permute-start(f32[256,128]{1,0:T(8,128)S(1)} %get-tuple-element.53), channel_id=1, source_target_pairs={{0,2},{1,3},{2,0},{3,1},{4,6},{5,7},{6,4},{7,5},{8,10},{9,11},{10,... | collective-permute-start | bytes 393224 | tf_op jit(solution)/shard_map/ppermute | solution.py:524
  246.1 9.1 %collective-permute-start.22 = (f32[256,128]{1,0:T(8,128)S(1)}, f32[256,128]{1,0:T(8,128)S(1)}, u32[]{:S(2)}, u32[]{:S(2)}) collective-permute-start(f32[256,128]{1,0:T(8,128)S(1)} %get-tuple-element.52), channel_id=1, source_target_pairs={{0,4},{1,5},{2,6},{3,7},{4,0},{5,1},{6,2},{7,3},{8,12},{9,13},{10,... | collective-permute-start | bytes 393224 | tf_op jit(solution)/shard_map/ppermute | solution.py:524
  248.7 6.5 %collective-permute-start.23 = (f32[256,128]{1,0:T(8,128)S(1)}, f32[256,128]{1,0:T(8,128)S(1)}, u32[]{:S(2)}, u32[]{:S(2)}) collective-permute-start(f32[256,128]{1,0:T(8,128)S(1)} %get-tuple-element.51), channel_id=1, source_target_pairs={{0,6},{1,7},{2,4},{3,5},{4,2},{5,3},{6,0},{7,1},{8,14},{9,15},{10,... | collective-permute-start | bytes 393224 | tf_op jit(solution)/shard_map/ppermute | solution.py:524
  250.0 5.2 %copy-start.15 = (f32[256,128]{1,0:T(8,128)}, f32[256,128]{1,0:T(8,128)S(1)}, u32[]{:S(2)}) copy-start(f32[256,128]{1,0:T(8,128)S(1)} %collective-permute-done.21.refs_0_) | copy-start | bytes 393220
  255.2 0.6 copy-start.16
  255.2 0.7 copy-start.17
  263.0 2.0 collective-permute-start.24
  284.6 3.7 %collective-permute-start.25 = (f32[16,6]{1,0:T(8,128)S(1)}, f32[16,6]{1,0:T(8,128)S(1)}, u32[]{:S(2)}, u32[]{:S(2)}) collective-permute-start(f32[16,6]{1,0:T(8,128)S(1)} %slice_select_fusion.22), channel_id=1, source_target_pairs={{0,4},{1,5},{2,6},{3,7},{4,0},{5,1},{6,2},{7,3},{8,12},{9,13},{10,... | collective-permute-start | bytes 1160 | tf_op jit(solution)/shard_map/ppermute | solution.py:551
  289.0 3.7 %collective-permute-start.26 = (f32[8,6]{1,0:T(8,128)S(1)}, f32[8,6]{1,0:T(8,128)S(1)}, u32[]{:S(2)}, u32[]{:S(2)}) collective-permute-start(f32[8,6]{1,0:T(8,128)S(1)} %slice_select_fusion.23), channel_id=1, source_target_pairs={{0,2},{1,3},{2,0},{3,1},{4,6},{5,7},{6,4},{7,5},{8,10},{9,11},{10,... | collective-permute-start | bytes 584 | tf_op jit(solution)/shard_map/ppermute | solution.py:551
  292.6 1.2 collective-permute-start.27
where the time goes:
time: 297 us; the launch traced here: 294 us
  Pallas kernels  115 us (39%)
  starting transfers between devices  78.3 us (26%)
  waiting for transfers between devices  36 us (12%)
  matrix products  22.6 us (8%)
  other arithmetic  22.1 us (7%)
  local copies, waits for them, and re-layouts  19.9 us (7%)
    pallas_call x4, Pallas kernels, taylor(): pl.pallas_call(functools.partial(taylor_kernel, span, shape, planes, b is...  91.5 us
    ppermute x5, starting transfers between devices, swap(): return lax.ppermute(array, 'grid', [(i, i ^ 1) for i in range(self.count)])  38.3 us
    pallas_call x1, Pallas kernels, elements(): pl.pallas_call(functools.partial(elements_kernel, n_states, parts, planes...  16.8 us
    ppermute x1, waiting for transfers between devices, on_device(): hops[0] = lax.ppermute(message(0, cut), 'grid', first_leg)  16.7 us
    ppermute x4, starting transfers between devices, on_device(): direct = lax.ppermute(block, 'grid', chip_pairs)  14.2 us
    dot_general x4, matrix products, transform_z(): return jnp.einsum('xyz,zl->xyl', density, self.table_z, precision=highest)  11 us
    slice x3, local copies, waits for them, and re-layouts, on_device(): block = own[:split, :, lo:hi].reshape(-1, hi - lo, size_z)  7.64 us
    slice x4, local copies, waits for them, and re-layouts, message(): own[split:, :, lo:hi].reshape(-1, hi - lo, size_z)  7.31 us
  transfers between devices with their start and end apart: 28, of which 9 were waited for; matrix products, arithmetic and copies ran while one was open for 17% of the time, Pallas kernels for 31%

commit v1 on v0

--- a/solution.py
+++ b/solution.py
@@ -18,9 +18,10 @@
 highest = lax.Precision.HIGHEST
 
 
-def sine_table(length):
+def sine_table(length, rows=None):
     indices = jnp.arange(length, dtype=jnp.int32) + 1
-    products = indices[:, None] * indices[None, :] % (2 * (length + 1))
+    rows = indices if rows is None else rows + 1
+    products = rows[:, None] * indices[None, :] % (2 * (length + 1))
     return jnp.sqrt(2.0 / (length + 1)) * jnp.sin(
         jnp.pi * products.astype(jnp.float32) / (length + 1)
     )
@@ -33,19 +34,61 @@
     return before, after
 
 
+def z_of(position, tiles):
+    return tiles * (position % LANES) + position // LANES
+
+
 def across_lanes(tiles):
     shape = tiles[0].shape
-    lane = lax.broadcasted_iota(jnp.int32, shape, len(shape) - 1)
-    up = [pltpu.roll(t, 1, len(shape) - 1) for t in tiles]
-    down = [pltpu.roll(t, LANES - 1, len(shape) - 1) for t in tiles]
-    sums = []
-    for m in range(len(tiles)):
-        low = up[m - 1] if m > 0 else 0.0
-        high = down[m + 1] if m < len(tiles) - 1 else 0.0
-        sums.append(
-            jnp.where(lane == 0, low, up[m]) + jnp.where(lane == LANES - 1, high, down[m])
-        )
-    return sums
+    axis = len(shape) - 1
+    lane = lax.broadcasted_iota(jnp.int32, shape, axis)
+    before = jnp.where(lane == 0, 0.0, pltpu.roll(tiles[-1], 1, axis))
+    after = jnp.where(lane == LANES - 1, 0.0, pltpu.roll(tiles[0], LANES - 1, axis))
+    line = [before] + tiles + [after]
+    return [line[m] + line[m + 2] for m in range(len(tiles))]
+
+
+def reorder_table(size_z, back=False):
+    row = lax.broadcasted_iota(jnp.int32, (size_z, size_z), 0)
+    col = lax.broadcasted_iota(jnp.int32, (size_z, size_z), 1)
+    z, position = (col, row) if back else (row, col)
+    return jnp.where(z == z_of(position, size_z // LANES), 1.0, 0.0).astype(jnp.bfloat16)
+
+
+def reorder_kernel(own_ref, pot_ref, add_ref, own_out, pot_out, add_out, table):
+    @pl.when(pl.program_id(0) == 0)
+    def _():
+        table[...] = reorder_table(table.shape[0])
+
+    def reorder(value):
+        total = None
+        for _ in range(3):
+            part = value.astype(jnp.bfloat16)
+            value = value - part.astype(jnp.float32)
+            moved = jnp.dot(part, table[...], preferred_element_type=jnp.float32)
+            total = moved if total is None else total + moved
+        return total
+
+    for j in range(own_ref.shape[0]):
+        own_out[j, 0] = reorder(own_ref[j, 0])
+    pot_out[0] = reorder(pot_ref[0])
+    add_out[0] = reorder(add_ref[0])
+
+
+def reorder(own, potential, added, rows):
+    n_fields, planes, _, size_z = own.shape
+    full = pl.BlockSpec((n_fields, 1, rows, size_z), lambda p: (0, p, 0, 0))
+    field = pl.BlockSpec((1, rows, size_z), lambda p: (p, 0, 0))
+    shape = lambda *lead: jax.ShapeDtypeStruct(lead + (planes, rows, size_z), jnp.float32)
+    return pl.pallas_call(
+        reorder_kernel,
+        grid=(planes,),
+        out_shape=(shape(n_fields), shape(), shape()),
+        in_specs=[full, field, field],
+        out_specs=(full, field, field),
+        scratch_shapes=[pltpu.VMEM((size_z, size_z), jnp.bfloat16)],
+        name="reorder",
+    )(own, potential, added)
 
 
 def neighbour_sum(ref, lead, p, r0, n):
@@ -82,7 +125,7 @@
 
 def taylor_kernel(
     span, sources, planes, first_call, flag_ref, mask_ref, own_ref, pot_ref, add_ref, mate_ref,
-    mate_pot, mate_add, *refs
+    mate_pot, mate_add, table_ref, *refs
 ):
     out_rows, _, window = span
     msgs, refs = refs[: 2 * len(sources)], refs[2 * len(sources) :]
@@ -293,8 +336,12 @@
     lax.fori_loop(0, n_vectors, vector, 0)
 
     def spread(p, carry):
+        flat = acc[p].reshape(height, tiles * LANES)
+        wave = jnp.dot(
+            flat, table_ref[...], precision=highest, preferred_element_type=jnp.float32
+        ).reshape(acc.shape[1:])
         for r in range(rows):
-            scatter(r_out, (p,), r, acc[p, r])
+            scatter(r_out, (p,), r, wave[r])
         return carry
 
     lax.fori_loop(0, planes, spread, 0)
@@ -312,7 +359,7 @@
         copy.wait()
 
 
-def taylor(span, flags, mask, own, potential, added, mates, sources, b):
+def taylor(span, flags, mask, own, potential, added, mates, table, sources, b):
     n_fields, planes, _, size_z = own.shape
     out_rows, _, window = span
     height = window[1] - window[0]
@@ -323,8 +370,9 @@
     natural = lambda *lead: pltpu.VMEM((tiles,) + lead + (height, LANES), jnp.float32)
     hbm = pl.BlockSpec(memory_space=pl.ANY)
     smem = pl.BlockSpec(memory_space=pltpu.SMEM)
+    vmem = pl.BlockSpec(memory_space=pltpu.VMEM)
     shape = [(piece, to) for _, piece, to in sources]
-    operands = [own, potential, added, *mates] + [m for msgs, _, _ in sources for m in msgs]
+    operands = [own, potential, added, *mates, table] + [m for msgs, _, _ in sources for m in msgs]
     aliases = {}
     if b is not None:
         operands.append(b)
@@ -335,7 +383,7 @@
             jax.ShapeDtypeStruct(own.shape, jnp.float32),
             jax.ShapeDtypeStruct((planes, out_rows[1] - out_rows[0], size_z), jnp.float32),
         ),
-        in_specs=[smem, smem] + [hbm] * len(operands),
+        in_specs=[smem, smem] + [hbm] * 6 + [vmem] + [hbm] * (len(operands) - 7),
         out_specs=(hbm, hbm),
         input_output_aliases=aliases,
         scratch_shapes=[
@@ -360,12 +408,13 @@
     )(flags, mask, *operands)
 
 
-def elements_kernel(n_states, parts, last_step, rec_ref, add_ref, b_ref, q_ref, out_ref, acc):
+def elements_kernel(n_states, parts, last_step, rec_ref, add_ref, b_ref, q_ref, out_ref, acc, table):
     step = pl.program_id(0) * pl.num_programs(1) + pl.program_id(1)
 
     @pl.when(step == 0)
     def _():
         acc[...] = jnp.zeros_like(acc)
+        table[...] = reorder_table(table.shape[0], back=True)
 
     field = rec_ref[0] + add_ref[0]
     group = 16
@@ -374,6 +423,8 @@
         at = slice(g * group, (g + 1) * group)
         weighted = [field[at] * b_ref[j, 0, at] for j in range(parts)]
         weighted = jnp.concatenate(weighted, axis=0).astype(jnp.bfloat16)
+        weighted = jnp.dot(weighted, table[...], preferred_element_type=jnp.float32)
+        weighted = weighted.astype(jnp.bfloat16)
         states = q_ref[:, 0, at].reshape(n_states * group, field.shape[-1])
         total += lax.dot_general(
             states, weighted, (((1,), (1,)), ((), ())), preferred_element_type=jnp.float32
@@ -407,7 +458,10 @@
         + [vec]
         + [pl.BlockSpec((n_states, 1, block, size_z), lambda p, y: (0, p, y, 0))],
         out_specs=pl.BlockSpec((n_states, parts), lambda p, y: (0, 0)),
-        scratch_shapes=[pltpu.VMEM((n_states * 16, parts * 16), jnp.float32)],
+        scratch_shapes=[
+            pltpu.VMEM((n_states * 16, parts * 16), jnp.float32),
+            pltpu.VMEM((size_z, size_z), jnp.bfloat16),
+        ],
         name="elements",
     )(received, added, b, states)
 
@@ -465,7 +519,9 @@
         self.chip, self.core = self.place // 2, self.place % 2
         self.first = self.core == 0
         self.planes, self.half = planes, size_z // 2
-        self.table_y, self.table_z = sine_table(size_y), sine_table(size_z)
+        self.table_y = sine_table(size_y)
+        at = jnp.arange(size_z, dtype=jnp.int32)
+        self.table_z = sine_table(size_z, z_of(at, size_z // LANES))
         full_x = planes * self.count
         sine_half = lambda n: jnp.sin(
             (0.5 * jnp.pi / (n + 1)) * (jnp.arange(n, dtype=jnp.int32) + 1).astype(jnp.float32)
@@ -495,9 +551,6 @@
 
     def swap(self, array):
         return lax.ppermute(array, "grid", [(i, i ^ 1) for i in range(self.count)])
-
-    def transform_z(self, density):
-        return jnp.einsum("xyz,zl->xyl", density, self.table_z, precision=highest)
 
     def add(self, piece, at):
         mine, got = self.pick(piece, True), self.swap(self.pick(piece, False))
@@ -534,7 +587,7 @@
         lower, upper = field[: self.planes], field[self.planes :]
         mine = jnp.where(self.first, lower, upper)
         got = self.swap(jnp.where(self.first, upper, lower))
-        flip = lambda mine: self.pick(self.table_z.T, mine).T
+        flip = lambda mine: self.pick(self.table_z, mine).T
         back = lambda part, table: jnp.einsum("xyl,lz->xyz", part, table, precision=highest)
         return back(mine, flip(True)) + back(got, flip(False))
 
@@ -556,7 +609,6 @@
 
 def on_device(vectors, potential, added_field, qp_states):
     own = vectors.reshape((-1,) + vectors.shape[3:])
-    added = added_field[0]
     count = lax.axis_size("grid")
     groups = lax.axis_size("grp")
     place = lax.axis_index("grid")
@@ -577,27 +629,35 @@
     layout = spans(size_y, SHARES)
     split = 4
 
+    def source(lo, hi):
+        return start if (lo, hi) == first_rows else (own, potential, added)
+
     def message(lo, hi):
+        vec, *parts = source(lo, hi)
         edge = lambda f: jnp.where(even, f[:-1, lo:hi], f[1:, lo:hi])
-        parts = [own[split:, :, lo:hi].reshape(-1, hi - lo, size_z), edge(potential), edge(added)]
-        return jnp.concatenate(parts)
-
-    cut = layout[0][1][1]
+        block = vec[split:, :, lo:hi].reshape(-1, hi - lo, size_z)
+        return jnp.concatenate([block] + [edge(f) for f in parts])
+
+    start = reorder(own, potential, added_field[0], layout[0][1][1])
+    own, potential, added = reorder(own, potential, added_field[0], size_y)
+    first_rows = layout[0][1]
     hops = [None] * len(layout)
     if relayed:
-        hops[0] = lax.ppermute(message(0, cut), "grid", first_leg)
+        hops[0] = lax.ppermute(message(*first_rows), "grid", first_leg)
     messages = []
     mates = None
     for c, (_, (lo, hi), _) in enumerate(layout):
-        block = own[:split, :, lo:hi].reshape(-1, hi - lo, size_z)
+        block = source(lo, hi)[0][:split, :, lo:hi].reshape(-1, hi - lo, size_z)
         direct = lax.ppermute(block, "grid", chip_pairs)
         rest, pairs = message(lo, hi), chip_pairs
         if mates is None:
             mates = [lax.ppermute(f, "grid", mate_pairs) for f in (own, potential, added)]
         if relayed:
             if c == 1:
-                late = lax.ppermute(message(cut, size_y), "grid", first_leg)
-                hops[1:] = [late[:, l - cut : h - cut] for _, (l, h), _ in layout[1:]]
+                hops[1] = lax.ppermute(message(lo, hi), "grid", first_leg)
+            if c == 2:
+                late = lax.ppermute(message(lo, size_y), "grid", first_leg)
+                hops[2:] = [late[:, l - lo : h - lo] for _, (l, h), _ in layout[2:]]
             ends = jnp.logical_or(place == 0, place == count - 1)
             rest = jnp.where(ends, hops[c], rest)
             pairs = [p for p in chip_pairs if set(p) != {left, right}] + second_leg
@@ -617,8 +677,8 @@
             b, arrived[c - 2] = lax.optimization_barrier((b, arrived[c - 2]))
         if c == len(layout) - 1:
             b, arrived[c - 1] = lax.optimization_barrier((b, arrived[c - 1]))
-        b, rho = taylor(span, flags, mask, own, potential, added, mates, sources, b)
-        arrived.append(lax.ppermute(poisson.transform_z(rho), "grp", group_pairs))
+        b, rho = taylor(span, flags, mask, own, potential, added, mates, poisson.table_z, sources, b)
+        arrived.append(lax.ppermute(rho, "grp", group_pairs))
     for c, ((o0, _), _, _) in enumerate(layout):
         poisson.add(arrived[c], o0)
     received = poisson.solve()

time: 297 us -> 293 us (0.987)
  matrix products: 22.6 us -> 11.5 us
  starting transfers between devices: 78.3 us -> 86.8 us
  waiting for transfers between devices: 36 us -> 29.2 us
  Pallas kernels: 115 us -> 120 us
    pallas_call x4, Pallas kernels: 91.5 us -> 76.9 us  [taylor(): pl.pallas_call(functools.partial(taylor_kernel, span, shape, planes, b is...]
    pallas_call x0 -> x2, Pallas kernels: none -> 14 us  [reorder(): pl.pallas_call(reorder_kernel, grid=(planes,), out_shape=(shape(n_fields)...]
    ppermute x6 -> x7, waiting for transfers between devices: 20 us -> 8.88 us  [the longest x1 5.29 us: on_device(): late = lax.ppermute(message(lo, size_y), 'grid', first_leg)]
    dot_general x4 -> x0, matrix products: 11 us -> none  [transform_z(): return jnp.einsum('xyz,zl->xyl', density, self.table_z, precision=highest)]
    ppermute x5, starting transfers between devices: 38.3 us -> 48.8 us  [swap(): return lax.ppermute(array, 'grid', [(i, i ^ 1) for i in range(self.count)])]
    pallas_call x1, Pallas kernels: 16.8 us -> 22.1 us  [elements(): pl.pallas_call(functools.partial(elements_kernel, n_states, parts, planes...]
    ppermute x4, waiting for transfers between devices: 4.02 us -> 7.42 us  [on_device(): messages.append((direct, lax.ppermute(rest, 'grid', pairs)))]
    ppermute x6 -> x7, starting transfers between devices: 11.8 us -> 13.6 us  [the longest x4 5.34 us: on_device(): arrived.append(lax.ppermute(rho, 'grp', group_pairs))]
  transfers between devices with their start and end apart: 28 -> 29, of which waited for: 9 -> 10; matrix products, arithmetic and copies ran while one was open for 17% -> 13% of each run, Pallas kernels for 31% -> 28%
where the time goes in v1:
time: 293 us; the launch traced here: 291 us
  Pallas kernels  120 us (41%)
  starting transfers between devices  86.8 us (30%)
  waiting for transfers between devices  29.2 us (10%)
  other arithmetic  25 us (9%)
  local copies, waits for them, and re-layouts  18 us (6%)
  matrix products  11.5 us (4%)
    pallas_call x4, Pallas kernels, taylor(): pl.pallas_call(functools.partial(taylor_kernel, span, shape, planes, b is...  76.9 us
    ppermute x5, starting transfers between devices, swap(): return lax.ppermute(array, 'grid', [(i, i ^ 1) for i in range(self.count)])  48.8 us
    pallas_call x1, Pallas kernels, elements(): pl.pallas_call(functools.partial(elements_kernel, n_states, parts, planes...  22.1 us
    pallas_call x2, Pallas kernels, reorder(): pl.pallas_call(reorder_kernel, grid=(planes,), out_shape=(shape(n_fields)...  14 us
    ppermute x4, starting transfers between devices, on_device(): direct = lax.ppermute(block, 'grid', chip_pairs)  13.1 us
    ppermute x4, waiting for transfers between devices, on_device(): messages.append((direct, lax.ppermute(rest, 'grid', pairs)))  7.42 us
    ppermute x3, waiting for transfers between devices, scatter_sum(): sent = lax.ppermute(jnp.where(upper, low, high), axis, pairs)  6.76 us
    slice x3, local copies, waits for them, and re-layouts, on_device(): block = source(lo, hi)[0][:split, :, lo:hi].reshape(-1, hi - lo, size_z)  6.5 us
  transfers between devices with their start and end apart: 29, of which 10 were waited for; matrix products, arithmetic and copies ran while one was open for 13% of the time, Pallas kernels for 28%

profile of v1, /device:TPU:28, one launch (start us, length us, event | category | flops | bytes accessed | tf_op | source)
XLA Modules:
  0.0 290.8 jit_solution(5980099532748663236)
XLA Ops:
  0.0 9.0 %reorder.2 = (f32[6,4,256,256]{3,2,1,0:T(8,128)}, f32[4,256,256]{2,1,0:T(8,128)}, f32[4,256,256]{2,1,0:T(8,128)}) custom-call(f32[6,4,256,256]{3,2,1,0:T(8,128)} %bitcast.47, f32[4,256,256]{2,1,0:T(8,128)} %pot_ref.3, f32[4,256,256]{2,1,0:T(8,128)} %bitcast.51), custom_call_target="tpu_custom_call" | custom-call | tf_op jit(solution)/shard_map/reorder/pallas_call | solution.py:83
  9.0 5.0 %reorder.3 = (f32[6,4,56,256]{3,2,1,0:T(8,128)}, f32[4,56,256]{2,1,0:T(8,128)}, f32[4,56,256]{2,1,0:T(8,128)}) custom-call(f32[6,4,256,256]{3,2,1,0:T(8,128)} %bitcast.48, f32[4,256,256]{2,1,0:T(8,128)} %pot_ref.3, f32[4,256,256]{2,1,0:T(8,128)} %bitcast.52), custom_call_target="tpu_custom_call" | custom-call | tf_op jit(solution)/shard_map/reorder/pallas_call | solution.py:83
  14.0 1.0 slice.191
  15.1 1.3 slice_select_fusion.9
  18.1 3.4 %collective-permute-start.4 = (f32[14,56,256]{2,1,0:T(8,128)}, f32[14,56,256]{2,1,0:T(8,128)}, u32[]{:S(2)}, u32[]{:S(2)}) collective-permute-start(f32[14,56,256]{2,1,0:T(8,128)} %pad_maximum_fusion.2), channel_id=1, source_target_pairs={{3,7},{4,0},{11,15},{12,8},{19,23},{20,16},{27,31},{28,24}} | collective-permute-start | bytes 2408456 | tf_op jit(solution)/shard_map/ppermute | solution.py:646
  21.6 1.0 slice.190
  22.6 4.2 %collective-permute-start.3 = (f32[16,56,256]{2,1,0:T(8,128)}, f32[16,56,256]{2,1,0:T(8,128)}, u32[]{:S(2)}, u32[]{:S(2)}) collective-permute-start(f32[16,56,256]{2,1,0:T(8,128)} %bitcast.11), channel_id=1, source_target_pairs={{1,2},{2,1},{3,4},{4,3},{5,6},{6,5},{9,10},{10,9},{11,12},{12,11},... | collective-permute-start | bytes 2752520 | tf_op jit(solution)/shard_map/ppermute | solution.py:651
  27.7 2.4 fusion.80
  30.0 1.1 pad_maximum_fusion.1
  31.1 2.3 collective-permute-start.7
  33.4 1.3 slice.206
  34.8 1.4 pad_maximum_fusion
  36.1 2.5 collective-permute-start.12
  38.7 1.2 multiply_exponential_fusion
  39.9 2.9 fusion.22
  43.4 1.7 slice.225
  45.1 2.0 slice.223
  47.1 3.0 %exponential-minus-one_negate_fusion = (f32[8,256,128]{2,1,0:T(8,128)}, f32[8,256,128]{2,1,0:T(8,128)}) fusion(f32[8]{0:T(128)S(1)} %get-tuple-element.90, f32[256,128]{1,0:T(8,128)} %get-tuple-element.75, f32[8]{0:T(128)S(1)} %get-tuple-element.91), kind=kLoop, calls=%fused_computation.9 | loop fusion | flops 1048576 | bytes 2228288 | tf_op jit(solution)/shard_map/neg | solution.py:537
  50.1 3.5 %fusion.81 = (f32[4,4,80,256]{3,2,1,0:T(8,128)}, f32[4,4,80,256]{3,2,1,0:T(8,128)}) fusion(f32[6,4,256,256]{3,2,1,0:T(8,128)} %get-tuple-element.27.own_ref), kind=kLoop, calls=%fused_computation.155 | loop fusion | bytes 5242880 | tf_op jit(solution)/shard_map/slice | solution.py:650
  54.3 2.4 collective-permute-start.6
  56.7 1.3 collective-permute-start.5
  58.0 1.2 broadcast_select_fusion
  59.2 5.3 %collective-permute-done.12 = f32[14,120,256]{2,1,0:T(8,128)} collective-permute-done((f32[14,120,256]{2,1,0:T(8,128)}, f32[14,120,256]{2,1,0:T(8,128)}, u32[]{:S(2)}, u32[]{:S(2)}) %collective-permute-start.12) | collective-permute-done | bytes 1720352 | tf_op jit(solution)/shard_map/ppermute | solution.py:659
  64.5 1.3 collective-permute-start.8
  65.8 2.0 slice_select_fusion.1
  67.8 2.6 slice_select_fusion
  70.4 1.9 collective-permute-start.11
  72.3 6.5 %collective-permute-done.5.refs_1_ = f32[14,56,256]{2,1,0:T(8,128)S(1)} collective-permute-done((f32[14,56,256]{2,1,0:T(8,128)S(1)}, f32[14,56,256]{2,1,0:T(8,128)S(1)}, u32[]{:S(2)}, u32[]{:S(2)}) %collective-permute-start.5) | collective-permute-done | bytes 802848 | tf_op jit(solution)/shard_map/ppermute | solution.py:664
  78.8 4.6 %collective-permute-start.18 = (f32[16,40,256]{2,1,0:T(8,128)}, f32[16,40,256]{2,1,0:T(8,128)S(1)}, u32[]{:S(2)}, u32[]{:S(2)}) collective-permute-start(f32[16,40,256]{2,1,0:T(8,128)} %bitcast.21), channel_id=1, source_target_pairs={{1,2},{2,1},{3,4},{4,3},{5,6},{6,5},{9,10},{10,9},{11,12},{12,11},... | collective-permute-start | bytes 1966088 | tf_op jit(solution)/shard_map/ppermute | solution.py:651
  83.4 1.3 collective-permute-start.13
  84.7 16.6 %taylor.4 = (f32[6,4,256,256]{3,2,1,0:T(8,128)}, f32[4,48,256]{2,1,0:T(8,128)}) custom-call(s32[2]{0:T(128)} %get-tuple-element.88.flag_ref, f32[2]{0:T(128)} %get-tuple-element.89.mask_ref, f32[6,4,256,256]{3,2,1,0:T(8,128)} %get-tuple-element.27.own_ref, f32[4,256,256]{2,1,0:T(8,128)} %get-tuple-element.28.pot_ref, ...), custom_call_target="tpu_custom_call" | custom-call | flops 6881280000 | bytes 20971520 | tf_op jit(solution)/shard_map/taylor/pallas_call | solution.py:380
  101.3 1.3 collective-permute-start.19
  103.5 1.3 collective-permute-start.9
  104.8 21.7 %taylor.5 = (f32[6,4,256,256]{3,2,1,0:T(8,128)}, f32[4,80,256]{2,1,0:T(8,128)}) custom-call(s32[2]{0:T(128)} %get-tuple-element.88.flag_ref, f32[2]{0:T(128)} %get-tuple-element.89.mask_ref, f32[6,4,256,256]{3,2,1,0:T(8,128)} %get-tuple-element.27.own_ref, f32[4,256,256]{2,1,0:T(8,128)} %get-tuple-element.28.pot_ref, ...), custom_call_target="tpu_custom_call", output_to_operand_aliasing={{0}: (13, {})} | custom-call | flops 11796480000 | bytes 20971520 | tf_op jit(solution)/shard_map/taylor/pallas_call | solution.py:380
  126.5 1.5 collective-permute-start.14
  128.0 1.0 copy-done.11
  129.1 1.0 copy-done.13
  130.1 21.7 %taylor.6 = (f32[6,4,256,256]{3,2,1,0:T(8,128)}, f32[4,80,256]{2,1,0:T(8,128)}) custom-call(s32[2]{0:T(128)} %get-tuple-element.88.flag_ref, f32[2]{0:T(128)} %get-tuple-element.89.mask_ref, f32[6,4,256,256]{3,2,1,0:T(8,128)} %get-tuple-element.27.own_ref, f32[4,256,256]{2,1,0:T(8,128)} %get-tuple-element.28.pot_ref, ...), custom_call_target="tpu_custom_call", output_to_operand_aliasing={{0}: (13, {})} | custom-call | flops 11796480000 | bytes 20971520 | tf_op jit(solution)/shard_map/taylor/pallas_call | solution.py:380
  151.7 1.3 collective-permute-start.16
  153.1 1.0 slice_select_fusion.14
  154.1 38.5 %collective-permute-start.15 = (f32[4,80,128]{2,1,0:T(8,128)S(1)}, f32[4,80,128]{2,1,0:T(8,128)S(1)}, u32[]{:S(2)}, u32[]{:S(2)}) collective-permute-start(f32[4,80,128]{2,1,0:T(8,128)S(1)} %get-tuple-element.58), channel_id=1, source_target_pairs={{0,1},{1,0},{2,3},{3,2},{4,5},{5,4},{6,7},{7,6},{8,9},{9,8},{10,11... | collective-permute-start | bytes 491528 | tf_op jit(solution)/shard_map/ppermute | solution.py:553
  193.6 1.0 fusion.7
  195.5 17.0 %taylor.7 = (f32[6,4,256,256]{3,2,1,0:T(8,128)}, f32[4,48,256]{2,1,0:T(8,128)}) custom-call(s32[2]{0:T(128)} %get-tuple-element.88.flag_ref, f32[2]{0:T(128)} %get-tuple-element.89.mask_ref, f32[6,4,256,256]{3,2,1,0:T(8,128)} %get-tuple-element.27.own_ref, f32[4,256,256]{2,1,0:T(8,128)} %get-tuple-element.28.pot_ref, ...), custom_call_target="tpu_custom_call", output_to_operand_aliasing={{0}: (13, {})} | custom-call | flops 6881280000 | bytes 20971520 | tf_op jit(solution)/shard_map/taylor/pallas_call | solution.py:380
  212.5 1.3 collective-permute-start.20
  213.8 7.6 %collective-permute-start.17 = (f32[4,80,128]{2,1,0:T(8,128)S(1)}, f32[4,80,128]{2,1,0:T(8,128)S(1)}, u32[]{:S(2)}, u32[]{:S(2)}) collective-permute-start(f32[4,80,128]{2,1,0:T(8,128)S(1)} %get-tuple-element.60), channel_id=1, source_target_pairs={{0,1},{1,0},{2,3},{3,2},{4,5},{5,4},{6,7},{7,6},{8,9},{9,8},{10,11... | collective-permute-start | bytes 491528 | tf_op jit(solution)/shard_map/ppermute | solution.py:553
  221.4 3.6 %collective-permute-done.20 = f32[4,48,256]{2,1,0:T(8,128)S(1)} collective-permute-done((f32[4,48,256]{2,1,0:T(8,128)}, f32[4,48,256]{2,1,0:T(8,128)S(1)}, u32[]{:S(2)}, u32[]{:S(2)}) %collective-permute-start.20) | collective-permute-done | bytes 196640 | tf_op jit(solution)/shard_map/ppermute | solution.py:681
  225.0 2.6 collective-permute-start.21
  227.6 1.0 fusion.13
  228.7 1.0 fusion.40
  229.7 2.1 fusion.2.f_ref
  231.8 2.9 moments.1
  234.7 1.0 broadcast_select_fusion.2
  235.7 2.4 collective-permute-start.22
  238.1 1.0 collective-permute-start.23
  240.3 2.0 collective-permute-done.22.refs_0_
  242.2 4.1 %collective-permute-done.23.refs_1_ = f32[256,128]{1,0:T(8,128)S(1)} collective-permute-done((f32[256,128]{1,0:T(8,128)S(1)}, f32[256,128]{1,0:T(8,128)S(1)}, u32[]{:S(2)}, u32[]{:S(2)}) %collective-permute-start.23) | collective-permute-done | bytes 131104 | tf_op jit(solution)/shard_map/ppermute | solution.py:577
  247.0 3.7 %solve.1 = f32[8,256,128]{2,1,0:T(8,128)} custom-call(f32[3]{0:T(128)} %add_convert_fusion.side_ref, f32[8,256,128]{2,1,0:T(8,128)} %fusion.2.f_ref, f32[8,256,128]{2,1,0:T(8,128)} %get-tuple-element.69.low_ref, f32[8,256,128]{2,1,0:T(8,128)} %get-tuple-element.68.high_ref, f32[256,128]{1,0:T(8,128)} %get-tuple-element.71.r_ref, ...), custom_call_target="tpu_custom_call" | custom-call | tf_op jit(solution)/shard_map/solve/pallas_call | solution.py:579
  250.8 3.3 %convolution_bitcast_fusion = f32[8,256,128]{2,1,0:T(8,128)S(1)} fusion(f32[8,256,128]{2,1,0:T(8,128)} %solve.1, s32[256]{0:T(256)S(1)} %get-tuple-element.87), kind=kOutput, calls=%fused_computation.2 | convolution fusion | flops 805961728 | bytes 2098176 | tf_op jit(solution)/shard_map/xkl,ky->xyl/dot_general | solution.py:586
  256.2 2.0 convolution_add_fusion.rec_ref
  258.2 22.1 %elements.1 = f32[32,6]{1,0:T(8,128)} custom-call(f32[4,256,256]{2,1,0:T(8,128)} %convolution_add_fusion.rec_ref, f32[4,256,256]{2,1,0:T(8,128)} %get-tuple-element.29.add_ref, f32[6,4,256,256]{3,2,1,0:T(8,128)} %get-tuple-element.48.b_ref, bf16[32,4,256,256]{3,2,1,0:T(8,128)(2,1)} %q_ref.1), custom_call_target="tpu_custom_call" | custom-call | tf_op jit(solution)/shard_map/elements/pallas_call | solution.py:453
  281.0 1.0 collective-permute-start.26
  282.0 2.7 collective-permute-done.26
  286.1 3.0 %collective-permute-done.27 = f32[8,6]{1,0:T(8,128)S(1)} collective-permute-done((f32[8,6]{1,0:T(8,128)S(1)}, f32[8,6]{1,0:T(8,128)S(1)}, u32[]{:S(2)}, u32[]{:S(2)}) %collective-permute-start.27) | collective-permute-done | bytes 224 | tf_op jit(solution)/shard_map/ppermute | solution.py:604
  289.1 1.1 collective-permute-done.28
  (99 shorter events, 13.6 us)
Async XLA Ops:
  9.0 74.4 %collective-permute-start = (f32[6,4,256,256]{3,2,1,0:T(8,128)}, f32[6,4,256,256]{3,2,1,0:T(8,128)}, u32[]{:S(2)}, u32[]{:S(2)}) collective-permute-start(f32[6,4,256,256]{3,2,1,0:T(8,128)} %get-tuple-element.27.own_ref), channel_id=1, source_target_pairs={{0,1},{1,0},{2,3},{3,2},{4,5},{5,4},{6,7},{7,6},{8,9},{9,8},{10,11... | collective-permute-start | bytes 18874376 | tf_op jit(solution)/shard_map/ppermute | solution.py:654
  15.1 6.5 %copy-start.10 = (f32[6,4,56,256]{3,2,1,0:T(8,128)S(1)}, f32[6,4,56,256]{3,2,1,0:T(8,128)}, u32[]{:S(2)}) copy-start(f32[6,4,56,256]{3,2,1,0:T(8,128)} %get-tuple-element.30) | copy-start | bytes 4128772
  16.4 0.7 copy-start.6
  16.4 0.7 copy-start.8
  17.1 9.6 %copy-start.1 = (f32[4,256,256]{2,1,0:T(8,128)S(1)}, f32[4,256,256]{2,1,0:T(8,128)}, u32[]{:S(2)}) copy-start(f32[4,256,256]{2,1,0:T(8,128)} %get-tuple-element.28.pot_ref) | copy-start | bytes 3145732
  18.1 8.7 %copy-start = (f32[4,256,256]{2,1,0:T(8,128)S(1)}, f32[4,256,256]{2,1,0:T(8,128)}, u32[]{:S(2)}) copy-start(f32[4,256,256]{2,1,0:T(8,128)} %get-tuple-element.29.add_ref) | copy-start | bytes 3145732
  18.1 29.0 %collective-permute-start.4 = (f32[14,56,256]{2,1,0:T(8,128)}, f32[14,56,256]{2,1,0:T(8,128)}, u32[]{:S(2)}, u32[]{:S(2)}) collective-permute-start(f32[14,56,256]{2,1,0:T(8,128)} %pad_maximum_fusion.2), channel_id=1, source_target_pairs={{3,7},{4,0},{11,15},{12,8},{19,23},{20,16},{27,31},{28,24}} | collective-permute-start | bytes 2408456 | tf_op jit(solution)/shard_map/ppermute | solution.py:646
  22.6 31.0 %collective-permute-start.3 = (f32[16,56,256]{2,1,0:T(8,128)}, f32[16,56,256]{2,1,0:T(8,128)}, u32[]{:S(2)}, u32[]{:S(2)}) collective-permute-start(f32[16,56,256]{2,1,0:T(8,128)} %bitcast.11), channel_id=1, source_target_pairs={{1,2},{2,1},{3,4},{4,3},{5,6},{6,5},{9,10},{10,9},{11,12},{12,11},... | collective-permute-start | bytes 2752520 | tf_op jit(solution)/shard_map/ppermute | solution.py:651
  27.7 2.4 copy-start.4
  31.1 25.6 %collective-permute-start.7 = (f32[14,80,256]{2,1,0:T(8,128)}, f32[14,80,256]{2,1,0:T(8,128)}, u32[]{:S(2)}, u32[]{:S(2)}) collective-permute-start(f32[14,80,256]{2,1,0:T(8,128)} %pad_maximum_fusion.1), channel_id=1, source_target_pairs={{3,7},{4,0},{11,15},{12,8},{19,23},{20,16},{27,31},{28,24}} | collective-permute-start | bytes 3440648 | tf_op jit(solution)/shard_map/ppermute | solution.py:657
  36.1 28.4 %collective-permute-start.12 = (f32[14,120,256]{2,1,0:T(8,128)}, f32[14,120,256]{2,1,0:T(8,128)}, u32[]{:S(2)}, u32[]{:S(2)}) collective-permute-start(f32[14,120,256]{2,1,0:T(8,128)} %pad_maximum_fusion), channel_id=1, source_target_pairs={{3,7},{4,0},{11,15},{12,8},{19,23},{20,16},{27,31},{28,24}} | collective-permute-start | bytes 5160968 | tf_op jit(solution)/shard_map/ppermute | solution.py:659
  47.1 7.1 %collective-permute-start.2 = (f32[4,256,256]{2,1,0:T(8,128)S(1)}, f32[4,256,256]{2,1,0:T(8,128)S(1)}, u32[]{:S(2)}, u32[]{:S(2)}) collective-permute-start(f32[4,256,256]{2,1,0:T(8,128)S(1)} %copy-done), channel_id=1, source_target_pairs={{0,1},{1,0},{2,3},{3,2},{4,5},{5,4},{6,7},{7,6},{8,9},{9,8},{10,11... | collective-permute-start | bytes 3145736 | tf_op jit(solution)/shard_map/ppermute | solution.py:654
  50.1 4.0 %copy-start.7 = (f32[3,56,256]{2,1,0:T(8,128)S(1)}, f32[3,56,256]{2,1,0:T(8,128)}, u32[]{:S(2)}) copy-start(f32[3,56,256]{2,1,0:T(8,128)} %copy-done.6) | copy-start | bytes 516100
  50.1 4.0 %copy-start.9 = (f32[3,56,256]{2,1,0:T(8,128)S(1)}, f32[3,56,256]{2,1,0:T(8,128)}, u32[]{:S(2)}) copy-start(f32[3,56,256]{2,1,0:T(8,128)} %copy-done.8) | copy-start | bytes 516100
  53.6 4.4 %copy-start.5 = (f32[3,80,256]{2,1,0:T(8,128)S(1)}, f32[3,80,256]{2,1,0:T(8,128)}, u32[]{:S(2)}) copy-start(f32[3,80,256]{2,1,0:T(8,128)} %copy-done.4) | copy-start | bytes 737284
  53.6 16.7 %collective-permute-start.1 = (f32[4,256,256]{2,1,0:T(8,128)S(1)}, f32[4,256,256]{2,1,0:T(8,128)S(1)}, u32[]{:S(2)}, u32[]{:S(2)}) collective-permute-start(f32[4,256,256]{2,1,0:T(8,128)S(1)} %copy-done.1), channel_id=1, source_target_pairs={{0,1},{1,0},{2,3},{3,2},{4,5},{5,4},{6,7},{7,6},{8,9},{9,8},{10,11... | collective-permute-start | bytes 3145736 | tf_op jit(solution)/shard_map/ppermute | solution.py:654
  54.3 3.8 %copy-start.15 = (f32[4,256,256]{2,1,0:T(8,128)}, f32[4,256,256]{2,1,0:T(8,128)S(1)}, u32[]{:S(2)}) copy-start(f32[4,256,256]{2,1,0:T(8,128)S(1)} %collective-permute-done.2.mate_add) | copy-start | bytes 3145732
  54.3 11.5 %copy-start.12 = (f32[2,4,40,256]{3,2,1,0:T(8,128)S(1)}, f32[2,4,40,256]{3,2,1,0:T(8,128)}, u32[]{:S(2)}) copy-start(f32[2,4,40,256]{3,2,1,0:T(8,128)} %slice.225) | copy-start | bytes 983044
  54.3 47.0 %collective-permute-start.6 = (f32[16,80,256]{2,1,0:T(8,128)}, f32[16,80,256]{2,1,0:T(8,128)}, u32[]{:S(2)}, u32[]{:S(2)}) collective-permute-start(f32[16,80,256]{2,1,0:T(8,128)} %bitcast.13), channel_id=1, source_target_pairs={{1,2},{2,1},{3,4},{4,3},{5,6},{6,5},{9,10},{10,9},{11,12},{12,11},... | collective-permute-start | bytes 3932168 | tf_op jit(solution)/shard_map/ppermute | solution.py:651
  56.7 22.1 %collective-permute-start.5 = (f32[14,56,256]{2,1,0:T(8,128)S(1)}, f32[14,56,256]{2,1,0:T(8,128)S(1)}, u32[]{:S(2)}, u32[]{:S(2)}) collective-permute-start(f32[14,56,256]{2,1,0:T(8,128)S(1)} %broadcast_select_fusion.1), channel_id=1, source_target_pairs={{1,2},{2,1},{5,6},{6,5},{7,4},{0,3},{9,10},{10,9},{13,14},{14,13},... | collective-permute-start | bytes 2408456 | tf_op jit(solution)/shard_map/ppermute | solution.py:664
  59.2 8.6 %copy-start.2 = (f32[2,4,80,256]{3,2,1,0:T(8,128)S(1)}, f32[2,4,80,256]{3,2,1,0:T(8,128)}, u32[]{:S(2)}) copy-start(f32[2,4,80,256]{3,2,1,0:T(8,128)} %get-tuple-element.50) | copy-start | bytes 1966084
  59.2 8.6 %copy-start.17 = (f32[3,80,256]{2,1,0:T(8,128)S(1)}, f32[3,80,256]{2,1,0:T(8,128)}, u32[]{:S(2)}) copy-start(f32[3,80,256]{2,1,0:T(8,128)} %get-tuple-element.56) | copy-start | bytes 737284
  59.2 8.6 %copy-start.18 = (f32[3,80,256]{2,1,0:T(8,128)S(1)}, f32[3,80,256]{2,1,0:T(8,128)}, u32[]{:S(2)}) copy-start(f32[3,80,256]{2,1,0:T(8,128)} %get-tuple-element.80) | copy-start | bytes 737284
  64.5 39.0 %collective-permute-start.8 = (f32[14,80,256]{2,1,0:T(8,128)}, f32[14,80,256]{2,1,0:T(8,128)}, u32[]{:S(2)}, u32[]{:S(2)}) collective-permute-start(f32[14,80,256]{2,1,0:T(8,128)} %broadcast_select_fusion), channel_id=1, source_target_pairs={{1,2},{2,1},{5,6},{6,5},{7,4},{0,3},{9,10},{10,9},{13,14},{14,13},... | collective-permute-start | bytes 3440648 | tf_op jit(solution)/shard_map/ppermute | solution.py:664
  70.4 13.0 %copy-start.16 = (f32[4,256,256]{2,1,0:T(8,128)}, f32[4,256,256]{2,1,0:T(8,128)S(1)}, u32[]{:S(2)}) copy-start(f32[4,256,256]{2,1,0:T(8,128)S(1)} %collective-permute-done.1.mate_pot) | copy-start | bytes 3145732
  70.4 57.6 %collective-permute-start.11 = (f32[16,80,256]{2,1,0:T(8,128)}, f32[16,80,256]{2,1,0:T(8,128)S(1)}, u32[]{:S(2)}, u32[]{:S(2)}) collective-permute-start(f32[16,80,256]{2,1,0:T(8,128)} %bitcast.16), channel_id=1, source_target_pairs={{1,2},{2,1},{3,4},{4,3},{5,6},{6,5},{9,10},{10,9},{11,12},{12,11},... | collective-permute-start | bytes 3932168 | tf_op jit(solution)/shard_map/ppermute | solution.py:651
  78.8 4.6 %copy-start.24 = (f32[14,56,256]{2,1,0:T(8,128)}, f32[14,56,256]{2,1,0:T(8,128)S(1)}, u32[]{:S(2)}) copy-start(f32[14,56,256]{2,1,0:T(8,128)S(1)} %collective-permute-done.5.refs_1_) | copy-start | bytes 2408452
  78.8 115.8 %collective-permute-start.18 = (f32[16,40,256]{2,1,0:T(8,128)}, f32[16,40,256]{2,1,0:T(8,128)S(1)}, u32[]{:S(2)}, u32[]{:S(2)}) collective-permute-start(f32[16,40,256]{2,1,0:T(8,128)} %bitcast.21), channel_id=1, source_target_pairs={{1,2},{2,1},{3,4},{4,3},{5,6},{6,5},{9,10},{10,9},{11,12},{12,11},... | collective-permute-start | bytes 1966088 | tf_op jit(solution)/shard_map/ppermute | solution.py:651
  83.4 44.6 %collective-permute-start.13 = (f32[14,80,256]{2,1,0:T(8,128)}, f32[14,80,256]{2,1,0:T(8,128)S(1)}, u32[]{:S(2)}, u32[]{:S(2)}) collective-permute-start(f32[14,80,256]{2,1,0:T(8,128)} %slice_select_fusion), channel_id=1, source_target_pairs={{1,2},{2,1},{5,6},{6,5},{7,4},{0,3},{9,10},{10,9},{13,14},{14,13},... | collective-permute-start | bytes 3440648 | tf_op jit(solution)/shard_map/ppermute | solution.py:664
  101.3 93.4 %collective-permute-start.19 = (f32[14,40,256]{2,1,0:T(8,128)}, f32[14,40,256]{2,1,0:T(8,128)}, u32[]{:S(2)}, u32[]{:S(2)}) collective-permute-start(f32[14,40,256]{2,1,0:T(8,128)} %slice_select_fusion.1), channel_id=1, source_target_pairs={{1,2},{2,1},{5,6},{6,5},{7,4},{0,3},{9,10},{10,9},{13,14},{14,13},... | collective-permute-start | bytes 1720328 | tf_op jit(solution)/shard_map/ppermute | solution.py:664
  103.5 23.0 %collective-permute-start.9 = (f32[4,48,256]{2,1,0:T(8,128)}, f32[4,48,256]{2,1,0:T(8,128)S(1)}, u32[]{:S(2)}, u32[]{:S(2)}) collective-permute-start(f32[4,48,256]{2,1,0:T(8,128)} %get-tuple-element.35), channel_id=1, source_target_pairs={{0,16},{8,24},{1,17},{9,25},{2,18},{10,26},{3,19},{11,27},{4,20},{... | collective-permute-start | bytes 589832 | tf_op jit(solution)/shard_map/ppermute | solution.py:681
  126.5 1.5 copy-start.20
  126.5 26.6 %collective-permute-start.14 = (f32[4,80,256]{2,1,0:T(8,128)}, f32[4,80,256]{2,1,0:T(8,128)}, u32[]{:S(2)}, u32[]{:S(2)}) collective-permute-start(f32[4,80,256]{2,1,0:T(8,128)} %get-tuple-element.39), channel_id=1, source_target_pairs={{0,16},{8,24},{1,17},{9,25},{2,18},{10,26},{3,19},{11,27},{4,20},{... | collective-permute-start | bytes 983048 | tf_op jit(solution)/shard_map/ppermute | solution.py:681
  128.0 65.6 %copy-start.14 = (f32[256,256]{1,0:T(8,128)S(1)}, f32[256,256]{1,0:T(8,128)}, u32[]{:S(2)}) copy-start(f32[256,256]{1,0:T(8,128)} %get-tuple-element.76) | copy-start | bytes 786436
  128.0 1.1 copy-start.11
  129.1 1.0 copy-start.13
  151.7 42.9 %collective-permute-start.16 = (f32[4,80,256]{2,1,0:T(8,128)}, f32[4,80,256]{2,1,0:T(8,128)S(1)}, u32[]{:S(2)}, u32[]{:S(2)}) collective-permute-start(f32[4,80,256]{2,1,0:T(8,128)} %get-tuple-element.42), channel_id=1, source_target_pairs={{0,16},{8,24},{1,17},{9,25},{2,18},{10,26},{3,19},{11,27},{4,20},{... | collective-permute-start | bytes 983048 | tf_op jit(solution)/shard_map/ppermute | solution.py:681
  154.1 39.5 %collective-permute-start.15 = (f32[4,80,128]{2,1,0:T(8,128)S(1)}, f32[4,80,128]{2,1,0:T(8,128)S(1)}, u32[]{:S(2)}, u32[]{:S(2)}) collective-permute-start(f32[4,80,128]{2,1,0:T(8,128)S(1)} %get-tuple-element.58), channel_id=1, source_target_pairs={{0,1},{1,0},{2,3},{3,2},{4,5},{5,4},{6,7},{7,6},{8,9},{9,8},{10,11... | collective-permute-start | bytes 491528 | tf_op jit(solution)/shard_map/ppermute | solution.py:553
  193.5 36.2 %collective-permute-start.10 = (f32[4,48,128]{2,1,0:T(8,128)S(1)}, f32[4,48,128]{2,1,0:T(8,128)S(1)}, u32[]{:S(2)}, u32[]{:S(2)}) collective-permute-start(f32[4,48,128]{2,1,0:T(8,128)S(1)} %get-tuple-element.65), channel_id=1, source_target_pairs={{0,1},{1,0},{2,3},{3,2},{4,5},{5,4},{6,7},{7,6},{8,9},{9,8},{10,11... | collective-permute-start | bytes 294920 | tf_op jit(solution)/shard_map/ppermute | solution.py:553
  194.7 0.8 copy-start.19
  212.5 12.5 %collective-permute-start.20 = (f32[4,48,256]{2,1,0:T(8,128)}, f32[4,48,256]{2,1,0:T(8,128)S(1)}, u32[]{:S(2)}, u32[]{:S(2)}) collective-permute-start(f32[4,48,256]{2,1,0:T(8,128)} %get-tuple-element.45), channel_id=1, source_target_pairs={{0,16},{8,24},{1,17},{9,25},{2,18},{10,26},{3,19},{11,27},{4,20},{... | collective-permute-start | bytes 589832 | tf_op jit(solution)/shard_map/ppermute | solution.py:681
  213.8 13.8 %collective-permute-start.17 = (f32[4,80,128]{2,1,0:T(8,128)S(1)}, f32[4,80,128]{2,1,0:T(8,128)S(1)}, u32[]{:S(2)}, u32[]{:S(2)}) collective-permute-start(f32[4,80,128]{2,1,0:T(8,128)S(1)} %get-tuple-element.60), channel_id=1, source_target_pairs={{0,1},{1,0},{2,3},{3,2},{4,5},{5,4},{6,7},{7,6},{8,9},{9,8},{10,11... | collective-permute-start | bytes 491528 | tf_op jit(solution)/shard_map/ppermute | solution.py:553
  225.0 3.7 %collective-permute-start.21 = (f32[4,48,128]{2,1,0:T(8,128)S(1)}, f32[4,48,128]{2,1,0:T(8,128)S(1)}, u32[]{:S(2)}, u32[]{:S(2)}) collective-permute-start(f32[4,48,128]{2,1,0:T(8,128)S(1)} %get-tuple-element.67), channel_id=1, source_target_pairs={{0,1},{1,0},{2,3},{3,2},{4,5},{5,4},{6,7},{7,6},{8,9},{9,8},{10,11... | collective-permute-start | bytes 294920 | tf_op jit(solution)/shard_map/ppermute | solution.py:553
  235.7 6.5 %collective-permute-start.22 = (f32[256,128]{1,0:T(8,128)S(1)}, f32[256,128]{1,0:T(8,128)S(1)}, u32[]{:S(2)}, u32[]{:S(2)}) collective-permute-start(f32[256,128]{1,0:T(8,128)S(1)} %get-tuple-element.63), channel_id=1, source_target_pairs={{0,2},{1,3},{2,0},{3,1},{4,6},{5,7},{6,4},{7,5},{8,10},{9,11},{10,... | collective-permute-start | bytes 393224 | tf_op jit(solution)/shard_map/ppermute | solution.py:577
  238.1 8.2 %collective-permute-start.23 = (f32[256,128]{1,0:T(8,128)S(1)}, f32[256,128]{1,0:T(8,128)S(1)}, u32[]{:S(2)}, u32[]{:S(2)}) collective-permute-start(f32[256,128]{1,0:T(8,128)S(1)} %get-tuple-element.62), channel_id=1, source_target_pairs={{0,4},{1,5},{2,6},{3,7},{4,0},{5,1},{6,2},{7,3},{8,12},{9,13},{10,... | collective-permute-start | bytes 393224 | tf_op jit(solution)/shard_map/ppermute | solution.py:577
  239.1 7.2 %collective-permute-start.24 = (f32[256,128]{1,0:T(8,128)S(1)}, f32[256,128]{1,0:T(8,128)S(1)}, u32[]{:S(2)}, u32[]{:S(2)}) collective-permute-start(f32[256,128]{1,0:T(8,128)S(1)} %get-tuple-element.61), channel_id=1, source_target_pairs={{0,6},{1,7},{2,4},{3,5},{4,2},{5,3},{6,0},{7,1},{8,14},{9,15},{10,... | collective-permute-start | bytes 393224 | tf_op jit(solution)/shard_map/ppermute | solution.py:577
  242.2 4.1 %copy-start.21 = (f32[256,128]{1,0:T(8,128)}, f32[256,128]{1,0:T(8,128)S(1)}, u32[]{:S(2)}) copy-start(f32[256,128]{1,0:T(8,128)S(1)} %collective-permute-done.22.refs_0_) | copy-start | bytes 393220
  246.3 0.7 copy-start.22
  246.4 0.7 copy-start.23
  254.1 1.0 copy-start.3
  254.2 2.0 collective-permute-start.25
  281.0 3.7 %collective-permute-start.26 = (f32[16,6]{1,0:T(8,128)S(1)}, f32[16,6]{1,0:T(8,128)S(1)}, u32[]{:S(2)}, u32[]{:S(2)}) collective-permute-start(f32[16,6]{1,0:T(8,128)S(1)} %slice_select_fusion.21), channel_id=1, source_target_pairs={{0,4},{1,5},{2,6},{3,7},{4,0},{5,1},{6,2},{7,3},{8,12},{9,13},{10,... | collective-permute-start | bytes 1160 | tf_op jit(solution)/shard_map/ppermute | solution.py:604
  285.4 3.7 %collective-permute-start.27 = (f32[8,6]{1,0:T(8,128)S(1)}, f32[8,6]{1,0:T(8,128)S(1)}, u32[]{:S(2)}, u32[]{:S(2)}) collective-permute-start(f32[8,6]{1,0:T(8,128)S(1)} %slice_select_fusion.22), channel_id=1, source_target_pairs={{0,2},{1,3},{2,0},{3,1},{4,6},{5,7},{6,4},{7,5},{8,10},{9,11},{10,... | collective-permute-start | bytes 584 | tf_op jit(solution)/shard_map/ppermute | solution.py:604
  289.0 1.2 collective-permute-start.28

commit v2 on v0

--- a/solution.py
+++ b/solution.py
@@ -11,7 +11,8 @@
 ORDER = 4
 LANES = 128
 SUBS = 8
-SHARES = (6, 10, 10, 6)
+SHARES = (6, 11, 11, 4)
+AHEAD = 2
 
 time_step = 0.2
 four_pi = 12.566370614359172
@@ -82,7 +83,7 @@
 
 def taylor_kernel(
     span, sources, planes, first_call, flag_ref, mask_ref, own_ref, pot_ref, add_ref, mate_ref,
-    mate_pot, mate_add, *refs
+    mate_pot, mate_add, table_ref, *refs
 ):
     out_rows, _, window = span
     msgs, refs = refs[: 2 * len(sources)], refs[2 * len(sources) :]
@@ -293,8 +294,12 @@
     lax.fori_loop(0, n_vectors, vector, 0)
 
     def spread(p, carry):
+        flat = acc[p].reshape(height, tiles * LANES)
+        wave = jnp.dot(
+            flat, table_ref[...], precision=highest, preferred_element_type=jnp.float32
+        ).reshape(acc.shape[1:])
         for r in range(rows):
-            scatter(r_out, (p,), r, acc[p, r])
+            scatter(r_out, (p,), r, wave[r])
         return carry
 
     lax.fori_loop(0, planes, spread, 0)
@@ -312,7 +317,7 @@
         copy.wait()
 
 
-def taylor(span, flags, mask, own, potential, added, mates, sources, b):
+def taylor(span, flags, mask, own, potential, added, mates, table, sources, b):
     n_fields, planes, _, size_z = own.shape
     out_rows, _, window = span
     height = window[1] - window[0]
@@ -323,8 +328,9 @@
     natural = lambda *lead: pltpu.VMEM((tiles,) + lead + (height, LANES), jnp.float32)
     hbm = pl.BlockSpec(memory_space=pl.ANY)
     smem = pl.BlockSpec(memory_space=pltpu.SMEM)
+    vmem = pl.BlockSpec(memory_space=pltpu.VMEM)
     shape = [(piece, to) for _, piece, to in sources]
-    operands = [own, potential, added, *mates] + [m for msgs, _, _ in sources for m in msgs]
+    operands = [own, potential, added, *mates, table] + [m for msgs, _, _ in sources for m in msgs]
     aliases = {}
     if b is not None:
         operands.append(b)
@@ -335,7 +341,7 @@
             jax.ShapeDtypeStruct(own.shape, jnp.float32),
             jax.ShapeDtypeStruct((planes, out_rows[1] - out_rows[0], size_z), jnp.float32),
         ),
-        in_specs=[smem, smem] + [hbm] * len(operands),
+        in_specs=[smem, smem] + [hbm] * 6 + [vmem] + [hbm] * (len(operands) - 7),
         out_specs=(hbm, hbm),
         input_output_aliases=aliases,
         scratch_shapes=[
@@ -412,7 +418,7 @@
     )(received, added, b, states)
 
 
-def moments_kernel(f_ref, low_ref, high_ref, r_ref, to_right, to_left):
+def moments_kernel(side_ref, f_ref, low_ref, high_ref, r_ref, *outs):
     planes = f_ref.shape[0]
 
     def step(q, carry):
@@ -424,8 +430,8 @@
         down = high_ref[planes - 1, at, :] * f_ref[planes - 1, at, :]
         for j in range(planes - 2, -1, -1):
             down = r * down + high_ref[j, at, :] * f_ref[j, at, :]
-        to_right[at, :] = up
-        to_left[at, :] = down
+        for k, out in enumerate(outs):
+            out[at, :] = jnp.where(side_ref[k] > 0.5, down, up)
         return carry
 
     lax.fori_loop(0, f_ref.shape[1] // SUBS, step, 0, unroll=4)
@@ -496,9 +502,6 @@
     def swap(self, array):
         return lax.ppermute(array, "grid", [(i, i ^ 1) for i in range(self.count)])
 
-    def transform_z(self, density):
-        return jnp.einsum("xyz,zl->xyl", density, self.table_z, precision=highest)
-
     def add(self, piece, at):
         mine, got = self.pick(piece, True), self.swap(self.pick(piece, False))
         both = jnp.where(
@@ -510,19 +513,18 @@
     def solve(self):
         shape = jax.ShapeDtypeStruct(self.r.shape, jnp.float32)
         vmem = pl.BlockSpec(memory_space=pltpu.VMEM)
-        to_right, to_left = pl.pallas_call(
+        smem = pl.BlockSpec(memory_space=pltpu.SMEM)
+        sums = pl.pallas_call(
             moments_kernel,
-            out_shape=(shape, shape),
-            in_specs=[vmem] * 4,
-            out_specs=(vmem, vmem),
+            out_shape=[shape] * len(self.hops),
+            in_specs=[smem] + [vmem] * 4,
+            out_specs=[vmem] * len(self.hops),
             name="moments",
-        )(self.total, self.low, self.high, self.r)
-        far = []
-        for k in self.hops:
-            sent = jnp.where((self.chip ^ k) > self.chip, to_right, to_left)
-            far.append(
-                lax.ppermute(sent, "grid", [(i, i ^ (2 * k)) for i in range(self.count)])
-            )
+        )(self.side, self.total, self.low, self.high, self.r)
+        far = [
+            lax.ppermute(sent, "grid", [(i, i ^ (2 * k)) for i in range(self.count)])
+            for k, sent in zip(self.hops, sums)
+        ]
         field = pl.pallas_call(
             functools.partial(solve_kernel, len(far)),
             out_shape=jax.ShapeDtypeStruct(self.total.shape, jnp.float32),
@@ -582,27 +584,28 @@
         parts = [own[split:, :, lo:hi].reshape(-1, hi - lo, size_z), edge(potential), edge(added)]
         return jnp.concatenate(parts)
 
-    cut = layout[0][1][1]
-    hops = [None] * len(layout)
-    if relayed:
-        hops[0] = lax.ppermute(message(0, cut), "grid", first_leg)
-    messages = []
-    mates = None
-    for c, (_, (lo, hi), _) in enumerate(layout):
-        block = own[:split, :, lo:hi].reshape(-1, hi - lo, size_z)
+    ends = jnp.logical_or(place == 0, place == count - 1)
+
+    def exchange(c, after):
+        lo, hi = layout[c][1]
+        block = own
+        if after is not None:
+            block, _ = lax.optimization_barrier((own, after))
+        block = block[:split, :, lo:hi].reshape(-1, hi - lo, size_z)
         direct = lax.ppermute(block, "grid", chip_pairs)
         rest, pairs = message(lo, hi), chip_pairs
-        if mates is None:
-            mates = [lax.ppermute(f, "grid", mate_pairs) for f in (own, potential, added)]
         if relayed:
-            if c == 1:
-                late = lax.ppermute(message(cut, size_y), "grid", first_leg)
-                hops[1:] = [late[:, l - cut : h - cut] for _, (l, h), _ in layout[1:]]
-            ends = jnp.logical_or(place == 0, place == count - 1)
-            rest = jnp.where(ends, hops[c], rest)
+            hop = lax.ppermute(rest, "grid", first_leg)
+            if after is not None:
+                hop, _ = lax.optimization_barrier((hop, after))
+            rest = jnp.where(ends, hop, rest)
             pairs = [p for p in chip_pairs if set(p) != {left, right}] + second_leg
-        messages.append((direct, lax.ppermute(rest, "grid", pairs)))
-
+        elif after is not None:
+            rest, _ = lax.optimization_barrier((rest, after))
+        return direct, lax.ppermute(rest, "grid", pairs)
+
+    messages = [exchange(c, None) for c in range(AHEAD)]
+    mates = [lax.ppermute(f, "grid", mate_pairs) for f in (own, potential, added)]
     poisson = Poisson(planes, size_y, size_z)
     group_pairs = [(g, g + groups // 2) for g in range(groups // 2)]
     b, arrived = None, []
@@ -617,8 +620,10 @@
             b, arrived[c - 2] = lax.optimization_barrier((b, arrived[c - 2]))
         if c == len(layout) - 1:
             b, arrived[c - 1] = lax.optimization_barrier((b, arrived[c - 1]))
-        b, rho = taylor(span, flags, mask, own, potential, added, mates, sources, b)
-        arrived.append(lax.ppermute(poisson.transform_z(rho), "grp", group_pairs))
+        b, rho = taylor(span, flags, mask, own, potential, added, mates, poisson.table_z, sources, b)
+        if c + AHEAD < len(layout):
+            messages.append(exchange(c + AHEAD, rho))
+        arrived.append(lax.ppermute(rho, "grp", group_pairs))
     for c, ((o0, _), _, _) in enumerate(layout):
         poisson.add(arrived[c], o0)
     received = poisson.solve()

time: 297 us -> 277 us (0.933)
  starting transfers between devices: 78.3 us -> 61.3 us
  matrix products: 22.6 us -> 12.4 us
  waiting for transfers between devices: 36 us -> 42.5 us
  local copies, waits for them, and re-layouts: 19.9 us -> 14.6 us
  Pallas kernels: 115 us -> 120 us
    ppermute x5, starting transfers between devices: 38.3 us -> 14.3 us  [swap(): return lax.ppermute(array, 'grid', [(i, i ^ 1) for i in range(self.count)])]
    dot_general x4 -> x0, matrix products: 11 us -> none  [transform_z(): return jnp.einsum('xyz,zl->xyl', density, self.table_z, precision=highest)]
    ppermute x14 -> x16, starting transfers between devices: 31.3 us -> 39.8 us  [the longest x4 15.2 us: exchange(): hop = lax.ppermute(rest, 'grid', first_leg)]
    ppermute x14 -> x16, waiting for transfers between devices: 24 us -> 30.7 us  [the longest x4 24.4 us: on_device(): arrived.append(lax.ppermute(rho, 'grp', group_pairs))]
    pallas_call x4, Pallas kernels: 91.5 us -> 96.3 us  [taylor(): pl.pallas_call(functools.partial(taylor_kernel, span, shape, planes, b is...]
    slice x4 -> x3, local copies, waits for them, and re-layouts: 7.31 us -> 3.64 us  [message(): own[split:, :, lo:hi].reshape(-1, hi - lo, size_z)]
    slice x3 -> x4, local copies, waits for them, and re-layouts: 7.64 us -> 8.48 us  [exchange(): block = block[:split, :, lo:hi].reshape(-1, hi - lo, size_z)]
  transfers between devices with their start and end apart: 28 -> 30, of which waited for: 9 -> 11; matrix products, arithmetic and copies ran while one was open for 17% -> 14% of each run, Pallas kernels for 31% -> 35%
where the time goes in v2:
time: 277 us; the launch traced here: 274 us
  Pallas kernels  120 us (43%)
  starting transfers between devices  61.3 us (22%)
  waiting for transfers between devices  42.5 us (15%)
  other arithmetic  23 us (8%)
  local copies, waits for them, and re-layouts  14.6 us (5%)
  matrix products  12.4 us (4%)
    pallas_call x4, Pallas kernels, taylor(): pl.pallas_call(functools.partial(taylor_kernel, span, shape, planes, b is...  96.3 us
    ppermute x4, waiting for transfers between devices, on_device(): arrived.append(lax.ppermute(rho, 'grp', group_pairs))  24.4 us
    pallas_call x1, Pallas kernels, elements(): pl.pallas_call(functools.partial(elements_kernel, n_states, parts, planes...  16.8 us
    ppermute x4, starting transfers between devices, exchange(): hop = lax.ppermute(rest, 'grid', first_leg)  15.2 us
    ppermute x5, starting transfers between devices, swap(): return lax.ppermute(array, 'grid', [(i, i ^ 1) for i in range(self.count)])  14.3 us
    ppermute x4, starting transfers between devices, exchange(): direct = lax.ppermute(block, 'grid', chip_pairs)  14.2 us
    slice x4, local copies, waits for them, and re-layouts, exchange(): block = block[:split, :, lo:hi].reshape(-1, hi - lo, size_z)  8.48 us
    select_n x4, other arithmetic, exchange(): rest = jnp.where(ends, hop, rest)  6.22 us
  transfers between devices with their start and end apart: 30, of which 11 were waited for; matrix products, arithmetic and copies ran while one was open for 14% of the time, Pallas kernels for 35%

profile of v2, /device:TPU:28, one launch (start us, length us, event | category | flops | bytes accessed | tf_op | source)
XLA Modules:
  0.0 274.4 jit_solution(17041539720641789114)
XLA Ops:
  0.5 1.0 slice.208
  1.6 1.0 slice_select_fusion.5
  2.7 1.0 pad_maximum_fusion.2
  3.7 3.3 %collective-permute-start.4 = (f32[14,56,256]{2,1,0:T(8,128)}, f32[14,56,256]{2,1,0:T(8,128)}, u32[]{:S(2)}, u32[]{:S(2)}) collective-permute-start(f32[14,56,256]{2,1,0:T(8,128)} %pad_maximum_fusion.2), channel_id=1, source_target_pairs={{3,7},{4,0},{11,15},{12,8},{19,23},{20,16},{27,31},{28,24}} | collective-permute-start | bytes 2408456 | tf_op jit(solution)/shard_map/ppermute | solution.py:598
  7.0 2.2 slice.207
  9.2 3.9 %collective-permute-start.3 = (f32[16,56,256]{2,1,0:T(8,128)}, f32[16,56,256]{2,1,0:T(8,128)}, u32[]{:S(2)}, u32[]{:S(2)}) collective-permute-start(f32[16,56,256]{2,1,0:T(8,128)} %bitcast.11), channel_id=1, source_target_pairs={{1,2},{2,1},{3,4},{4,3},{5,6},{6,5},{9,10},{10,9},{11,12},{12,11},... | collective-permute-start | bytes 2752520 | tf_op jit(solution)/shard_map/ppermute | solution.py:595
  13.2 1.6 fusion.68
  14.9 1.2 pad_maximum_fusion
  16.1 2.4 collective-permute-start.7
  19.7 1.2 pad_maximum_fusion.1
  20.9 1.8 fusion.22.table_ref
  23.5 1.2 multiply_exponential_fusion
  24.7 2.0 broadcast_select_fusion.2
  26.7 6.0 %collective-permute-done.3.refs_0_ = f32[16,56,256]{2,1,0:T(8,128)} collective-permute-done((f32[16,56,256]{2,1,0:T(8,128)}, f32[16,56,256]{2,1,0:T(8,128)}, u32[]{:S(2)}, u32[]{:S(2)}) %collective-permute-start.3) | collective-permute-done | bytes 917536 | tf_op jit(solution)/shard_map/ppermute | solution.py:595
  32.6 1.3 collective-permute-start.5
  34.6 2.6 slice.211
  37.2 1.0 slice.221
  38.2 1.7 pad_maximum_fusion.3
  39.9 3.7 %collective-permute-start.6 = (f32[16,88,256]{2,1,0:T(8,128)}, f32[16,88,256]{2,1,0:T(8,128)}, u32[]{:S(2)}, u32[]{:S(2)}) collective-permute-start(f32[16,88,256]{2,1,0:T(8,128)} %bitcast.75), channel_id=1, source_target_pairs={{1,2},{2,1},{3,4},{4,3},{5,6},{6,5},{9,10},{10,9},{11,12},{12,11},... | collective-permute-start | bytes 4325384 | tf_op jit(solution)/shard_map/ppermute | solution.py:595
  43.5 4.9 %collective-permute-start.12 = (f32[14,88,256]{2,1,0:T(8,128)}, f32[14,88,256]{2,1,0:T(8,128)}, u32[]{:S(2)}, u32[]{:S(2)}) collective-permute-start(f32[14,88,256]{2,1,0:T(8,128)} %pad_maximum_fusion.1), channel_id=1, source_target_pairs={{3,7},{4,0},{11,15},{12,8},{19,23},{20,16},{27,31},{28,24}} | collective-permute-start | bytes 3784712 | tf_op jit(solution)/shard_map/ppermute | solution.py:598
  48.5 2.2 broadcast_select_fusion.1
  50.7 1.3 collective-permute-start.8
  52.6 2.1 exponential-minus-one_negate_fusion
  55.0 4.6 %collective-permute-start.19 = (f32[14,24,256]{2,1,0:T(8,128)}, f32[14,24,256]{2,1,0:T(8,128)S(1)}, u32[]{:S(2)}, u32[]{:S(2)}) collective-permute-start(f32[14,24,256]{2,1,0:T(8,128)} %pad_maximum_fusion.3), channel_id=1, source_target_pairs={{3,7},{4,0},{11,15},{12,8},{19,23},{20,16},{27,31},{28,24}} | collective-permute-start | bytes 1032200 | tf_op jit(solution)/shard_map/ppermute | solution.py:598
  59.6 20.2 %taylor.4 = (f32[6,4,256,256]{3,2,1,0:T(8,128)}, f32[4,48,256]{2,1,0:T(8,128)}) custom-call(s32[2]{0:T(128)} %add_convert_fusion.1.flag_ref, f32[2]{0:T(128)} %add_convert_fusion.2.mask_ref, f32[6,4,256,256]{3,2,1,0:T(8,128)} %bitcast.52, f32[4,256,256]{2,1,0:T(8,128)} %pot_ref.7, f32[4,256,256]{2,1,0:T(8,128)} %bitcast.60, ...), custom_call_target="tpu_custom_call" | custom-call | flops 6881280000 | bytes 20971520 | tf_op jit(solution)/shard_map/taylor/pallas_call | solution.py:338
  79.8 1.3 collective-permute-start.9
  81.1 2.7 slice.174
  83.8 3.5 %collective-permute-start.11 = (f32[16,88,256]{2,1,0:T(8,128)}, f32[16,88,256]{2,1,0:T(8,128)}, u32[]{:S(2)}, u32[]{:S(2)}) collective-permute-start(f32[16,88,256]{2,1,0:T(8,128)} %bitcast.16), channel_id=1, source_target_pairs={{1,2},{2,1},{3,4},{4,3},{5,6},{6,5},{9,10},{10,9},{11,12},{12,11},... | collective-permute-start | bytes 4325384 | tf_op jit(solution)/shard_map/ppermute | solution.py:595
  87.3 1.3 broadcast_select_fusion
  88.6 1.3 collective-permute-start.13
  89.9 29.2 %taylor.5 = (f32[6,4,256,256]{3,2,1,0:T(8,128)}, f32[4,88,256]{2,1,0:T(8,128)}) custom-call(s32[2]{0:T(128)} %add_convert_fusion.1.flag_ref, f32[2]{0:T(128)} %add_convert_fusion.2.mask_ref, f32[6,4,256,256]{3,2,1,0:T(8,128)} %bitcast.54, f32[4,256,256]{2,1,0:T(8,128)} %pot_ref.7, f32[4,256,256]{2,1,0:T(8,128)} %bitcast.61, ...), custom_call_target="tpu_custom_call", output_to_operand_aliasing={{0}: (13, {})} | custom-call | flops 12779520000 | bytes 20971520 | tf_op jit(solution)/shard_map/taylor/pallas_call | solution.py:338
  119.1 1.3 collective-permute-start.14
  120.4 0.8 broadcast_select_fusion.3
  121.2 1.3 collective-permute-start.20
  122.5 1.0 slice.186
  123.5 3.1 %collective-permute-start.18 = (f32[16,24,256]{2,1,0:T(8,128)S(1)}, f32[16,24,256]{2,1,0:T(8,128)S(1)}, u32[]{:S(2)}, u32[]{:S(2)}) collective-permute-start(f32[16,24,256]{2,1,0:T(8,128)S(1)} %bitcast.76), channel_id=1, source_target_pairs={{1,2},{2,1},{3,4},{4,3},{5,6},{6,5},{9,10},{10,9},{11,12},{12,11},... | collective-permute-start | bytes 1179656 | tf_op jit(solution)/shard_map/ppermute | solution.py:595
  126.7 1.0 copy-done.8
  127.7 29.1 %taylor.6 = (f32[6,4,256,256]{3,2,1,0:T(8,128)}, f32[4,88,256]{2,1,0:T(8,128)}) custom-call(s32[2]{0:T(128)} %add_convert_fusion.1.flag_ref, f32[2]{0:T(128)} %add_convert_fusion.2.mask_ref, f32[6,4,256,256]{3,2,1,0:T(8,128)} %bitcast.56, f32[4,256,256]{2,1,0:T(8,128)} %pot_ref.7, f32[4,256,256]{2,1,0:T(8,128)} %bitcast.62, ...), custom_call_target="tpu_custom_call", output_to_operand_aliasing={{0}: (13, {})} | custom-call | flops 12779520000 | bytes 20971520 | tf_op jit(solution)/shard_map/taylor/pallas_call | solution.py:338
  156.9 14.0 %collective-permute-start.15 = (f32[4,88,128]{2,1,0:T(8,128)S(1)}, f32[4,88,128]{2,1,0:T(8,128)S(1)}, u32[]{:S(2)}, u32[]{:S(2)}) collective-permute-start(f32[4,88,128]{2,1,0:T(8,128)S(1)} %get-tuple-element.54), channel_id=1, source_target_pairs={{0,1},{1,0},{2,3},{3,2},{4,5},{5,4},{6,7},{7,6},{8,9},{9,8},{10,11... | collective-permute-start | bytes 540680 | tf_op jit(solution)/shard_map/ppermute | solution.py:503
  170.9 1.3 collective-permute-start.16
  172.3 1.9 fusion.7
  174.2 17.6 %collective-permute-done.16 = f32[4,88,256]{2,1,0:T(8,128)S(1)} collective-permute-done((f32[4,88,256]{2,1,0:T(8,128)}, f32[4,88,256]{2,1,0:T(8,128)S(1)}, u32[]{:S(2)}, u32[]{:S(2)}) %collective-permute-start.16) | collective-permute-done | bytes 360480 | tf_op jit(solution)/shard_map/ppermute | solution.py:626
  192.6 17.8 %taylor.7 = (f32[6,4,256,256]{3,2,1,0:T(8,128)}, f32[4,32,256]{2,1,0:T(8,128)}) custom-call(s32[2]{0:T(128)} %add_convert_fusion.1.flag_ref, f32[2]{0:T(128)} %add_convert_fusion.2.mask_ref, f32[6,4,256,256]{3,2,1,0:T(8,128)} %bitcast.57, f32[4,256,256]{2,1,0:T(8,128)} %pot_ref.7, f32[4,256,256]{2,1,0:T(8,128)} %bitcast.63, ...), custom_call_target="tpu_custom_call", output_to_operand_aliasing={{0}: (13, {})} | custom-call | flops 4915200000 | bytes 20971520 | tf_op jit(solution)/shard_map/taylor/pallas_call | solution.py:338
  210.4 1.5 collective-permute-start.21
  212.1 6.8 %collective-permute-done.21 = f32[4,32,256]{2,1,0:T(8,128)S(1)} collective-permute-done((f32[4,32,256]{2,1,0:T(8,128)}, f32[4,32,256]{2,1,0:T(8,128)S(1)}, u32[]{:S(2)}, u32[]{:S(2)}) %collective-permute-start.21) | collective-permute-done | bytes 131104 | tf_op jit(solution)/shard_map/ppermute | solution.py:626
  219.0 1.0 fusion.13
  220.2 1.0 fusion.41
  221.2 2.1 fusion.2.f_ref
  223.3 2.9 %moments.1 = (f32[256,128]{1,0:T(8,128)}, f32[256,128]{1,0:T(8,128)}, f32[256,128]{1,0:T(8,128)}) custom-call(f32[3]{0:T(128)} %add_convert_fusion.side_ref, f32[8,256,128]{2,1,0:T(8,128)} %fusion.2.f_ref, f32[8,256,128]{2,1,0:T(8,128)} %get-tuple-element.60.low_ref, f32[8,256,128]{2,1,0:T(8,128)} %get-tuple-element.59.high_ref, ...), custom_call_target="tpu_custom_call" | custom-call | tf_op jit(solution)/shard_map/moments/pallas_call | solution.py:517
  226.7 1.3 collective-permute-start.24
  227.9 1.9 collective-permute-start.25
  229.8 3.1 %collective-permute-done.23.refs_0_ = f32[256,128]{1,0:T(8,128)S(1)} collective-permute-done((f32[256,128]{1,0:T(8,128)}, f32[256,128]{1,0:T(8,128)S(1)}, u32[]{:S(2)}, u32[]{:S(2)}) %collective-permute-start.23) | collective-permute-done | bytes 131104 | tf_op jit(solution)/shard_map/ppermute | solution.py:525
  232.9 2.3 collective-permute-done.24.refs_1_
  235.8 3.7 %solve.1 = f32[8,256,128]{2,1,0:T(8,128)} custom-call(f32[3]{0:T(128)} %add_convert_fusion.side_ref, f32[8,256,128]{2,1,0:T(8,128)} %fusion.2.f_ref, f32[8,256,128]{2,1,0:T(8,128)} %get-tuple-element.60.low_ref, f32[8,256,128]{2,1,0:T(8,128)} %get-tuple-element.59.high_ref, f32[256,128]{1,0:T(8,128)} %get-tuple-element.64.r_ref, ...), custom_call_target="tpu_custom_call" | custom-call | tf_op jit(solution)/shard_map/solve/pallas_call | solution.py:528
  239.6 3.3 %convolution_bitcast_fusion = f32[8,256,128]{2,1,0:T(8,128)S(1)} fusion(f32[8,256,128]{2,1,0:T(8,128)} %solve.1, s32[256]{0:T(256)S(1)} %iota_add_fusion), kind=kOutput, calls=%fused_computation.1 | convolution fusion | flops 805961728 | bytes 2098176 | tf_op jit(solution)/shard_map/xkl,ky->xyl/dot_general | solution.py:535
  243.1 1.0 fusion.3
  244.1 0.9 collective-permute-done.26
  245.0 2.0 convolution_add_fusion.rec_ref
  247.0 16.8 %elements.1 = f32[32,6]{1,0:T(8,128)} custom-call(f32[4,256,256]{2,1,0:T(8,128)} %convolution_add_fusion.rec_ref, f32[4,256,256]{2,1,0:T(8,128)} %bitcast.64, f32[6,4,256,256]{3,2,1,0:T(8,128)} %get-tuple-element.46.b_ref, bf16[32,4,256,256]{3,2,1,0:T(8,128)(2,1)} %q_ref.1), custom_call_target="tpu_custom_call" | custom-call | tf_op jit(solution)/shard_map/elements/pallas_call | solution.py:408
  264.5 1.3 collective-permute-start.27
  265.8 2.3 collective-permute-done.27
  268.9 1.7 collective-permute-start.28
  270.6 1.9 collective-permute-done.28
  272.6 1.1 collective-permute-done.29
  (84 shorter events, 9.0 us)
Async XLA Ops:
  0.0 2.6 copy-start.1
  0.0 59.6 %collective-permute-start = (f32[6,4,256,256]{3,2,1,0:T(8,128)}, f32[6,4,256,256]{3,2,1,0:T(8,128)}, u32[]{:S(2)}, u32[]{:S(2)}) collective-permute-start(f32[6,4,256,256]{3,2,1,0:T(8,128)} %bitcast.46), channel_id=1, source_target_pairs={{0,1},{1,0},{2,3},{3,2},{4,5},{5,4},{6,7},{7,6},{8,9},{9,8},{10,11... | collective-permute-start | bytes 18874376 | tf_op jit(solution)/shard_map/ppermute | solution.py:608
  0.0 39.8 %collective-permute-start.2 = (f32[4,256,256]{2,1,0:T(8,128)}, f32[4,256,256]{2,1,0:T(8,128)}, u32[]{:S(2)}, u32[]{:S(2)}) collective-permute-start(f32[4,256,256]{2,1,0:T(8,128)} %bitcast.58), channel_id=1, source_target_pairs={{0,1},{1,0},{2,3},{3,2},{4,5},{5,4},{6,7},{7,6},{8,9},{9,8},{10,11... | collective-permute-start | bytes 3145736 | tf_op jit(solution)/shard_map/ppermute | solution.py:608
  2.6 6.6 %copy-start.6 = (f32[3,56,256]{2,1,0:T(8,128)}, f32[3,56,256]{2,1,0:T(8,128)S(1)}, u32[]{:S(2)}) copy-start(f32[3,56,256]{2,1,0:T(8,128)S(1)} %slice_select_fusion.5) | copy-start | bytes 516100
  2.7 6.5 %copy-start.7 = (f32[3,56,256]{2,1,0:T(8,128)}, f32[3,56,256]{2,1,0:T(8,128)S(1)}, u32[]{:S(2)}) copy-start(f32[3,56,256]{2,1,0:T(8,128)S(1)} %slice_select_fusion.6) | copy-start | bytes 516100
  3.7 19.0 %collective-permute-start.4 = (f32[14,56,256]{2,1,0:T(8,128)}, f32[14,56,256]{2,1,0:T(8,128)}, u32[]{:S(2)}, u32[]{:S(2)}) collective-permute-start(f32[14,56,256]{2,1,0:T(8,128)} %pad_maximum_fusion.2), channel_id=1, source_target_pairs={{3,7},{4,0},{11,15},{12,8},{19,23},{20,16},{27,31},{28,24}} | collective-permute-start | bytes 2408456 | tf_op jit(solution)/shard_map/ppermute | solution.py:598
  9.2 3.9 %copy-start = (f32[1,4,256,256]{3,2,1,0:T(8,128)S(1)}, f32[1,4,256,256]{3,2,1,0:T(8,128)}, u32[]{:S(2)}) copy-start(f32[1,4,256,256]{3,2,1,0:T(8,128)} %param.6) | copy-start | bytes 3145732
  9.2 23.4 %collective-permute-start.3 = (f32[16,56,256]{2,1,0:T(8,128)}, f32[16,56,256]{2,1,0:T(8,128)}, u32[]{:S(2)}, u32[]{:S(2)}) collective-permute-start(f32[16,56,256]{2,1,0:T(8,128)} %bitcast.11), channel_id=1, source_target_pairs={{1,2},{2,1},{3,4},{4,3},{5,6},{6,5},{9,10},{10,9},{11,12},{12,11},... | collective-permute-start | bytes 2752520 | tf_op jit(solution)/shard_map/ppermute | solution.py:595
  13.1 1.7 copy-start.3
  13.2 1.6 copy-start.5
  16.1 27.4 %collective-permute-start.7 = (f32[14,88,256]{2,1,0:T(8,128)}, f32[14,88,256]{2,1,0:T(8,128)}, u32[]{:S(2)}, u32[]{:S(2)}) collective-permute-start(f32[14,88,256]{2,1,0:T(8,128)} %pad_maximum_fusion), channel_id=1, source_target_pairs={{3,7},{4,0},{11,15},{12,8},{19,23},{20,16},{27,31},{28,24}} | collective-permute-start | bytes 3784712 | tf_op jit(solution)/shard_map/ppermute | solution.py:598
  22.8 27.9 %collective-permute-start.1 = (f32[4,256,256]{2,1,0:T(8,128)S(1)}, f32[4,256,256]{2,1,0:T(8,128)}, u32[]{:S(2)}, u32[]{:S(2)}) collective-permute-start(f32[4,256,256]{2,1,0:T(8,128)S(1)} %copy-done.1), channel_id=1, source_target_pairs={{0,1},{1,0},{2,3},{3,2},{4,5},{5,4},{6,7},{7,6},{8,9},{9,8},{10,11... | collective-permute-start | bytes 3145736 | tf_op jit(solution)/shard_map/ppermute | solution.py:608
  32.6 22.4 %collective-permute-start.5 = (f32[14,56,256]{2,1,0:T(8,128)}, f32[14,56,256]{2,1,0:T(8,128)}, u32[]{:S(2)}, u32[]{:S(2)}) collective-permute-start(f32[14,56,256]{2,1,0:T(8,128)} %broadcast_select_fusion.2), channel_id=1, source_target_pairs={{1,2},{2,1},{5,6},{6,5},{7,4},{0,3},{9,10},{10,9},{13,14},{14,13},... | collective-permute-start | bytes 2408456 | tf_op jit(solution)/shard_map/ppermute | solution.py:605
  37.2 11.3 %copy-start.4 = (f32[3,88,256]{2,1,0:T(8,128)S(1)}, f32[3,88,256]{2,1,0:T(8,128)}, u32[]{:S(2)}) copy-start(f32[3,88,256]{2,1,0:T(8,128)} %copy-done.3) | copy-start | bytes 811012
  39.9 12.8 %copy-start.11 = (f32[256,128]{1,0:T(8,128)S(1)}, f32[256,128]{1,0:T(8,128)}, u32[]{:S(2)}) copy-start(f32[256,128]{1,0:T(8,128)} %get-tuple-element.68) | copy-start | bytes 393220
  39.9 48.7 %collective-permute-start.6 = (f32[16,88,256]{2,1,0:T(8,128)}, f32[16,88,256]{2,1,0:T(8,128)}, u32[]{:S(2)}, u32[]{:S(2)}) collective-permute-start(f32[16,88,256]{2,1,0:T(8,128)} %bitcast.75), channel_id=1, source_target_pairs={{1,2},{2,1},{3,4},{4,3},{5,6},{6,5},{9,10},{10,9},{11,12},{12,11},... | collective-permute-start | bytes 4325384 | tf_op jit(solution)/shard_map/ppermute | solution.py:595
  43.5 37.6 %collective-permute-start.12 = (f32[14,88,256]{2,1,0:T(8,128)}, f32[14,88,256]{2,1,0:T(8,128)}, u32[]{:S(2)}, u32[]{:S(2)}) collective-permute-start(f32[14,88,256]{2,1,0:T(8,128)} %pad_maximum_fusion.1), channel_id=1, source_target_pairs={{3,7},{4,0},{11,15},{12,8},{19,23},{20,16},{27,31},{28,24}} | collective-permute-start | bytes 3784712 | tf_op jit(solution)/shard_map/ppermute | solution.py:598
  50.7 39.2 %collective-permute-start.8 = (f32[14,88,256]{2,1,0:T(8,128)}, f32[14,88,256]{2,1,0:T(8,128)}, u32[]{:S(2)}, u32[]{:S(2)}) collective-permute-start(f32[14,88,256]{2,1,0:T(8,128)} %broadcast_select_fusion.1), channel_id=1, source_target_pairs={{1,2},{2,1},{5,6},{6,5},{7,4},{0,3},{9,10},{10,9},{13,14},{14,13},... | collective-permute-start | bytes 3784712 | tf_op jit(solution)/shard_map/ppermute | solution.py:605
  55.0 65.4 %collective-permute-start.19 = (f32[14,24,256]{2,1,0:T(8,128)}, f32[14,24,256]{2,1,0:T(8,128)S(1)}, u32[]{:S(2)}, u32[]{:S(2)}) collective-permute-start(f32[14,24,256]{2,1,0:T(8,128)} %pad_maximum_fusion.3), channel_id=1, source_target_pairs={{3,7},{4,0},{11,15},{12,8},{19,23},{20,16},{27,31},{28,24}} | collective-permute-start | bytes 1032200 | tf_op jit(solution)/shard_map/ppermute | solution.py:598
  79.8 43.7 %collective-permute-start.9 = (f32[4,48,256]{2,1,0:T(8,128)}, f32[4,48,256]{2,1,0:T(8,128)S(1)}, u32[]{:S(2)}, u32[]{:S(2)}) collective-permute-start(f32[4,48,256]{2,1,0:T(8,128)} %get-tuple-element.28), channel_id=1, source_target_pairs={{0,16},{8,24},{1,17},{9,25},{2,18},{10,26},{3,19},{11,27},{4,20},{... | collective-permute-start | bytes 589832 | tf_op jit(solution)/shard_map/ppermute | solution.py:626
  83.8 42.9 %collective-permute-start.11 = (f32[16,88,256]{2,1,0:T(8,128)}, f32[16,88,256]{2,1,0:T(8,128)}, u32[]{:S(2)}, u32[]{:S(2)}) collective-permute-start(f32[16,88,256]{2,1,0:T(8,128)} %bitcast.16), channel_id=1, source_target_pairs={{1,2},{2,1},{3,4},{4,3},{5,6},{6,5},{9,10},{10,9},{11,12},{12,11},... | collective-permute-start | bytes 4325384 | tf_op jit(solution)/shard_map/ppermute | solution.py:595
  88.6 38.1 %collective-permute-start.13 = (f32[14,88,256]{2,1,0:T(8,128)}, f32[14,88,256]{2,1,0:T(8,128)S(1)}, u32[]{:S(2)}, u32[]{:S(2)}) collective-permute-start(f32[14,88,256]{2,1,0:T(8,128)} %broadcast_select_fusion), channel_id=1, source_target_pairs={{1,2},{2,1},{5,6},{6,5},{7,4},{0,3},{9,10},{10,9},{13,14},{14,13},... | collective-permute-start | bytes 3784712 | tf_op jit(solution)/shard_map/ppermute | solution.py:605
  89.9 30.5 %copy-start.9 = (f32[3,24,256]{2,1,0:T(8,128)S(1)}, f32[3,24,256]{2,1,0:T(8,128)}, u32[]{:S(2)}) copy-start(f32[3,24,256]{2,1,0:T(8,128)} %slice_select_fusion.13) | copy-start | bytes 221188
  89.9 30.5 %copy-start.10 = (f32[3,24,256]{2,1,0:T(8,128)S(1)}, f32[3,24,256]{2,1,0:T(8,128)}, u32[]{:S(2)}) copy-start(f32[3,24,256]{2,1,0:T(8,128)} %slice_select_fusion.14) | copy-start | bytes 221188
  119.1 37.8 %collective-permute-start.14 = (f32[4,88,256]{2,1,0:T(8,128)}, f32[4,88,256]{2,1,0:T(8,128)S(1)}, u32[]{:S(2)}, u32[]{:S(2)}) collective-permute-start(f32[4,88,256]{2,1,0:T(8,128)} %get-tuple-element.34), channel_id=1, source_target_pairs={{0,16},{8,24},{1,17},{9,25},{2,18},{10,26},{3,19},{11,27},{4,20},{... | collective-permute-start | bytes 1081352 | tf_op jit(solution)/shard_map/ppermute | solution.py:626
  121.2 70.6 %collective-permute-start.20 = (f32[14,24,256]{2,1,0:T(8,128)}, f32[14,24,256]{2,1,0:T(8,128)}, u32[]{:S(2)}, u32[]{:S(2)}) collective-permute-start(f32[14,24,256]{2,1,0:T(8,128)} %broadcast_select_fusion.3), channel_id=1, source_target_pairs={{1,2},{2,1},{5,6},{6,5},{7,4},{0,3},{9,10},{10,9},{13,14},{14,13},... | collective-permute-start | bytes 1032200 | tf_op jit(solution)/shard_map/ppermute | solution.py:605
  123.5 68.3 %collective-permute-start.18 = (f32[16,24,256]{2,1,0:T(8,128)S(1)}, f32[16,24,256]{2,1,0:T(8,128)S(1)}, u32[]{:S(2)}, u32[]{:S(2)}) collective-permute-start(f32[16,24,256]{2,1,0:T(8,128)S(1)} %bitcast.76), channel_id=1, source_target_pairs={{1,2},{2,1},{3,4},{4,3},{5,6},{6,5},{9,10},{10,9},{11,12},{12,11},... | collective-permute-start | bytes 1179656 | tf_op jit(solution)/shard_map/ppermute | solution.py:595
  126.6 1.1 copy-start.8
  156.9 15.4 %collective-permute-start.15 = (f32[4,88,128]{2,1,0:T(8,128)S(1)}, f32[4,88,128]{2,1,0:T(8,128)S(1)}, u32[]{:S(2)}, u32[]{:S(2)}) collective-permute-start(f32[4,88,128]{2,1,0:T(8,128)S(1)} %get-tuple-element.54), channel_id=1, source_target_pairs={{0,1},{1,0},{2,3},{3,2},{4,5},{5,4},{6,7},{7,6},{8,9},{9,8},{10,11... | collective-permute-start | bytes 540680 | tf_op jit(solution)/shard_map/ppermute | solution.py:503
  170.9 20.9 %collective-permute-start.16 = (f32[4,88,256]{2,1,0:T(8,128)}, f32[4,88,256]{2,1,0:T(8,128)S(1)}, u32[]{:S(2)}, u32[]{:S(2)}) collective-permute-start(f32[4,88,256]{2,1,0:T(8,128)} %get-tuple-element.37), channel_id=1, source_target_pairs={{0,16},{8,24},{1,17},{9,25},{2,18},{10,26},{3,19},{11,27},{4,20},{... | collective-permute-start | bytes 1081352 | tf_op jit(solution)/shard_map/ppermute | solution.py:626
  172.2 49.0 %collective-permute-start.10 = (f32[4,48,128]{2,1,0:T(8,128)S(1)}, f32[4,48,128]{2,1,0:T(8,128)S(1)}, u32[]{:S(2)}, u32[]{:S(2)}) collective-permute-start(f32[4,48,128]{2,1,0:T(8,128)S(1)} %get-tuple-element.58), channel_id=1, source_target_pairs={{0,1},{1,0},{2,3},{3,2},{4,5},{5,4},{6,7},{7,6},{8,9},{9,8},{10,11... | collective-permute-start | bytes 294920 | tf_op jit(solution)/shard_map/ppermute | solution.py:503
  174.2 44.7 %copy-start.2 = (f32[256,256]{1,0:T(8,128)S(1)}, f32[256,256]{1,0:T(8,128)}, u32[]{:S(2)}) copy-start(f32[256,256]{1,0:T(8,128)} %fusion.22.table_ref) | copy-start | bytes 786436
  191.8 0.8 copy-start.12
  210.4 8.4 %collective-permute-start.21 = (f32[4,32,256]{2,1,0:T(8,128)}, f32[4,32,256]{2,1,0:T(8,128)S(1)}, u32[]{:S(2)}, u32[]{:S(2)}) collective-permute-start(f32[4,32,256]{2,1,0:T(8,128)} %get-tuple-element.42), channel_id=1, source_target_pairs={{0,16},{8,24},{1,17},{9,25},{2,18},{10,26},{3,19},{11,27},{4,20},{... | collective-permute-start | bytes 393224 | tf_op jit(solution)/shard_map/ppermute | solution.py:626
  212.0 7.0 %collective-permute-start.17 = (f32[4,88,128]{2,1,0:T(8,128)S(1)}, f32[4,88,128]{2,1,0:T(8,128)S(1)}, u32[]{:S(2)}, u32[]{:S(2)}) collective-permute-start(f32[4,88,128]{2,1,0:T(8,128)S(1)} %get-tuple-element.56), channel_id=1, source_target_pairs={{0,1},{1,0},{2,3},{3,2},{4,5},{5,4},{6,7},{7,6},{8,9},{9,8},{10,11... | collective-permute-start | bytes 540680 | tf_op jit(solution)/shard_map/ppermute | solution.py:503
  218.9 1.3 collective-permute-start.22
  226.3 6.6 %collective-permute-start.23 = (f32[256,128]{1,0:T(8,128)}, f32[256,128]{1,0:T(8,128)S(1)}, u32[]{:S(2)}, u32[]{:S(2)}) collective-permute-start(f32[256,128]{1,0:T(8,128)} %get-tuple-element.43), channel_id=1, source_target_pairs={{0,2},{1,3},{2,0},{3,1},{4,6},{5,7},{6,4},{7,5},{8,10},{9,11},{10,... | collective-permute-start | bytes 393224 | tf_op jit(solution)/shard_map/ppermute | solution.py:525
  226.7 8.5 %collective-permute-start.24 = (f32[256,128]{1,0:T(8,128)}, f32[256,128]{1,0:T(8,128)S(1)}, u32[]{:S(2)}, u32[]{:S(2)}) collective-permute-start(f32[256,128]{1,0:T(8,128)} %get-tuple-element.44), channel_id=1, source_target_pairs={{0,4},{1,5},{2,6},{3,7},{4,0},{5,1},{6,2},{7,3},{8,12},{9,13},{10,... | collective-permute-start | bytes 393224 | tf_op jit(solution)/shard_map/ppermute | solution.py:525
  227.9 7.2 %collective-permute-start.25 = (f32[256,128]{1,0:T(8,128)}, f32[256,128]{1,0:T(8,128)S(1)}, u32[]{:S(2)}, u32[]{:S(2)}) collective-permute-start(f32[256,128]{1,0:T(8,128)} %get-tuple-element.45), channel_id=1, source_target_pairs={{0,6},{1,7},{2,4},{3,5},{4,2},{5,3},{6,0},{7,1},{8,14},{9,15},{10,... | collective-permute-start | bytes 393224 | tf_op jit(solution)/shard_map/ppermute | solution.py:525
  232.9 2.3 copy-start.13
  235.1 0.7 copy-start.14
  235.1 0.7 copy-start.15
  243.0 2.0 collective-permute-start.26
  264.5 3.7 %collective-permute-start.27 = (f32[16,6]{1,0:T(8,128)S(1)}, f32[16,6]{1,0:T(8,128)S(1)}, u32[]{:S(2)}, u32[]{:S(2)}) collective-permute-start(f32[16,6]{1,0:T(8,128)S(1)} %slice_select_fusion.17), channel_id=1, source_target_pairs={{0,4},{1,5},{2,6},{3,7},{4,0},{5,1},{6,2},{7,3},{8,12},{9,13},{10,... | collective-permute-start | bytes 1160 | tf_op jit(solution)/shard_map/ppermute | solution.py:553
  268.9 3.7 %collective-permute-start.28 = (f32[8,6]{1,0:T(8,128)S(1)}, f32[8,6]{1,0:T(8,128)S(1)}, u32[]{:S(2)}, u32[]{:S(2)}) collective-permute-start(f32[8,6]{1,0:T(8,128)S(1)} %slice_select_fusion.18), channel_id=1, source_target_pairs={{0,2},{1,3},{2,0},{3,1},{4,6},{5,7},{6,4},{7,5},{8,10},{9,11},{10,... | collective-permute-start | bytes 584 | tf_op jit(solution)/shard_map/ppermute | solution.py:553
  272.6 1.2 collective-permute-start.29

commit v3 on v2

--- a/solution.py
+++ b/solution.py
@@ -11,7 +11,7 @@
 ORDER = 4
 LANES = 128
 SUBS = 8
-SHARES = (6, 11, 11, 4)
+SHARES = (6, 10, 10, 6)
 AHEAD = 2
 
 time_step = 0.2
@@ -244,7 +244,7 @@
                 finish(u1, (chain, p))
             return carry
 
-        lax.fori_loop(0, reach[1], order_1, 0)
+        lax.fori_loop(0, reach[1], order_1, 0, unroll=2)
         for k, source, target in ((2, u1, u2), (3, u2, u3)):
 
             def order_k(p, carry, k=k, source=source, target=target):
@@ -258,7 +258,7 @@
                     finish(target, (chain, p))
                 return carry
 
-            lax.fori_loop(0, reach[k], order_k, 0)
+            lax.fori_loop(0, reach[k], order_k, 0, unroll=2)
 
         def last(p, carry):
             for r0, n in pieces(rows):
@@ -286,7 +286,7 @@
                     scatter(b_out, (2 * i + 1, p), r0 + j, imag[j])
             return carry
 
-        lax.fori_loop(0, planes, last, 0)
+        lax.fori_loop(0, planes, last, 0, unroll=2)
         for copy in b_copies(i):
             copy.start()
         return carry
@@ -302,7 +302,7 @@
             scatter(r_out, (p,), r, wave[r])
         return carry
 
-    lax.fori_loop(0, planes, spread, 0)
+    lax.fori_loop(0, planes, spread, 0, unroll=2)
     out = [
         pltpu.make_async_copy(
             r_out.at[m, :, inner], rho_out.at[:, :, lanes(m)], o_sems.at[n_vectors * tiles + m]
@@ -588,21 +588,15 @@
 
     def exchange(c, after):
         lo, hi = layout[c][1]
-        block = own
-        if after is not None:
-            block, _ = lax.optimization_barrier((own, after))
-        block = block[:split, :, lo:hi].reshape(-1, hi - lo, size_z)
-        direct = lax.ppermute(block, "grid", chip_pairs)
+        held = lambda a: a if after is None else lax.optimization_barrier((a, after))[0]
+        block = own[:split, :, lo:hi].reshape(-1, hi - lo, size_z)
         rest, pairs = message(lo, hi), chip_pairs
         if relayed:
             hop = lax.ppermute(rest, "grid", first_leg)
-            if after is not None:
-                hop, _ = lax.optimization_barrier((hop, after))
             rest = jnp.where(ends, hop, rest)
             pairs = [p for p in chip_pairs if set(p) != {left, right}] + second_leg
-        elif after is not None:
-            rest, _ = lax.optimization_barrier((rest, after))
-        return direct, lax.ppermute(rest, "grid", pairs)
+        direct = lax.ppermute(held(block), "grid", chip_pairs)
+        return direct, lax.ppermute(held(rest), "grid", pairs)
 
     messages = [exchange(c, None) for c in range(AHEAD)]
     mates = [lax.ppermute(f, "grid", mate_pairs) for f in (own, potential, added)]
@@ -622,7 +616,7 @@
             b, arrived[c - 1] = lax.optimization_barrier((b, arrived[c - 1]))
         b, rho = taylor(span, flags, mask, own, potential, added, mates, poisson.table_z, sources, b)
         if c + AHEAD < len(layout):
-            messages.append(exchange(c + AHEAD, rho))
+            messages.append(exchange(c + AHEAD, (messages[c + AHEAD - 1], rho)))
         arrived.append(lax.ppermute(rho, "grp", group_pairs))
     for c, ((o0, _), _, _) in enumerate(layout):
         poisson.add(arrived[c], o0)

time: 277 us -> 277 us (level)
  Pallas kernels: 120 us -> 106 us
  starting transfers between devices: 61.3 us -> 72.1 us
    pallas_call x4, Pallas kernels: 96.3 us -> 82.1 us  [taylor(): pl.pallas_call(functools.partial(taylor_kernel, span, shape, planes, b is...]
    ppermute x5, starting transfers between devices: 14.3 us -> 26.8 us  [swap(): return lax.ppermute(array, 'grid', [(i, i ^ 1) for i in range(self.count)])]
    unnamed x32 -> x58, local copies, waits for them, and re-layouts: 2.52 us -> 6.11 us
    select_n x4, other arithmetic: 6.22 us -> 2.66 us  [exchange(): rest = jnp.where(ends, hop, rest)]
    slice x4 -> x3, local copies, waits for them, and re-layouts: 8.48 us -> 7.72 us  [exchange(): block = own[:split, :, lo:hi].reshape(-1, hi - lo, size_z)]
  transfers between devices with their start and end apart: 30 -> 30, of which waited for: 11 -> 11; matrix products, arithmetic and copies ran while one was open for 14% -> 13% of each run, Pallas kernels for 35% -> 30%
where the time goes in v3:
time: 277 us; the launch traced here: 275 us
  Pallas kernels  106 us (38%)
  starting transfers between devices  72.1 us (26%)
  waiting for transfers between devices  44.6 us (16%)
  other arithmetic  20.8 us (8%)
  local copies, waits for them, and re-layouts  17.3 us (6%)
  matrix products  13.4 us (5%)
    pallas_call x4, Pallas kernels, taylor(): pl.pallas_call(functools.partial(taylor_kernel, span, shape, planes, b is...  82.1 us
    ppermute x5, starting transfers between devices, swap(): return lax.ppermute(array, 'grid', [(i, i ^ 1) for i in range(self.count)])  26.8 us
    ppermute x4, waiting for transfers between devices, on_device(): arrived.append(lax.ppermute(rho, 'grp', group_pairs))  23.5 us
    pallas_call x1, Pallas kernels, elements(): pl.pallas_call(functools.partial(elements_kernel, n_states, parts, planes...  16.8 us
    ppermute x4, starting transfers between devices, exchange(): hop = lax.ppermute(rest, 'grid', first_leg)  14.7 us
    ppermute x4, starting transfers between devices, exchange(): direct = lax.ppermute(held(block), 'grid', chip_pairs)  13.3 us
    slice x3, local copies, waits for them, and re-layouts, exchange(): block = own[:split, :, lo:hi].reshape(-1, hi - lo, size_z)  7.72 us
    dot_general x4, matrix products, add(): self.total += jnp.einsum('xyl,yk->xkl', both, rows, precision=highest)  7.08 us
  transfers between devices with their start and end apart: 30, of which 11 were waited for; matrix products, arithmetic and copies ran while one was open for 13% of the time, Pallas kernels for 30%

profile of v3, /device:TPU:28, one launch (start us, length us, event | category | flops | bytes accessed | tf_op | source)
XLA Modules:
  0.0 274.5 jit_solution(7540189008713941661)
XLA Ops:
  0.5 1.1 slice.208
  1.6 1.2 slice_select_fusion.5
  2.8 1.0 pad_maximum_fusion.2
  3.8 3.3 %collective-permute-start.4 = (f32[14,56,256]{2,1,0:T(8,128)}, f32[14,56,256]{2,1,0:T(8,128)}, u32[]{:S(2)}, u32[]{:S(2)}) collective-permute-start(f32[14,56,256]{2,1,0:T(8,128)} %pad_maximum_fusion.2), channel_id=1, source_target_pairs={{3,7},{4,0},{11,15},{12,8},{19,23},{20,16},{27,31},{28,24}} | collective-permute-start | bytes 2408456 | tf_op jit(solution)/shard_map/ppermute | solution.py:595
  7.1 2.2 slice.207
  9.3 3.9 %collective-permute-start.3 = (f32[16,56,256]{2,1,0:T(8,128)}, f32[16,56,256]{2,1,0:T(8,128)}, u32[]{:S(2)}, u32[]{:S(2)}) collective-permute-start(f32[16,56,256]{2,1,0:T(8,128)} %bitcast.11), channel_id=1, source_target_pairs={{1,2},{2,1},{3,4},{4,3},{5,6},{6,5},{9,10},{10,9},{11,12},{12,11},... | collective-permute-start | bytes 2752520 | tf_op jit(solution)/shard_map/ppermute | solution.py:598
  14.8 1.5 fusion.68
  16.2 1.1 pad_maximum_fusion
  17.4 2.4 collective-permute-start.7
  19.8 2.2 pad_maximum_fusion.1
  22.0 1.1 multiply_exponential_fusion
  23.1 2.1 exponential-minus-one_negate_fusion
  25.8 2.3 collective-permute-start.12
  28.8 1.0 slice.223
  29.9 3.5 %fusion.69 = (f32[4,4,80,256]{3,2,1,0:T(8,128)}, f32[4,4,80,256]{3,2,1,0:T(8,128)}) fusion(f32[6,4,256,256]{3,2,1,0:T(8,128)} %bitcast.51), kind=kLoop, calls=%fused_computation.132 | loop fusion | bytes 5242880 | tf_op jit(solution)/shard_map/slice | solution.py:592
  33.6 1.4 collective-permute-start.5
  35.7 2.0 slice.222
  37.7 3.0 %collective-permute-start.6 = (f32[16,80,256]{2,1,0:T(8,128)}, f32[16,80,256]{2,1,0:T(8,128)}, u32[]{:S(2)}, u32[]{:S(2)}) collective-permute-start(f32[16,80,256]{2,1,0:T(8,128)} %bitcast.13), channel_id=1, source_target_pairs={{1,2},{2,1},{3,4},{4,3},{5,6},{6,5},{9,10},{10,9},{11,12},{12,11},... | collective-permute-start | bytes 3932168 | tf_op jit(solution)/shard_map/ppermute | solution.py:598
  40.8 1.2 broadcast_select_fusion.1
  42.0 2.6 collective-permute-done.12
  44.6 1.3 collective-permute-start.8
  45.9 1.8 fusion.22.table_ref
  47.7 1.2 broadcast_select_fusion
  48.9 1.0 copy-done.16
  49.9 6.7 %collective-permute-start.19 = (f32[14,40,256]{2,1,0:T(8,128)S(1)}, f32[14,40,256]{2,1,0:T(8,128)S(1)}, u32[]{:S(2)}, u32[]{:S(2)}) collective-permute-start(f32[14,40,256]{2,1,0:T(8,128)S(1)} %pad_maximum_fusion.3), channel_id=1, source_target_pairs={{3,7},{4,0},{11,15},{12,8},{19,23},{20,16},{27,31},{28,24}} | collective-permute-start | bytes 1720328 | tf_op jit(solution)/shard_map/ppermute | solution.py:595
  56.7 0.9 copy-done.27
  57.5 16.7 %taylor.4 = (f32[6,4,256,256]{3,2,1,0:T(8,128)}, f32[4,48,256]{2,1,0:T(8,128)}) custom-call(s32[2]{0:T(128)} %add_convert_fusion.1.flag_ref, f32[2]{0:T(128)} %add_convert_fusion.2.mask_ref, f32[6,4,256,256]{3,2,1,0:T(8,128)} %bitcast.53, f32[4,256,256]{2,1,0:T(8,128)} %pot_ref.7, f32[4,256,256]{2,1,0:T(8,128)} %bitcast.59, ...), custom_call_target="tpu_custom_call" | custom-call | flops 6881280000 | bytes 20971520 | tf_op jit(solution)/shard_map/taylor/pallas_call | solution.py:338
  74.3 5.5 %collective-permute-done.8.refs_3_.refs_1_ = f32[14,80,256]{2,1,0:T(8,128)} collective-permute-done((f32[14,80,256]{2,1,0:T(8,128)}, f32[14,80,256]{2,1,0:T(8,128)}, u32[]{:S(2)}, u32[]{:S(2)}) %collective-permute-start.8) | collective-permute-done | bytes 1146912 | tf_op jit(solution)/shard_map/ppermute | solution.py:599
  79.9 1.3 collective-permute-start.13
  81.1 3.9 %collective-permute-start.11 = (f32[16,80,256]{2,1,0:T(8,128)}, f32[16,80,256]{2,1,0:T(8,128)S(1)}, u32[]{:S(2)}, u32[]{:S(2)}) collective-permute-start(f32[16,80,256]{2,1,0:T(8,128)} %bitcast.74), channel_id=1, source_target_pairs={{1,2},{2,1},{3,4},{4,3},{5,6},{6,5},{9,10},{10,9},{11,12},{12,11},... | collective-permute-start | bytes 3932168 | tf_op jit(solution)/shard_map/ppermute | solution.py:598
  85.1 1.3 collective-permute-start.9
  86.4 24.1 %taylor.5 = (f32[6,4,256,256]{3,2,1,0:T(8,128)}, f32[4,80,256]{2,1,0:T(8,128)}) custom-call(s32[2]{0:T(128)} %add_convert_fusion.1.flag_ref, f32[2]{0:T(128)} %add_convert_fusion.2.mask_ref, f32[6,4,256,256]{3,2,1,0:T(8,128)} %bitcast.54, f32[4,256,256]{2,1,0:T(8,128)} %pot_ref.7, f32[4,256,256]{2,1,0:T(8,128)} %bitcast.60, ...), custom_call_target="tpu_custom_call", output_to_operand_aliasing={{0}: (13, {})} | custom-call | flops 11796480000 | bytes 20971520 | tf_op jit(solution)/shard_map/taylor/pallas_call | solution.py:338
  110.5 1.5 collective-permute-start.14
  112.0 1.1 copy-done.15
  113.1 24.1 %taylor.6 = (f32[6,4,256,256]{3,2,1,0:T(8,128)}, f32[4,80,256]{2,1,0:T(8,128)}) custom-call(s32[2]{0:T(128)} %add_convert_fusion.1.flag_ref, f32[2]{0:T(128)} %add_convert_fusion.2.mask_ref, f32[6,4,256,256]{3,2,1,0:T(8,128)} %bitcast.55, f32[4,256,256]{2,1,0:T(8,128)} %pot_ref.7, f32[4,256,256]{2,1,0:T(8,128)} %bitcast.61, ...), custom_call_target="tpu_custom_call", output_to_operand_aliasing={{0}: (13, {})} | custom-call | flops 11796480000 | bytes 20971520 | tf_op jit(solution)/shard_map/taylor/pallas_call | solution.py:338
  137.2 1.3 collective-permute-start.20
  138.5 2.6 collective-permute-start.18
  141.1 1.0 slice_select_fusion.10
  142.1 26.5 %collective-permute-start.15 = (f32[4,80,128]{2,1,0:T(8,128)S(1)}, f32[4,80,128]{2,1,0:T(8,128)S(1)}, u32[]{:S(2)}, u32[]{:S(2)}) collective-permute-start(f32[4,80,128]{2,1,0:T(8,128)S(1)} %get-tuple-element.56), channel_id=1, source_target_pairs={{0,1},{1,0},{2,3},{3,2},{4,5},{5,4},{6,7},{7,6},{8,9},{9,8},{10,11... | collective-permute-start | bytes 491528 | tf_op jit(solution)/shard_map/ppermute | solution.py:503
  168.6 1.3 collective-permute-start.16
  169.9 1.0 slice_select_fusion.16
  171.0 1.9 fusion.7
  172.9 15.3 %collective-permute-done.16 = f32[4,80,256]{2,1,0:T(8,128)S(1)} collective-permute-done((f32[4,80,256]{2,1,0:T(8,128)}, f32[4,80,256]{2,1,0:T(8,128)S(1)}, u32[]{:S(2)}, u32[]{:S(2)}) %collective-permute-start.16) | collective-permute-done | bytes 327712 | tf_op jit(solution)/shard_map/ppermute | solution.py:620
  189.7 0.9 copy-done.17
  190.6 17.2 %taylor.7 = (f32[6,4,256,256]{3,2,1,0:T(8,128)}, f32[4,48,256]{2,1,0:T(8,128)}) custom-call(s32[2]{0:T(128)} %add_convert_fusion.1.flag_ref, f32[2]{0:T(128)} %add_convert_fusion.2.mask_ref, f32[6,4,256,256]{3,2,1,0:T(8,128)} %bitcast.56, f32[4,256,256]{2,1,0:T(8,128)} %pot_ref.7, f32[4,256,256]{2,1,0:T(8,128)} %bitcast.62, ...), custom_call_target="tpu_custom_call", output_to_operand_aliasing={{0}: (13, {})} | custom-call | flops 6881280000 | bytes 20971520 | tf_op jit(solution)/shard_map/taylor/pallas_call | solution.py:338
  207.8 1.5 collective-permute-start.21
  209.5 8.2 %collective-permute-done.21 = f32[4,48,256]{2,1,0:T(8,128)S(1)} collective-permute-done((f32[4,48,256]{2,1,0:T(8,128)}, f32[4,48,256]{2,1,0:T(8,128)S(1)}, u32[]{:S(2)}, u32[]{:S(2)}) %collective-permute-start.21) | collective-permute-done | bytes 196640 | tf_op jit(solution)/shard_map/ppermute | solution.py:620
  217.8 1.0 fusion.13
  219.0 1.0 fusion.33
  220.1 3.1 %fusion.2.f_ref = f32[8,256,128]{2,1,0:T(8,128)} fusion(f32[256,8,128]{2,0,1:T(8,128)S(1)} %fusion.33, f32[256,8,128]{2,0,1:T(8,128)S(1)} %fusion.13, f32[256,8,128]{2,0,1:T(8,128)S(1)} %fusion.7, f32[4,48,128]{2,1,0:T(8,128)} %collective-permute-done.10, f32[4,48,128]{2,1,0:T(8,128)S(1)} %get-tuple-element.59, pred[]{:T(512)} %eq.31, ...), kind=kOutput, calls=%fused_computation.5 | convolution fusion | flops 151928832 | bytes 4440065 | tf_op jit(solution)/shard_map/xyl,yk->xkl/dot_general | solution.py:511
  223.2 2.9 %moments.1 = (f32[256,128]{1,0:T(8,128)}, f32[256,128]{1,0:T(8,128)}, f32[256,128]{1,0:T(8,128)}) custom-call(f32[3]{0:T(128)} %add_convert_fusion.side_ref, f32[8,256,128]{2,1,0:T(8,128)} %fusion.2.f_ref, f32[8,256,128]{2,1,0:T(8,128)} %get-tuple-element.64.low_ref, f32[8,256,128]{2,1,0:T(8,128)} %get-tuple-element.63.high_ref, ...), custom_call_target="tpu_custom_call" | custom-call | tf_op jit(solution)/shard_map/moments/pallas_call | solution.py:517
  227.6 2.0 collective-permute-start.25
  229.6 3.1 %collective-permute-done.23.refs_0_ = f32[256,128]{1,0:T(8,128)S(1)} collective-permute-done((f32[256,128]{1,0:T(8,128)}, f32[256,128]{1,0:T(8,128)S(1)}, u32[]{:S(2)}, u32[]{:S(2)}) %collective-permute-start.23) | collective-permute-done | bytes 131104 | tf_op jit(solution)/shard_map/ppermute | solution.py:525
  232.7 2.6 collective-permute-done.24.refs_1_
  236.0 3.7 %solve.1 = f32[8,256,128]{2,1,0:T(8,128)} custom-call(f32[3]{0:T(128)} %add_convert_fusion.side_ref, f32[8,256,128]{2,1,0:T(8,128)} %fusion.2.f_ref, f32[8,256,128]{2,1,0:T(8,128)} %get-tuple-element.64.low_ref, f32[8,256,128]{2,1,0:T(8,128)} %get-tuple-element.63.high_ref, f32[256,128]{1,0:T(8,128)} %get-tuple-element.66.r_ref, ...), custom_call_target="tpu_custom_call" | custom-call | tf_op jit(solution)/shard_map/solve/pallas_call | solution.py:528
  239.7 3.3 %convolution_bitcast_fusion = f32[8,256,128]{2,1,0:T(8,128)S(1)} fusion(f32[8,256,128]{2,1,0:T(8,128)} %solve.1, s32[256]{0:T(256)S(1)} %iota_add_fusion), kind=kOutput, calls=%fused_computation.1 | convolution fusion | flops 805961728 | bytes 2098176 | tf_op jit(solution)/shard_map/xkl,ky->xyl/dot_general | solution.py:535
  243.3 1.0 fusion.3
  245.1 2.0 convolution_add_fusion.rec_ref
  247.1 16.8 %elements.1 = f32[32,6]{1,0:T(8,128)} custom-call(f32[4,256,256]{2,1,0:T(8,128)} %convolution_add_fusion.rec_ref, f32[4,256,256]{2,1,0:T(8,128)} %bitcast.63, f32[6,4,256,256]{3,2,1,0:T(8,128)} %get-tuple-element.46.b_ref, bf16[32,4,256,256]{3,2,1,0:T(8,128)(2,1)} %q_ref.1), custom_call_target="tpu_custom_call" | custom-call | tf_op jit(solution)/shard_map/elements/pallas_call | solution.py:408
  264.7 0.9 collective-permute-start.27
  265.6 2.7 collective-permute-done.27
  269.1 1.3 collective-permute-start.28
  270.4 2.3 collective-permute-done.28
  272.8 1.1 collective-permute-done.29
  (109 shorter events, 11.7 us)
Async XLA Ops:
  0.0 2.8 %copy-start.1 = (f32[4,256,256]{2,1,0:T(8,128)S(1)}, f32[4,256,256]{2,1,0:T(8,128)}, u32[]{:S(2)}) copy-start(f32[4,256,256]{2,1,0:T(8,128)} %pot_ref.7) | copy-start | bytes 3145732
  0.0 57.5 %collective-permute-start = (f32[6,4,256,256]{3,2,1,0:T(8,128)}, f32[6,4,256,256]{3,2,1,0:T(8,128)}, u32[]{:S(2)}, u32[]{:S(2)}) collective-permute-start(f32[6,4,256,256]{3,2,1,0:T(8,128)} %bitcast.46), channel_id=1, source_target_pairs={{0,1},{1,0},{2,3},{3,2},{4,5},{5,4},{6,7},{7,6},{8,9},{9,8},{10,11... | collective-permute-start | bytes 18874376 | tf_op jit(solution)/shard_map/ppermute | solution.py:602
  0.0 33.6 %collective-permute-start.2 = (f32[4,256,256]{2,1,0:T(8,128)}, f32[4,256,256]{2,1,0:T(8,128)}, u32[]{:S(2)}, u32[]{:S(2)}) collective-permute-start(f32[4,256,256]{2,1,0:T(8,128)} %bitcast.57), channel_id=1, source_target_pairs={{0,1},{1,0},{2,3},{3,2},{4,5},{5,4},{6,7},{7,6},{8,9},{9,8},{10,11... | collective-permute-start | bytes 3145736 | tf_op jit(solution)/shard_map/ppermute | solution.py:602
  1.6 2.2 copy-start.3
  2.8 6.6 %copy-start.11 = (f32[3,56,256]{2,1,0:T(8,128)}, f32[3,56,256]{2,1,0:T(8,128)S(1)}, u32[]{:S(2)}) copy-start(f32[3,56,256]{2,1,0:T(8,128)S(1)} %slice_select_fusion.5) | copy-start | bytes 516100
  2.8 6.5 %copy-start.13 = (f32[3,56,256]{2,1,0:T(8,128)}, f32[3,56,256]{2,1,0:T(8,128)S(1)}, u32[]{:S(2)}) copy-start(f32[3,56,256]{2,1,0:T(8,128)S(1)} %slice_select_fusion.6) | copy-start | bytes 516100
  3.8 22.0 %collective-permute-start.4 = (f32[14,56,256]{2,1,0:T(8,128)}, f32[14,56,256]{2,1,0:T(8,128)}, u32[]{:S(2)}, u32[]{:S(2)}) collective-permute-start(f32[14,56,256]{2,1,0:T(8,128)} %pad_maximum_fusion.2), channel_id=1, source_target_pairs={{3,7},{4,0},{11,15},{12,8},{19,23},{20,16},{27,31},{28,24}} | collective-permute-start | bytes 2408456 | tf_op jit(solution)/shard_map/ppermute | solution.py:595
  9.3 4.6 %copy-start = (f32[1,4,256,256]{3,2,1,0:T(8,128)S(1)}, f32[1,4,256,256]{3,2,1,0:T(8,128)}, u32[]{:S(2)}) copy-start(f32[1,4,256,256]{3,2,1,0:T(8,128)} %param.6) | copy-start | bytes 3145732
  9.3 24.1 %collective-permute-start.3 = (f32[16,56,256]{2,1,0:T(8,128)}, f32[16,56,256]{2,1,0:T(8,128)}, u32[]{:S(2)}, u32[]{:S(2)}) collective-permute-start(f32[16,56,256]{2,1,0:T(8,128)} %bitcast.11), channel_id=1, source_target_pairs={{1,2},{2,1},{3,4},{4,3},{5,6},{6,5},{9,10},{10,9},{11,12},{12,11},... | collective-permute-start | bytes 2752520 | tf_op jit(solution)/shard_map/ppermute | solution.py:598
  14.0 2.3 copy-start.7
  14.7 1.5 copy-start.9
  17.4 20.3 %collective-permute-start.7 = (f32[14,80,256]{2,1,0:T(8,128)}, f32[14,80,256]{2,1,0:T(8,128)}, u32[]{:S(2)}, u32[]{:S(2)}) collective-permute-start(f32[14,80,256]{2,1,0:T(8,128)} %pad_maximum_fusion), channel_id=1, source_target_pairs={{3,7},{4,0},{11,15},{12,8},{19,23},{20,16},{27,31},{28,24}} | collective-permute-start | bytes 3440648 | tf_op jit(solution)/shard_map/ppermute | solution.py:595
  25.8 18.8 %collective-permute-start.12 = (f32[14,80,256]{2,1,0:T(8,128)}, f32[14,80,256]{2,1,0:T(8,128)}, u32[]{:S(2)}, u32[]{:S(2)}) collective-permute-start(f32[14,80,256]{2,1,0:T(8,128)} %pad_maximum_fusion.1), channel_id=1, source_target_pairs={{3,7},{4,0},{11,15},{12,8},{19,23},{20,16},{27,31},{28,24}} | collective-permute-start | bytes 3440648 | tf_op jit(solution)/shard_map/ppermute | solution.py:595
  29.9 3.5 %copy-start.4 = (f32[2,4,56,256]{3,2,1,0:T(8,128)S(1)}, f32[2,4,56,256]{3,2,1,0:T(8,128)}, u32[]{:S(2)}) copy-start(f32[2,4,56,256]{3,2,1,0:T(8,128)} %copy-done.3) | copy-start | bytes 1376260
  29.9 3.5 %copy-start.12 = (f32[3,56,256]{2,1,0:T(8,128)S(1)}, f32[3,56,256]{2,1,0:T(8,128)}, u32[]{:S(2)}) copy-start(f32[3,56,256]{2,1,0:T(8,128)} %copy-done.11) | copy-start | bytes 516100
  29.9 3.5 %copy-start.14 = (f32[3,56,256]{2,1,0:T(8,128)S(1)}, f32[3,56,256]{2,1,0:T(8,128)}, u32[]{:S(2)}) copy-start(f32[3,56,256]{2,1,0:T(8,128)} %copy-done.13) | copy-start | bytes 516100
  33.4 15.5 %collective-permute-start.1 = (f32[4,256,256]{2,1,0:T(8,128)S(1)}, f32[4,256,256]{2,1,0:T(8,128)S(1)}, u32[]{:S(2)}, u32[]{:S(2)}) collective-permute-start(f32[4,256,256]{2,1,0:T(8,128)S(1)} %copy-done.1), channel_id=1, source_target_pairs={{0,1},{1,0},{2,3},{3,2},{4,5},{5,4},{6,7},{7,6},{8,9},{9,8},{10,11... | collective-permute-start | bytes 3145736 | tf_op jit(solution)/shard_map/ppermute | solution.py:602
  33.6 7.1 %copy-start.8 = (f32[3,80,256]{2,1,0:T(8,128)S(1)}, f32[3,80,256]{2,1,0:T(8,128)}, u32[]{:S(2)}) copy-start(f32[3,80,256]{2,1,0:T(8,128)} %copy-done.7) | copy-start | bytes 737284
  33.6 7.1 %copy-start.10 = (f32[3,80,256]{2,1,0:T(8,128)S(1)}, f32[3,80,256]{2,1,0:T(8,128)}, u32[]{:S(2)}) copy-start(f32[3,80,256]{2,1,0:T(8,128)} %copy-done.9) | copy-start | bytes 737284
  33.6 23.0 %collective-permute-start.5 = (f32[14,56,256]{2,1,0:T(8,128)S(1)}, f32[14,56,256]{2,1,0:T(8,128)S(1)}, u32[]{:S(2)}, u32[]{:S(2)}) collective-permute-start(f32[14,56,256]{2,1,0:T(8,128)S(1)} %broadcast_select_fusion.2), channel_id=1, source_target_pairs={{1,2},{2,1},{5,6},{6,5},{7,4},{0,3},{9,10},{10,9},{13,14},{14,13},... | collective-permute-start | bytes 2408456 | tf_op jit(solution)/shard_map/ppermute | solution.py:599
  37.7 10.0 %copy-start.5 = (f32[3,80,256]{2,1,0:T(8,128)S(1)}, f32[3,80,256]{2,1,0:T(8,128)}, u32[]{:S(2)}) copy-start(f32[3,80,256]{2,1,0:T(8,128)} %get-tuple-element.51) | copy-start | bytes 737284
  37.7 10.0 %copy-start.6 = (f32[3,80,256]{2,1,0:T(8,128)S(1)}, f32[3,80,256]{2,1,0:T(8,128)}, u32[]{:S(2)}) copy-start(f32[3,80,256]{2,1,0:T(8,128)} %get-tuple-element.53) | copy-start | bytes 737284
  37.7 36.6 %collective-permute-start.6 = (f32[16,80,256]{2,1,0:T(8,128)}, f32[16,80,256]{2,1,0:T(8,128)}, u32[]{:S(2)}, u32[]{:S(2)}) collective-permute-start(f32[16,80,256]{2,1,0:T(8,128)} %bitcast.13), channel_id=1, source_target_pairs={{1,2},{2,1},{3,4},{4,3},{5,6},{6,5},{9,10},{10,9},{11,12},{12,11},... | collective-permute-start | bytes 3932168 | tf_op jit(solution)/shard_map/ppermute | solution.py:598
  44.6 35.2 %collective-permute-start.8 = (f32[14,80,256]{2,1,0:T(8,128)}, f32[14,80,256]{2,1,0:T(8,128)}, u32[]{:S(2)}, u32[]{:S(2)}) collective-permute-start(f32[14,80,256]{2,1,0:T(8,128)} %broadcast_select_fusion.1), channel_id=1, source_target_pairs={{1,2},{2,1},{5,6},{6,5},{7,4},{0,3},{9,10},{10,9},{13,14},{14,13},... | collective-permute-start | bytes 3440648 | tf_op jit(solution)/shard_map/ppermute | solution.py:599
  48.9 1.0 copy-start.16
  49.9 35.1 %collective-permute-start.19 = (f32[14,40,256]{2,1,0:T(8,128)S(1)}, f32[14,40,256]{2,1,0:T(8,128)S(1)}, u32[]{:S(2)}, u32[]{:S(2)}) collective-permute-start(f32[14,40,256]{2,1,0:T(8,128)S(1)} %pad_maximum_fusion.3), channel_id=1, source_target_pairs={{3,7},{4,0},{11,15},{12,8},{19,23},{20,16},{27,31},{28,24}} | collective-permute-start | bytes 1720328 | tf_op jit(solution)/shard_map/ppermute | solution.py:595
  56.7 0.9 copy-start.27
  74.3 10.8 %copy-start.28 = (f32[4,48,256]{2,1,0:T(8,128)S(1)}, f32[4,48,256]{2,1,0:T(8,128)}, u32[]{:S(2)}) copy-start(f32[4,48,256]{2,1,0:T(8,128)} %get-tuple-element.28) | copy-start | bytes 589828
  79.9 32.1 %collective-permute-start.13 = (f32[14,80,256]{2,1,0:T(8,128)}, f32[14,80,256]{2,1,0:T(8,128)}, u32[]{:S(2)}, u32[]{:S(2)}) collective-permute-start(f32[14,80,256]{2,1,0:T(8,128)} %broadcast_select_fusion), channel_id=1, source_target_pairs={{1,2},{2,1},{5,6},{6,5},{7,4},{0,3},{9,10},{10,9},{13,14},{14,13},... | collective-permute-start | bytes 3440648 | tf_op jit(solution)/shard_map/ppermute | solution.py:599
  81.1 30.9 %collective-permute-start.11 = (f32[16,80,256]{2,1,0:T(8,128)}, f32[16,80,256]{2,1,0:T(8,128)S(1)}, u32[]{:S(2)}, u32[]{:S(2)}) collective-permute-start(f32[16,80,256]{2,1,0:T(8,128)} %bitcast.74), channel_id=1, source_target_pairs={{1,2},{2,1},{3,4},{4,3},{5,6},{6,5},{9,10},{10,9},{11,12},{12,11},... | collective-permute-start | bytes 3932168 | tf_op jit(solution)/shard_map/ppermute | solution.py:598
  85.1 26.9 %collective-permute-start.9 = (f32[4,48,256]{2,1,0:T(8,128)S(1)}, f32[4,48,256]{2,1,0:T(8,128)S(1)}, u32[]{:S(2)}, u32[]{:S(2)}) collective-permute-start(f32[4,48,256]{2,1,0:T(8,128)S(1)} %copy-done.28), channel_id=1, source_target_pairs={{0,16},{8,24},{1,17},{9,25},{2,18},{10,26},{3,19},{11,27},{4,20},{... | collective-permute-start | bytes 589832 | tf_op jit(solution)/shard_map/ppermute | solution.py:620
  110.5 26.7 %collective-permute-start.14 = (f32[4,80,256]{2,1,0:T(8,128)}, f32[4,80,256]{2,1,0:T(8,128)S(1)}, u32[]{:S(2)}, u32[]{:S(2)}) collective-permute-start(f32[4,80,256]{2,1,0:T(8,128)} %get-tuple-element.34), channel_id=1, source_target_pairs={{0,16},{8,24},{1,17},{9,25},{2,18},{10,26},{3,19},{11,27},{4,20},{... | collective-permute-start | bytes 983048 | tf_op jit(solution)/shard_map/ppermute | solution.py:620
  112.0 25.2 %copy-start.23 = (f32[4,48,256]{2,1,0:T(8,128)}, f32[4,48,256]{2,1,0:T(8,128)S(1)}, u32[]{:S(2)}) copy-start(f32[4,48,256]{2,1,0:T(8,128)S(1)} %collective-permute-done.9) | copy-start | bytes 589828
  112.0 26.5 %copy-start.18 = (f32[4,4,40,256]{3,2,1,0:T(8,128)S(1)}, f32[4,4,40,256]{3,2,1,0:T(8,128)}, u32[]{:S(2)}) copy-start(f32[4,4,40,256]{3,2,1,0:T(8,128)} %slice.222) | copy-start | bytes 1966084
  112.0 1.1 copy-start.15
  137.2 1.3 copy-start.22
  137.2 51.0 %collective-permute-start.20 = (f32[14,40,256]{2,1,0:T(8,128)S(1)}, f32[14,40,256]{2,1,0:T(8,128)S(1)}, u32[]{:S(2)}, u32[]{:S(2)}) collective-permute-start(f32[14,40,256]{2,1,0:T(8,128)S(1)} %broadcast_select_fusion.3), channel_id=1, source_target_pairs={{1,2},{2,1},{5,6},{6,5},{7,4},{0,3},{9,10},{10,9},{13,14},{14,13},... | collective-permute-start | bytes 1720328 | tf_op jit(solution)/shard_map/ppermute | solution.py:599
  138.5 51.2 %collective-permute-start.18 = (f32[16,40,256]{2,1,0:T(8,128)S(1)}, f32[16,40,256]{2,1,0:T(8,128)S(1)}, u32[]{:S(2)}, u32[]{:S(2)}) collective-permute-start(f32[16,40,256]{2,1,0:T(8,128)S(1)} %bitcast.75), channel_id=1, source_target_pairs={{1,2},{2,1},{3,4},{4,3},{5,6},{6,5},{9,10},{10,9},{11,12},{12,11},... | collective-permute-start | bytes 1966088 | tf_op jit(solution)/shard_map/ppermute | solution.py:598
  142.1 28.8 %collective-permute-start.15 = (f32[4,80,128]{2,1,0:T(8,128)S(1)}, f32[4,80,128]{2,1,0:T(8,128)S(1)}, u32[]{:S(2)}, u32[]{:S(2)}) collective-permute-start(f32[4,80,128]{2,1,0:T(8,128)S(1)} %get-tuple-element.56), channel_id=1, source_target_pairs={{0,1},{1,0},{2,3},{3,2},{4,5},{5,4},{6,7},{7,6},{8,9},{9,8},{10,11... | collective-permute-start | bytes 491528 | tf_op jit(solution)/shard_map/ppermute | solution.py:503
  168.6 19.6 %collective-permute-start.16 = (f32[4,80,256]{2,1,0:T(8,128)}, f32[4,80,256]{2,1,0:T(8,128)S(1)}, u32[]{:S(2)}, u32[]{:S(2)}) collective-permute-start(f32[4,80,256]{2,1,0:T(8,128)} %get-tuple-element.37), channel_id=1, source_target_pairs={{0,16},{8,24},{1,17},{9,25},{2,18},{10,26},{3,19},{11,27},{4,20},{... | collective-permute-start | bytes 983048 | tf_op jit(solution)/shard_map/ppermute | solution.py:620
  170.9 49.2 %collective-permute-start.10 = (f32[4,48,128]{2,1,0:T(8,128)S(1)}, f32[4,48,128]{2,1,0:T(8,128)}, u32[]{:S(2)}, u32[]{:S(2)}) collective-permute-start(f32[4,48,128]{2,1,0:T(8,128)S(1)} %get-tuple-element.60), channel_id=1, source_target_pairs={{0,1},{1,0},{2,3},{3,2},{4,5},{5,4},{6,7},{7,6},{8,9},{9,8},{10,11... | collective-permute-start | bytes 294920 | tf_op jit(solution)/shard_map/ppermute | solution.py:503
  172.9 44.9 %copy-start.2 = (f32[256,256]{1,0:T(8,128)S(1)}, f32[256,256]{1,0:T(8,128)}, u32[]{:S(2)}) copy-start(f32[256,256]{1,0:T(8,128)} %fusion.22.table_ref) | copy-start | bytes 786436
  188.2 0.7 copy-start.20
  188.9 0.8 copy-start.19
  189.7 0.9 copy-start.17
  190.6 18.7 %copy-start.21 = (f32[4,80,256]{2,1,0:T(8,128)S(1)}, f32[4,80,256]{2,1,0:T(8,128)}, u32[]{:S(2)}) copy-start(f32[4,80,256]{2,1,0:T(8,128)} %copy-done.20) | copy-start | bytes 983044
  207.8 9.8 %collective-permute-start.21 = (f32[4,48,256]{2,1,0:T(8,128)}, f32[4,48,256]{2,1,0:T(8,128)S(1)}, u32[]{:S(2)}, u32[]{:S(2)}) collective-permute-start(f32[4,48,256]{2,1,0:T(8,128)} %get-tuple-element.42), channel_id=1, source_target_pairs={{0,16},{8,24},{1,17},{9,25},{2,18},{10,26},{3,19},{11,27},{4,20},{... | collective-permute-start | bytes 589832 | tf_op jit(solution)/shard_map/ppermute | solution.py:620
  209.4 8.4 %collective-permute-start.17 = (f32[4,80,128]{2,1,0:T(8,128)S(1)}, f32[4,80,128]{2,1,0:T(8,128)S(1)}, u32[]{:S(2)}, u32[]{:S(2)}) collective-permute-start(f32[4,80,128]{2,1,0:T(8,128)S(1)} %get-tuple-element.58), channel_id=1, source_target_pairs={{0,1},{1,0},{2,3},{3,2},{4,5},{5,4},{6,7},{7,6},{8,9},{9,8},{10,11... | collective-permute-start | bytes 491528 | tf_op jit(solution)/shard_map/ppermute | solution.py:503
  217.7 1.4 collective-permute-start.22
  226.1 6.6 %collective-permute-start.23 = (f32[256,128]{1,0:T(8,128)}, f32[256,128]{1,0:T(8,128)S(1)}, u32[]{:S(2)}, u32[]{:S(2)}) collective-permute-start(f32[256,128]{1,0:T(8,128)} %get-tuple-element.43), channel_id=1, source_target_pairs={{0,2},{1,3},{2,0},{3,1},{4,6},{5,7},{6,4},{7,5},{8,10},{9,11},{10,... | collective-permute-start | bytes 393224 | tf_op jit(solution)/shard_map/ppermute | solution.py:525
  226.9 8.4 %collective-permute-start.24 = (f32[256,128]{1,0:T(8,128)}, f32[256,128]{1,0:T(8,128)S(1)}, u32[]{:S(2)}, u32[]{:S(2)}) collective-permute-start(f32[256,128]{1,0:T(8,128)} %get-tuple-element.44), channel_id=1, source_target_pairs={{0,4},{1,5},{2,6},{3,7},{4,0},{5,1},{6,2},{7,3},{8,12},{9,13},{10,... | collective-permute-start | bytes 393224 | tf_op jit(solution)/shard_map/ppermute | solution.py:525
  227.6 7.7 %collective-permute-start.25 = (f32[256,128]{1,0:T(8,128)}, f32[256,128]{1,0:T(8,128)S(1)}, u32[]{:S(2)}, u32[]{:S(2)}) collective-permute-start(f32[256,128]{1,0:T(8,128)} %get-tuple-element.45), channel_id=1, source_target_pairs={{0,6},{1,7},{2,4},{3,5},{4,2},{5,3},{6,0},{7,1},{8,14},{9,15},{10,... | collective-permute-start | bytes 393224 | tf_op jit(solution)/shard_map/ppermute | solution.py:525
  232.7 2.6 copy-start.24
  235.3 0.7 copy-start.25
  235.3 0.7 copy-start.26
  243.1 2.0 collective-permute-start.26
  264.7 3.7 %collective-permute-start.27 = (f32[16,6]{1,0:T(8,128)S(1)}, f32[16,6]{1,0:T(8,128)S(1)}, u32[]{:S(2)}, u32[]{:S(2)}) collective-permute-start(f32[16,6]{1,0:T(8,128)S(1)} %slice_select_fusion.17), channel_id=1, source_target_pairs={{0,4},{1,5},{2,6},{3,7},{4,0},{5,1},{6,2},{7,3},{8,12},{9,13},{10,... | collective-permute-start | bytes 1160 | tf_op jit(solution)/shard_map/ppermute | solution.py:553
  269.1 3.7 %collective-permute-start.28 = (f32[8,6]{1,0:T(8,128)S(1)}, f32[8,6]{1,0:T(8,128)S(1)}, u32[]{:S(2)}, u32[]{:S(2)}) collective-permute-start(f32[8,6]{1,0:T(8,128)S(1)} %slice_select_fusion.18), channel_id=1, source_target_pairs={{0,2},{1,3},{2,0},{3,1},{4,6},{5,7},{6,4},{7,5},{8,10},{9,11},{10,... | collective-permute-start | bytes 584 | tf_op jit(solution)/shard_map/ppermute | solution.py:553
  272.7 1.2 collective-permute-start.29

commit v4 on v3

--- a/solution.py
+++ b/solution.py
@@ -382,20 +382,22 @@
         weighted = jnp.concatenate(weighted, axis=0).astype(jnp.bfloat16)
         states = q_ref[:, 0, at].reshape(n_states * group, field.shape[-1])
         total += lax.dot_general(
-            states, weighted, (((1,), (1,)), ((), ())), preferred_element_type=jnp.float32
+            weighted, states, (((1,), (1,)), ((), ())), preferred_element_type=jnp.float32
         )
     acc[...] = total
 
     @pl.when(step == last_step)
     def _():
-        found = acc[...].reshape(n_states, group, parts * group)
+        found = acc[...].reshape(parts, group, n_states * group)
         row = lax.broadcasted_iota(jnp.int32, found.shape, 1)
         col = lax.broadcasted_iota(jnp.int32, found.shape, 2)
         own = jnp.sum(jnp.where(row == col % group, found, 0.0), axis=1)
-        fold_r = lax.broadcasted_iota(jnp.int32, (parts * group, parts), 0)
-        fold_c = lax.broadcasted_iota(jnp.int32, (parts * group, parts), 1)
-        fold = jnp.where(fold_r // group == fold_c, 1.0, 0.0)
-        out_ref[...] = jnp.dot(own, fold, precision=highest, preferred_element_type=jnp.float32)
+        fold_r = lax.broadcasted_iota(jnp.int32, (n_states, n_states * group), 0)
+        fold_c = lax.broadcasted_iota(jnp.int32, (n_states, n_states * group), 1)
+        fold = jnp.where(fold_c // group == fold_r, 1.0, 0.0)
+        out_ref[...] = lax.dot_general(
+            fold, own, (((1,), (1,)), ((), ())), precision=highest, preferred_element_type=jnp.float32
+        )
 
 
 def elements(received, added, b, states):
@@ -413,7 +415,7 @@
         + [vec]
         + [pl.BlockSpec((n_states, 1, block, size_z), lambda p, y: (0, p, y, 0))],
         out_specs=pl.BlockSpec((n_states, parts), lambda p, y: (0, 0)),
-        scratch_shapes=[pltpu.VMEM((n_states * 16, parts * 16), jnp.float32)],
+        scratch_shapes=[pltpu.VMEM((parts * 16, n_states * 16), jnp.float32)],
         name="elements",
     )(received, added, b, states)
 
@@ -493,7 +495,7 @@
             jnp.exp(-(2.0 * planes) * theta * (jnp.abs(o - self.chip) - 1).astype(jnp.float32))
             for o in other
         ]
-        self.total = 0.0
+        self.pieces = []
 
     def pick(self, array, mine):
         take = self.first if mine else jnp.logical_not(self.first)
@@ -502,15 +504,16 @@
     def swap(self, array):
         return lax.ppermute(array, "grid", [(i, i ^ 1) for i in range(self.count)])
 
-    def add(self, piece, at):
+    def add(self, piece):
         mine, got = self.pick(piece, True), self.swap(self.pick(piece, False))
         both = jnp.where(
             self.first, jnp.concatenate([mine, got]), jnp.concatenate([got, mine])
         )
-        rows = self.table_y[at : at + piece.shape[1]]
-        self.total += jnp.einsum("xyl,yk->xkl", both, rows, precision=highest)
+        self.pieces.append(both)
 
     def solve(self):
+        whole = jnp.concatenate(self.pieces, axis=1)
+        total = jnp.einsum("xyl,yk->xkl", whole, self.table_y, precision=highest)
         shape = jax.ShapeDtypeStruct(self.r.shape, jnp.float32)
         vmem = pl.BlockSpec(memory_space=pltpu.VMEM)
         smem = pl.BlockSpec(memory_space=pltpu.SMEM)
@@ -520,18 +523,18 @@
             in_specs=[smem] + [vmem] * 4,
             out_specs=[vmem] * len(self.hops),
             name="moments",
-        )(self.side, self.total, self.low, self.high, self.r)
+        )(self.side, total, self.low, self.high, self.r)
         far = [
             lax.ppermute(sent, "grid", [(i, i ^ (2 * k)) for i in range(self.count)])
             for k, sent in zip(self.hops, sums)
         ]
         field = pl.pallas_call(
             functools.partial(solve_kernel, len(far)),
-            out_shape=jax.ShapeDtypeStruct(self.total.shape, jnp.float32),
+            out_shape=jax.ShapeDtypeStruct(total.shape, jnp.float32),
             in_specs=[pl.BlockSpec(memory_space=pltpu.SMEM)] + [vmem] * (5 + 2 * len(far)),
             out_specs=vmem,
             name="solve",
-        )(self.side, self.total, self.low, self.high, self.r, self.scale, *far, *self.decay)
+        )(self.side, total, self.low, self.high, self.r, self.scale, *far, *self.decay)
         field = jnp.einsum("xkl,ky->xyl", field, self.table_y, precision=highest)
         lower, upper = field[: self.planes], field[self.planes :]
         mine = jnp.where(self.first, lower, upper)
@@ -541,19 +544,19 @@
         return back(mine, flip(True)) + back(got, flip(False))
 
 
-def scatter_sum(value, axis):
-    count = lax.axis_size(axis)
-    place = lax.axis_index(axis)
-    step = count // 2
-    while step:
-        half = value.shape[0] // 2
-        upper = (place // step) % 2 == 1
-        low, high = value[:half], value[half:]
-        pairs = [(i, i ^ step) for i in range(count)]
-        sent = lax.ppermute(jnp.where(upper, low, high), axis, pairs)
-        value = jnp.where(upper, high, low) + sent
-        step //= 2
-    return value
+def scatter_sum(value):
+    count = lax.axis_size("grid")
+    place = lax.axis_index("grid")
+    blocks = value.reshape(count // 2, 2, -1, value.shape[1])
+    first = place % 2 == 0
+    sent = jnp.where(first, blocks[:, 1], blocks[:, 0])
+    mine = jnp.where(first, blocks[:, 0], blocks[:, 1])
+    mine = mine + lax.ppermute(sent, "grid", [(i, i ^ 1) for i in range(count)])
+    pick = lambda k: lax.dynamic_index_in_dim(mine, (place // 2) ^ k, 0, keepdims=False)
+    total = pick(0)
+    for k in range(1, count // 2):
+        total = total + lax.ppermute(pick(k), "grid", [(i, i ^ (2 * k)) for i in range(count)])
+    return total
 
 
 def on_device(vectors, potential, added_field, qp_states):
@@ -616,13 +619,14 @@
             b, arrived[c - 1] = lax.optimization_barrier((b, arrived[c - 1]))
         b, rho = taylor(span, flags, mask, own, potential, added, mates, poisson.table_z, sources, b)
         if c + AHEAD < len(layout):
-            messages.append(exchange(c + AHEAD, (messages[c + AHEAD - 1], rho)))
+            after = (messages[c + AHEAD - 1], rho) if c == 0 else rho
+            messages.append(exchange(c + AHEAD, after))
         arrived.append(lax.ppermute(rho, "grp", group_pairs))
-    for c, ((o0, _), _, _) in enumerate(layout):
-        poisson.add(arrived[c], o0)
+    for c in range(len(layout)):
+        poisson.add(arrived[c])
     received = poisson.solve()
     partial = elements(received, added, b, qp_states)
-    return scatter_sum(partial, "grid")[None]
+    return scatter_sum(partial)[None]
 
 
 def solution(mesh):

time: 277 us -> 292 us (1.054)
  waiting for transfers between devices: 44.6 us -> 67.8 us
  starting transfers between devices: 72.1 us -> 66.3 us
  matrix products: 13.4 us -> 9.42 us
    ppermute x4, waiting for transfers between devices: 5.55 us -> 18.1 us  [exchange(): return (direct, lax.ppermute(held(rest), 'grid', pairs))]
    ppermute x4, waiting for transfers between devices: 2.64 us -> 13.2 us  [exchange(): hop = lax.ppermute(rest, 'grid', first_leg)]
    dot_general x4 -> x1, matrix products: 7.08 us -> 3.11 us  [solve(): total = jnp.einsum('xyl,yk->xkl', whole, self.table_y, precision=highest)]
    ppermute x5, starting transfers between devices: 26.8 us -> 23.1 us  [swap(): return lax.ppermute(array, 'grid', [(i, i ^ 1) for i in range(self.count)])]
    ppermute x3 -> x4, waiting for transfers between devices: 6.19 us -> 4.06 us  [the longest x3 3.02 us: scatter_sum(): lax.ppermute(pick(k), 'grid', [(i, i ^ 2 * k) for i in range(count)])]
    unnamed x58 -> x56, local copies, waits for them, and re-layouts: 6.11 us -> 6.05 us
  transfers between devices with their start and end apart: 30 -> 31, of which waited for: 11 -> 14; matrix products, arithmetic and copies ran while one was open for 13% -> 11% of each run, Pallas kernels for 30% -> 22%
where the time goes in v4:
time: 292 us; the launch traced here: 290 us
  Pallas kernels  106 us (36%)
  waiting for transfers between devices  67.8 us (23%)
  starting transfers between devices  66.3 us (23%)
  other arithmetic  22.6 us (8%)
  local copies, waits for them, and re-layouts  17.4 us (6%)
  matrix products  9.42 us (3%)
    pallas_call x4, Pallas kernels, taylor(): pl.pallas_call(functools.partial(taylor_kernel, span, shape, planes, b is...  82.1 us
    ppermute x4, waiting for transfers between devices, on_device(): arrived.append(lax.ppermute(rho, 'grp', group_pairs))  25.9 us
    ppermute x5, starting transfers between devices, swap(): return lax.ppermute(array, 'grid', [(i, i ^ 1) for i in range(self.count)])  23.1 us
    ppermute x4, waiting for transfers between devices, exchange(): return (direct, lax.ppermute(held(rest), 'grid', pairs))  18.1 us
    pallas_call x1, Pallas kernels, elements(): pl.pallas_call(functools.partial(elements_kernel, n_states, parts, planes...  17 us
    ppermute x4, waiting for transfers between devices, exchange(): hop = lax.ppermute(rest, 'grid', first_leg)  13.2 us
    ppermute x4, starting transfers between devices, exchange(): direct = lax.ppermute(held(block), 'grid', chip_pairs)  13.1 us
    ppermute x4, starting transfers between devices, exchange(): hop = lax.ppermute(rest, 'grid', first_leg)  12.4 us
  transfers between devices with their start and end apart: 31, of which 14 were waited for; matrix products, arithmetic and copies ran while one was open for 11% of the time, Pallas kernels for 22%

profile of v4, /device:TPU:28, one launch (start us, length us, event | category | flops | bytes accessed | tf_op | source)
XLA Modules:
  0.0 289.8 jit_solution(10882826934587704126)
XLA Ops:
  0.0 1.1 slice.177
  1.2 1.2 slice_select_fusion.5
  2.4 1.0 pad_maximum_fusion.2
  3.4 3.4 %collective-permute-start.4 = (f32[14,56,256]{2,1,0:T(8,128)}, f32[14,56,256]{2,1,0:T(8,128)}, u32[]{:S(2)}, u32[]{:S(2)}) collective-permute-start(f32[14,56,256]{2,1,0:T(8,128)} %pad_maximum_fusion.2), channel_id=1, source_target_pairs={{3,7},{4,0},{11,15},{12,8},{19,23},{20,16},{27,31},{28,24}} | collective-permute-start | bytes 2408456 | tf_op jit(solution)/shard_map/ppermute | solution.py:598
  6.8 2.2 slice.176
  9.1 4.1 %collective-permute-start.3 = (f32[16,56,256]{2,1,0:T(8,128)}, f32[16,56,256]{2,1,0:T(8,128)}, u32[]{:S(2)}, u32[]{:S(2)}) collective-permute-start(f32[16,56,256]{2,1,0:T(8,128)} %bitcast.10), channel_id=1, source_target_pairs={{1,2},{2,1},{3,4},{4,3},{5,6},{6,5},{9,10},{10,9},{11,12},{12,11},... | collective-permute-start | bytes 2752520 | tf_op jit(solution)/shard_map/ppermute | solution.py:601
  14.7 1.5 fusion.51
  16.2 1.2 pad_maximum_fusion
  17.4 2.4 collective-permute-start.7
  19.7 1.0 slice.189
  22.3 2.1 collective-permute-start.19
  24.5 1.8 fusion.14.table_ref
  26.3 1.1 multiply_exponential_fusion
  28.0 10.5 %collective-permute-done.19 = f32[14,40,256]{2,1,0:T(8,128)} collective-permute-done((f32[14,40,256]{2,1,0:T(8,128)}, f32[14,40,256]{2,1,0:T(8,128)}, u32[]{:S(2)}, u32[]{:S(2)}) %collective-permute-start.19) | collective-permute-done | bytes 573472 | tf_op jit(solution)/shard_map/ppermute | solution.py:598
  39.2 2.0 slice.188
  41.2 1.2 pad_maximum_fusion.1
  42.4 4.5 %collective-permute-start.12 = (f32[14,80,256]{2,1,0:T(8,128)S(1)}, f32[14,80,256]{2,1,0:T(8,128)S(1)}, u32[]{:S(2)}, u32[]{:S(2)}) collective-permute-start(f32[14,80,256]{2,1,0:T(8,128)S(1)} %pad_maximum_fusion.1), channel_id=1, source_target_pairs={{3,7},{4,0},{11,15},{12,8},{19,23},{20,16},{27,31},{28,24}} | collective-permute-start | bytes 3440648 | tf_op jit(solution)/shard_map/ppermute | solution.py:598
  46.9 2.1 exponential-minus-one_negate_fusion
  48.9 3.5 %fusion.52 = (f32[4,4,80,256]{3,2,1,0:T(8,128)}, f32[4,4,80,256]{3,2,1,0:T(8,128)}) fusion(f32[6,4,256,256]{3,2,1,0:T(8,128)} %bitcast.73), kind=kLoop, calls=%fused_computation.112 | loop fusion | bytes 5242880 | tf_op jit(solution)/shard_map/slice | solution.py:595
  52.7 2.1 collective-permute-start.6
  54.8 1.3 collective-permute-start.5
  56.1 1.2 broadcast_select_fusion.1
  57.4 2.8 collective-permute-done.12
  60.1 1.3 collective-permute-start.8
  61.4 0.9 broadcast_select_fusion.3
  62.3 1.2 broadcast_select_fusion
  63.6 1.0 copy-done.21
  64.6 12.3 %collective-permute-done.5.refs_1_ = f32[14,56,256]{2,1,0:T(8,128)S(1)} collective-permute-done((f32[14,56,256]{2,1,0:T(8,128)S(1)}, f32[14,56,256]{2,1,0:T(8,128)S(1)}, u32[]{:S(2)}, u32[]{:S(2)}) %collective-permute-start.5) | collective-permute-done | bytes 802848 | tf_op jit(solution)/shard_map/ppermute | solution.py:602
  77.8 16.7 %taylor.4 = (f32[6,4,256,256]{3,2,1,0:T(8,128)}, f32[4,48,256]{2,1,0:T(8,128)}) custom-call(s32[2]{0:T(128)} %add_convert_fusion.1.flag_ref, f32[2]{0:T(128)} %add_convert_fusion.2.mask_ref, f32[6,4,256,256]{3,2,1,0:T(8,128)} %bitcast.74, f32[4,256,256]{2,1,0:T(8,128)} %pot_ref.7, f32[4,256,256]{2,1,0:T(8,128)} %bitcast.79, ...), custom_call_target="tpu_custom_call" | custom-call | flops 6881280000 | bytes 20971520 | tf_op jit(solution)/shard_map/taylor/pallas_call | solution.py:338
  94.5 1.3 collective-permute-start.9
  95.8 5.7 %collective-permute-done.8.refs_3_.refs_1_ = f32[14,80,256]{2,1,0:T(8,128)} collective-permute-done((f32[14,80,256]{2,1,0:T(8,128)}, f32[14,80,256]{2,1,0:T(8,128)}, u32[]{:S(2)}, u32[]{:S(2)}) %collective-permute-start.8) | collective-permute-done | bytes 1146912 | tf_op jit(solution)/shard_map/ppermute | solution.py:602
  101.6 1.3 collective-permute-start.13
  102.9 4.8 %collective-permute-start.11 = (f32[16,80,256]{2,1,0:T(8,128)S(1)}, f32[16,80,256]{2,1,0:T(8,128)S(1)}, u32[]{:S(2)}, u32[]{:S(2)}) collective-permute-start(f32[16,80,256]{2,1,0:T(8,128)S(1)} %bitcast.95), channel_id=1, source_target_pairs={{1,2},{2,1},{3,4},{4,3},{5,6},{6,5},{9,10},{10,9},{11,12},{12,11},... | collective-permute-start | bytes 3932168 | tf_op jit(solution)/shard_map/ppermute | solution.py:601
  107.7 24.1 %taylor.5 = (f32[6,4,256,256]{3,2,1,0:T(8,128)}, f32[4,80,256]{2,1,0:T(8,128)}) custom-call(s32[2]{0:T(128)} %add_convert_fusion.1.flag_ref, f32[2]{0:T(128)} %add_convert_fusion.2.mask_ref, f32[6,4,256,256]{3,2,1,0:T(8,128)} %bitcast.75, f32[4,256,256]{2,1,0:T(8,128)} %pot_ref.7, f32[4,256,256]{2,1,0:T(8,128)} %bitcast.80, ...), custom_call_target="tpu_custom_call", output_to_operand_aliasing={{0}: (13, {})} | custom-call | flops 11796480000 | bytes 20971520 | tf_op jit(solution)/shard_map/taylor/pallas_call | solution.py:338
  131.8 1.3 collective-permute-start.14
  133.1 1.3 collective-permute-start.20
  134.4 2.1 collective-permute-start.18
  136.5 1.0 slice_select_fusion.16
  137.5 22.7 %collective-permute-start.10 = (f32[4,48,128]{2,1,0:T(8,128)S(1)}, f32[4,48,128]{2,1,0:T(8,128)}, u32[]{:S(2)}, u32[]{:S(2)}) collective-permute-start(f32[4,48,128]{2,1,0:T(8,128)S(1)} %get-tuple-element.60), channel_id=1, source_target_pairs={{0,1},{1,0},{2,3},{3,2},{4,5},{5,4},{6,7},{7,6},{8,9},{9,8},{10,11... | collective-permute-start | bytes 294920 | tf_op jit(solution)/shard_map/ppermute | solution.py:505
  160.2 1.1 copy-done.17
  161.3 24.1 %taylor.6 = (f32[6,4,256,256]{3,2,1,0:T(8,128)}, f32[4,80,256]{2,1,0:T(8,128)}) custom-call(s32[2]{0:T(128)} %add_convert_fusion.1.flag_ref, f32[2]{0:T(128)} %add_convert_fusion.2.mask_ref, f32[6,4,256,256]{3,2,1,0:T(8,128)} %bitcast.76, f32[4,256,256]{2,1,0:T(8,128)} %pot_ref.7, f32[4,256,256]{2,1,0:T(8,128)} %bitcast.81, ...), custom_call_target="tpu_custom_call", output_to_operand_aliasing={{0}: (13, {})} | custom-call | flops 11796480000 | bytes 20971520 | tf_op jit(solution)/shard_map/taylor/pallas_call | solution.py:338
  185.4 1.0 slice_select_fusion.10
  186.5 1.3 collective-permute-start.16
  188.5 1.0 maximum_select_fusion.2
  189.5 17.8 %collective-permute-done.16 = f32[4,80,256]{2,1,0:T(8,128)S(1)} collective-permute-done((f32[4,80,256]{2,1,0:T(8,128)}, f32[4,80,256]{2,1,0:T(8,128)S(1)}, u32[]{:S(2)}, u32[]{:S(2)}) %collective-permute-start.16) | collective-permute-done | bytes 327712 | tf_op jit(solution)/shard_map/ppermute | solution.py:624
  208.1 17.1 %taylor.7 = (f32[6,4,256,256]{3,2,1,0:T(8,128)}, f32[4,48,256]{2,1,0:T(8,128)}) custom-call(s32[2]{0:T(128)} %add_convert_fusion.1.flag_ref, f32[2]{0:T(128)} %add_convert_fusion.2.mask_ref, f32[6,4,256,256]{3,2,1,0:T(8,128)} %bitcast.77, f32[4,256,256]{2,1,0:T(8,128)} %pot_ref.7, f32[4,256,256]{2,1,0:T(8,128)} %bitcast.82, ...), custom_call_target="tpu_custom_call", output_to_operand_aliasing={{0}: (13, {})} | custom-call | flops 6881280000 | bytes 20971520 | tf_op jit(solution)/shard_map/taylor/pallas_call | solution.py:338
  225.3 1.5 collective-permute-start.21
  227.0 8.2 %collective-permute-done.21 = f32[4,48,256]{2,1,0:T(8,128)S(1)} collective-permute-done((f32[4,48,256]{2,1,0:T(8,128)}, f32[4,48,256]{2,1,0:T(8,128)S(1)}, u32[]{:S(2)}, u32[]{:S(2)}) %collective-permute-start.21) | collective-permute-done | bytes 196640 | tf_op jit(solution)/shard_map/ppermute | solution.py:624
  235.3 1.2 collective-permute-done.22
  236.6 3.1 %convolution_bitcast_fusion.1.f_ref = f32[8,256,128]{2,1,0:T(8,128)} fusion(f32[8,48,128]{2,1,0:T(8,128)S(1)} %maximum_select_fusion.3, f32[8,80,128]{2,1,0:T(8,128)S(1)} %maximum_select_fusion.1, f32[8,80,128]{2,1,0:T(8,128)S(1)} %maximum_select_fusion, f32[8,48,128]{2,1,0:T(8,128)S(1)} %maximum_select_fusion.2, s32[256]{0:T(256)S(1)} %iota_add_fusion), kind=kOutput, calls=%fused_computation.2 | convolution fusion | flops 806748160 | bytes 2098176 | tf_op jit(solution)/shard_map/xyl,yk->xkl/dot_general | solution.py:516
  239.7 2.9 %moments.1 = (f32[256,128]{1,0:T(8,128)}, f32[256,128]{1,0:T(8,128)}, f32[256,128]{1,0:T(8,128)}) custom-call(f32[3]{0:T(128)} %add_convert_fusion.side_ref, f32[8,256,128]{2,1,0:T(8,128)} %convolution_bitcast_fusion.1.f_ref, f32[8,256,128]{2,1,0:T(8,128)} %get-tuple-element.64.low_ref, f32[8,256,128]{2,1,0:T(8,128)} %get-tuple-element.63.high_ref, ...), custom_call_target="tpu_custom_call" | custom-call | tf_op jit(solution)/shard_map/moments/pallas_call | solution.py:520
  242.8 3.3 %collective-permute-start.25 = (f32[256,128]{1,0:T(8,128)}, f32[256,128]{1,0:T(8,128)S(1)}, u32[]{:S(2)}, u32[]{:S(2)}) collective-permute-start(f32[256,128]{1,0:T(8,128)} %get-tuple-element.45), channel_id=1, source_target_pairs={{0,6},{1,7},{2,4},{3,5},{4,2},{5,3},{6,0},{7,1},{8,14},{9,15},{10,... | collective-permute-start | bytes 393224 | tf_op jit(solution)/shard_map/ppermute | solution.py:528
  246.1 3.1 %collective-permute-done.23.refs_0_ = f32[256,128]{1,0:T(8,128)S(1)} collective-permute-done((f32[256,128]{1,0:T(8,128)}, f32[256,128]{1,0:T(8,128)S(1)}, u32[]{:S(2)}, u32[]{:S(2)}) %collective-permute-start.23) | collective-permute-done | bytes 131104 | tf_op jit(solution)/shard_map/ppermute | solution.py:528
  249.2 2.0 collective-permute-done.24.refs_1_
  251.9 3.7 %solve.1 = f32[8,256,128]{2,1,0:T(8,128)} custom-call(f32[3]{0:T(128)} %add_convert_fusion.side_ref, f32[8,256,128]{2,1,0:T(8,128)} %convolution_bitcast_fusion.1.f_ref, f32[8,256,128]{2,1,0:T(8,128)} %get-tuple-element.64.low_ref, f32[8,256,128]{2,1,0:T(8,128)} %get-tuple-element.63.high_ref, f32[256,128]{1,0:T(8,128)} %get-tuple-element.69.r_ref, ...), custom_call_target="tpu_custom_call" | custom-call | tf_op jit(solution)/shard_map/solve/pallas_call | solution.py:531
  255.7 3.3 %convolution_bitcast_fusion = f32[8,256,128]{2,1,0:T(8,128)S(1)} fusion(f32[8,256,128]{2,1,0:T(8,128)} %solve.1, s32[256]{0:T(256)S(1)} %iota_add_fusion), kind=kOutput, calls=%fused_computation.1 | convolution fusion | flops 805961728 | bytes 2098176 | tf_op jit(solution)/shard_map/xkl,ky->xyl/dot_general | solution.py:538
  260.0 1.0 fusion.7
  261.1 2.0 convolution_add_fusion.rec_ref
  263.0 17.0 %elements.1 = f32[32,6]{1,0:T(8,128)} custom-call(f32[4,256,256]{2,1,0:T(8,128)} %convolution_add_fusion.rec_ref, f32[4,256,256]{2,1,0:T(8,128)} %bitcast.83, f32[6,4,256,256]{3,2,1,0:T(8,128)} %get-tuple-element.46.b_ref, bf16[32,4,256,256]{3,2,1,0:T(8,128)(2,1)} %q_ref.1), custom_call_target="tpu_custom_call" | custom-call | tf_op jit(solution)/shard_map/elements/pallas_call | solution.py:410
  280.9 1.0 collective-permute-done.27
  282.7 1.8 collective-permute-start.28
  284.8 1.5 collective-permute-start.30
  286.3 1.7 collective-permute-done.29
  288.1 1.2 collective-permute-done.30
  (108 shorter events, 12.0 us)
Async XLA Ops:
  0.0 2.4 copy-start.1
  0.0 77.8 %collective-permute-start = (f32[6,4,256,256]{3,2,1,0:T(8,128)}, f32[6,4,256,256]{3,2,1,0:T(8,128)}, u32[]{:S(2)}, u32[]{:S(2)}) collective-permute-start(f32[6,4,256,256]{3,2,1,0:T(8,128)} %bitcast.67), channel_id=1, source_target_pairs={{0,1},{1,0},{2,3},{3,2},{4,5},{5,4},{6,7},{7,6},{8,9},{9,8},{10,11... | collective-permute-start | bytes 18874376 | tf_op jit(solution)/shard_map/ppermute | solution.py:605
  1.2 2.2 copy-start.2
  2.4 6.7 %copy-start.13 = (f32[3,56,256]{2,1,0:T(8,128)}, f32[3,56,256]{2,1,0:T(8,128)S(1)}, u32[]{:S(2)}) copy-start(f32[3,56,256]{2,1,0:T(8,128)S(1)} %slice_select_fusion.5) | copy-start | bytes 516100
  2.4 6.7 %copy-start.15 = (f32[3,56,256]{2,1,0:T(8,128)}, f32[3,56,256]{2,1,0:T(8,128)S(1)}, u32[]{:S(2)}) copy-start(f32[3,56,256]{2,1,0:T(8,128)S(1)} %slice_select_fusion.6) | copy-start | bytes 516100
  3.4 9.8 %copy-start = (f32[1,4,256,256]{3,2,1,0:T(8,128)S(1)}, f32[1,4,256,256]{3,2,1,0:T(8,128)}, u32[]{:S(2)}) copy-start(f32[1,4,256,256]{3,2,1,0:T(8,128)} %param.6) | copy-start | bytes 3145732
  3.4 39.0 %collective-permute-start.4 = (f32[14,56,256]{2,1,0:T(8,128)}, f32[14,56,256]{2,1,0:T(8,128)}, u32[]{:S(2)}, u32[]{:S(2)}) collective-permute-start(f32[14,56,256]{2,1,0:T(8,128)} %pad_maximum_fusion.2), channel_id=1, source_target_pairs={{3,7},{4,0},{11,15},{12,8},{19,23},{20,16},{27,31},{28,24}} | collective-permute-start | bytes 2408456 | tf_op jit(solution)/shard_map/ppermute | solution.py:598
  9.1 43.4 %collective-permute-start.3 = (f32[16,56,256]{2,1,0:T(8,128)}, f32[16,56,256]{2,1,0:T(8,128)}, u32[]{:S(2)}, u32[]{:S(2)}) collective-permute-start(f32[16,56,256]{2,1,0:T(8,128)} %bitcast.10), channel_id=1, source_target_pairs={{1,2},{2,1},{3,4},{4,3},{5,6},{6,5},{9,10},{10,9},{11,12},{12,11},... | collective-permute-start | bytes 2752520 | tf_op jit(solution)/shard_map/ppermute | solution.py:601
  13.9 2.3 copy-start.9
  14.7 1.5 copy-start.11
  17.4 37.4 %collective-permute-start.7 = (f32[14,80,256]{2,1,0:T(8,128)}, f32[14,80,256]{2,1,0:T(8,128)}, u32[]{:S(2)}, u32[]{:S(2)}) collective-permute-start(f32[14,80,256]{2,1,0:T(8,128)} %pad_maximum_fusion), channel_id=1, source_target_pairs={{3,7},{4,0},{11,15},{12,8},{19,23},{20,16},{27,31},{28,24}} | collective-permute-start | bytes 3440648 | tf_op jit(solution)/shard_map/ppermute | solution.py:598
  20.7 0.7 copy-start.4
  20.8 1.5 copy-start.19
  22.3 16.2 %collective-permute-start.19 = (f32[14,40,256]{2,1,0:T(8,128)}, f32[14,40,256]{2,1,0:T(8,128)}, u32[]{:S(2)}, u32[]{:S(2)}) collective-permute-start(f32[14,40,256]{2,1,0:T(8,128)} %pad_maximum_fusion.3), channel_id=1, source_target_pairs={{3,7},{4,0},{11,15},{12,8},{19,23},{20,16},{27,31},{28,24}} | collective-permute-start | bytes 1720328 | tf_op jit(solution)/shard_map/ppermute | solution.py:598
  38.5 14.2 %collective-permute-start.2 = (f32[4,256,256]{2,1,0:T(8,128)S(1)}, f32[4,256,256]{2,1,0:T(8,128)}, u32[]{:S(2)}, u32[]{:S(2)}) collective-permute-start(f32[4,256,256]{2,1,0:T(8,128)S(1)} %bitcast.86), channel_id=1, source_target_pairs={{0,1},{1,0},{2,3},{3,2},{4,5},{5,4},{6,7},{7,6},{8,9},{9,8},{10,11... | collective-permute-start | bytes 3145736 | tf_op jit(solution)/shard_map/ppermute | solution.py:605
  41.2 5.7 %copy-start.23 = (f32[256,128]{1,0:T(8,128)S(1)}, f32[256,128]{1,0:T(8,128)}, u32[]{:S(2)}) copy-start(f32[256,128]{1,0:T(8,128)} %get-tuple-element.73) | copy-start | bytes 393220
  42.4 17.7 %collective-permute-start.12 = (f32[14,80,256]{2,1,0:T(8,128)S(1)}, f32[14,80,256]{2,1,0:T(8,128)S(1)}, u32[]{:S(2)}, u32[]{:S(2)}) collective-permute-start(f32[14,80,256]{2,1,0:T(8,128)S(1)} %pad_maximum_fusion.1), channel_id=1, source_target_pairs={{3,7},{4,0},{11,15},{12,8},{19,23},{20,16},{27,31},{28,24}} | collective-permute-start | bytes 3440648 | tf_op jit(solution)/shard_map/ppermute | solution.py:598
  48.9 3.6 %copy-start.3 = (f32[2,4,56,256]{3,2,1,0:T(8,128)S(1)}, f32[2,4,56,256]{3,2,1,0:T(8,128)}, u32[]{:S(2)}) copy-start(f32[2,4,56,256]{3,2,1,0:T(8,128)} %copy-done.2) | copy-start | bytes 1376260
  48.9 3.6 %copy-start.14 = (f32[3,56,256]{2,1,0:T(8,128)S(1)}, f32[3,56,256]{2,1,0:T(8,128)}, u32[]{:S(2)}) copy-start(f32[3,56,256]{2,1,0:T(8,128)} %copy-done.13) | copy-start | bytes 516100
  48.9 3.6 %copy-start.16 = (f32[3,56,256]{2,1,0:T(8,128)S(1)}, f32[3,56,256]{2,1,0:T(8,128)}, u32[]{:S(2)}) copy-start(f32[3,56,256]{2,1,0:T(8,128)} %copy-done.15) | copy-start | bytes 516100
  52.4 3.7 %copy-start.10 = (f32[3,80,256]{2,1,0:T(8,128)S(1)}, f32[3,80,256]{2,1,0:T(8,128)}, u32[]{:S(2)}) copy-start(f32[3,80,256]{2,1,0:T(8,128)} %copy-done.9) | copy-start | bytes 737284
  52.4 3.7 %copy-start.12 = (f32[3,80,256]{2,1,0:T(8,128)S(1)}, f32[3,80,256]{2,1,0:T(8,128)}, u32[]{:S(2)}) copy-start(f32[3,80,256]{2,1,0:T(8,128)} %copy-done.11) | copy-start | bytes 737284
  52.5 11.1 %collective-permute-start.1 = (f32[4,256,256]{2,1,0:T(8,128)S(1)}, f32[4,256,256]{2,1,0:T(8,128)S(1)}, u32[]{:S(2)}, u32[]{:S(2)}) collective-permute-start(f32[4,256,256]{2,1,0:T(8,128)S(1)} %copy-done.1), channel_id=1, source_target_pairs={{0,1},{1,0},{2,3},{3,2},{4,5},{5,4},{6,7},{7,6},{8,9},{9,8},{10,11... | collective-permute-start | bytes 3145736 | tf_op jit(solution)/shard_map/ppermute | solution.py:605
  52.7 8.7 %copy-start.5 = (f32[2,4,40,256]{3,2,1,0:T(8,128)S(1)}, f32[2,4,40,256]{3,2,1,0:T(8,128)}, u32[]{:S(2)}) copy-start(f32[2,4,40,256]{3,2,1,0:T(8,128)} %copy-done.4) | copy-start | bytes 983044
  52.7 8.7 %copy-start.20 = (f32[3,40,256]{2,1,0:T(8,128)S(1)}, f32[3,40,256]{2,1,0:T(8,128)}, u32[]{:S(2)}) copy-start(f32[3,40,256]{2,1,0:T(8,128)} %copy-done.19) | copy-start | bytes 368644
  52.7 43.1 %collective-permute-start.6 = (f32[16,80,256]{2,1,0:T(8,128)}, f32[16,80,256]{2,1,0:T(8,128)}, u32[]{:S(2)}, u32[]{:S(2)}) collective-permute-start(f32[16,80,256]{2,1,0:T(8,128)} %bitcast.12), channel_id=1, source_target_pairs={{1,2},{2,1},{3,4},{4,3},{5,6},{6,5},{9,10},{10,9},{11,12},{12,11},... | collective-permute-start | bytes 3932168 | tf_op jit(solution)/shard_map/ppermute | solution.py:601
  54.8 22.1 %collective-permute-start.5 = (f32[14,56,256]{2,1,0:T(8,128)S(1)}, f32[14,56,256]{2,1,0:T(8,128)S(1)}, u32[]{:S(2)}, u32[]{:S(2)}) collective-permute-start(f32[14,56,256]{2,1,0:T(8,128)S(1)} %broadcast_select_fusion.2), channel_id=1, source_target_pairs={{1,2},{2,1},{5,6},{6,5},{7,4},{0,3},{9,10},{10,9},{13,14},{14,13},... | collective-permute-start | bytes 2408456 | tf_op jit(solution)/shard_map/ppermute | solution.py:602
  57.4 5.0 %copy-start.7 = (f32[3,80,256]{2,1,0:T(8,128)S(1)}, f32[3,80,256]{2,1,0:T(8,128)}, u32[]{:S(2)}) copy-start(f32[3,80,256]{2,1,0:T(8,128)} %get-tuple-element.53) | copy-start | bytes 737284
  57.4 5.0 %copy-start.8 = (f32[3,80,256]{2,1,0:T(8,128)S(1)}, f32[3,80,256]{2,1,0:T(8,128)}, u32[]{:S(2)}) copy-start(f32[3,80,256]{2,1,0:T(8,128)} %get-tuple-element.51) | copy-start | bytes 737284
  60.1 41.5 %collective-permute-start.8 = (f32[14,80,256]{2,1,0:T(8,128)}, f32[14,80,256]{2,1,0:T(8,128)}, u32[]{:S(2)}, u32[]{:S(2)}) collective-permute-start(f32[14,80,256]{2,1,0:T(8,128)} %broadcast_select_fusion.1), channel_id=1, source_target_pairs={{1,2},{2,1},{5,6},{6,5},{7,4},{0,3},{9,10},{10,9},{13,14},{14,13},... | collective-permute-start | bytes 3440648 | tf_op jit(solution)/shard_map/ppermute | solution.py:602
  63.6 39.3 %copy-start.18 = (f32[4,4,80,256]{3,2,1,0:T(8,128)S(1)}, f32[4,4,80,256]{3,2,1,0:T(8,128)}, u32[]{:S(2)}) copy-start(f32[4,4,80,256]{3,2,1,0:T(8,128)} %get-tuple-element.50) | copy-start | bytes 3932164
  63.6 1.0 copy-start.21
  76.9 0.9 copy-start.27
  94.5 39.9 %collective-permute-start.9 = (f32[4,48,256]{2,1,0:T(8,128)}, f32[4,48,256]{2,1,0:T(8,128)}, u32[]{:S(2)}, u32[]{:S(2)}) collective-permute-start(f32[4,48,256]{2,1,0:T(8,128)} %get-tuple-element.28), channel_id=1, source_target_pairs={{0,16},{8,24},{1,17},{9,25},{2,18},{10,26},{3,19},{11,27},{4,20},{... | collective-permute-start | bytes 589832 | tf_op jit(solution)/shard_map/ppermute | solution.py:624
  101.6 35.9 %collective-permute-start.13 = (f32[14,80,256]{2,1,0:T(8,128)}, f32[14,80,256]{2,1,0:T(8,128)}, u32[]{:S(2)}, u32[]{:S(2)}) collective-permute-start(f32[14,80,256]{2,1,0:T(8,128)} %broadcast_select_fusion), channel_id=1, source_target_pairs={{1,2},{2,1},{5,6},{6,5},{7,4},{0,3},{9,10},{10,9},{13,14},{14,13},... | collective-permute-start | bytes 3440648 | tf_op jit(solution)/shard_map/ppermute | solution.py:602
  102.9 57.3 %collective-permute-start.11 = (f32[16,80,256]{2,1,0:T(8,128)S(1)}, f32[16,80,256]{2,1,0:T(8,128)S(1)}, u32[]{:S(2)}, u32[]{:S(2)}) collective-permute-start(f32[16,80,256]{2,1,0:T(8,128)S(1)} %bitcast.95), channel_id=1, source_target_pairs={{1,2},{2,1},{3,4},{4,3},{5,6},{6,5},{9,10},{10,9},{11,12},{12,11},... | collective-permute-start | bytes 3932168 | tf_op jit(solution)/shard_map/ppermute | solution.py:601
  131.8 53.6 %collective-permute-start.14 = (f32[4,80,256]{2,1,0:T(8,128)}, f32[4,80,256]{2,1,0:T(8,128)}, u32[]{:S(2)}, u32[]{:S(2)}) collective-permute-start(f32[4,80,256]{2,1,0:T(8,128)} %get-tuple-element.34), channel_id=1, source_target_pairs={{0,16},{8,24},{1,17},{9,25},{2,18},{10,26},{3,19},{11,27},{4,20},{... | collective-permute-start | bytes 983048 | tf_op jit(solution)/shard_map/ppermute | solution.py:624
  133.1 74.1 %collective-permute-start.20 = (f32[14,40,256]{2,1,0:T(8,128)}, f32[14,40,256]{2,1,0:T(8,128)}, u32[]{:S(2)}, u32[]{:S(2)}) collective-permute-start(f32[14,40,256]{2,1,0:T(8,128)} %broadcast_select_fusion.3), channel_id=1, source_target_pairs={{1,2},{2,1},{5,6},{6,5},{7,4},{0,3},{9,10},{10,9},{13,14},{14,13},... | collective-permute-start | bytes 1720328 | tf_op jit(solution)/shard_map/ppermute | solution.py:602
  134.4 72.8 %collective-permute-start.18 = (f32[16,40,256]{2,1,0:T(8,128)}, f32[16,40,256]{2,1,0:T(8,128)S(1)}, u32[]{:S(2)}, u32[]{:S(2)}) collective-permute-start(f32[16,40,256]{2,1,0:T(8,128)} %bitcast.96), channel_id=1, source_target_pairs={{1,2},{2,1},{3,4},{4,3},{5,6},{6,5},{9,10},{10,9},{11,12},{12,11},... | collective-permute-start | bytes 1966088 | tf_op jit(solution)/shard_map/ppermute | solution.py:601
  137.5 51.0 %collective-permute-start.10 = (f32[4,48,128]{2,1,0:T(8,128)S(1)}, f32[4,48,128]{2,1,0:T(8,128)}, u32[]{:S(2)}, u32[]{:S(2)}) collective-permute-start(f32[4,48,128]{2,1,0:T(8,128)S(1)} %get-tuple-element.60), channel_id=1, source_target_pairs={{0,1},{1,0},{2,3},{3,2},{4,5},{5,4},{6,7},{7,6},{8,9},{9,8},{10,11... | collective-permute-start | bytes 294920 | tf_op jit(solution)/shard_map/ppermute | solution.py:505
  160.2 1.1 copy-start.17
  186.4 3.0 %collective-permute-start.15 = (f32[4,80,128]{2,1,0:T(8,128)S(1)}, f32[4,80,128]{2,1,0:T(8,128)S(1)}, u32[]{:S(2)}, u32[]{:S(2)}) collective-permute-start(f32[4,80,128]{2,1,0:T(8,128)S(1)} %get-tuple-element.56), channel_id=1, source_target_pairs={{0,1},{1,0},{2,3},{3,2},{4,5},{5,4},{6,7},{7,6},{8,9},{9,8},{10,11... | collective-permute-start | bytes 491528 | tf_op jit(solution)/shard_map/ppermute | solution.py:505
  186.5 20.7 %collective-permute-start.16 = (f32[4,80,256]{2,1,0:T(8,128)}, f32[4,80,256]{2,1,0:T(8,128)S(1)}, u32[]{:S(2)}, u32[]{:S(2)}) collective-permute-start(f32[4,80,256]{2,1,0:T(8,128)} %get-tuple-element.37), channel_id=1, source_target_pairs={{0,16},{8,24},{1,17},{9,25},{2,18},{10,26},{3,19},{11,27},{4,20},{... | collective-permute-start | bytes 983048 | tf_op jit(solution)/shard_map/ppermute | solution.py:624
  207.3 0.9 copy-start.22
  225.3 9.9 %collective-permute-start.21 = (f32[4,48,256]{2,1,0:T(8,128)}, f32[4,48,256]{2,1,0:T(8,128)S(1)}, u32[]{:S(2)}, u32[]{:S(2)}) collective-permute-start(f32[4,48,256]{2,1,0:T(8,128)} %get-tuple-element.42), channel_id=1, source_target_pairs={{0,16},{8,24},{1,17},{9,25},{2,18},{10,26},{3,19},{11,27},{4,20},{... | collective-permute-start | bytes 589832 | tf_op jit(solution)/shard_map/ppermute | solution.py:624
  226.8 8.4 %collective-permute-start.17 = (f32[4,80,128]{2,1,0:T(8,128)S(1)}, f32[4,80,128]{2,1,0:T(8,128)S(1)}, u32[]{:S(2)}, u32[]{:S(2)}) collective-permute-start(f32[4,80,128]{2,1,0:T(8,128)S(1)} %get-tuple-element.58), channel_id=1, source_target_pairs={{0,1},{1,0},{2,3},{3,2},{4,5},{5,4},{6,7},{7,6},{8,9},{9,8},{10,11... | collective-permute-start | bytes 491528 | tf_op jit(solution)/shard_map/ppermute | solution.py:505
  235.2 1.4 collective-permute-start.22
  242.7 6.6 %collective-permute-start.23 = (f32[256,128]{1,0:T(8,128)}, f32[256,128]{1,0:T(8,128)S(1)}, u32[]{:S(2)}, u32[]{:S(2)}) collective-permute-start(f32[256,128]{1,0:T(8,128)} %get-tuple-element.43), channel_id=1, source_target_pairs={{0,2},{1,3},{2,0},{3,1},{4,6},{5,7},{6,4},{7,5},{8,10},{9,11},{10,... | collective-permute-start | bytes 393224 | tf_op jit(solution)/shard_map/ppermute | solution.py:528
  242.8 8.4 %collective-permute-start.24 = (f32[256,128]{1,0:T(8,128)}, f32[256,128]{1,0:T(8,128)S(1)}, u32[]{:S(2)}, u32[]{:S(2)}) collective-permute-start(f32[256,128]{1,0:T(8,128)} %get-tuple-element.44), channel_id=1, source_target_pairs={{0,4},{1,5},{2,6},{3,7},{4,0},{5,1},{6,2},{7,3},{8,12},{9,13},{10,... | collective-permute-start | bytes 393224 | tf_op jit(solution)/shard_map/ppermute | solution.py:528
  242.8 8.4 %collective-permute-start.25 = (f32[256,128]{1,0:T(8,128)}, f32[256,128]{1,0:T(8,128)S(1)}, u32[]{:S(2)}, u32[]{:S(2)}) collective-permute-start(f32[256,128]{1,0:T(8,128)} %get-tuple-element.45), channel_id=1, source_target_pairs={{0,6},{1,7},{2,4},{3,5},{4,2},{5,3},{6,0},{7,1},{8,14},{9,15},{10,... | collective-permute-start | bytes 393224 | tf_op jit(solution)/shard_map/ppermute | solution.py:528
  249.2 2.0 copy-start.24
  251.2 0.6 copy-start.25
  251.2 0.7 copy-start.26
  259.0 1.0 copy-start.6
  259.1 2.0 collective-permute-start.26
  280.8 1.2 collective-permute-start.27
  282.7 3.6 %collective-permute-start.28 = (f32[4,6]{1,0:T(4,128)S(1)}, f32[4,6]{1,0:T(4,128)S(1)}, u32[]{:S(2)}, u32[]{:S(2)}) collective-permute-start(f32[4,6]{1,0:T(4,128)S(1)} %get-tuple-element.65), channel_id=1, source_target_pairs={{0,2},{1,3},{2,0},{3,1},{4,6},{5,7},{6,4},{7,5},{8,10},{9,11},{10,... | collective-permute-start | bytes 296 | tf_op jit(solution)/shard_map/ppermute | solution.py:558
  284.5 3.6 %collective-permute-start.29 = (f32[4,6]{1,0:T(4,128)S(1)}, f32[4,6]{1,0:T(4,128)S(1)}, u32[]{:S(2)}, u32[]{:S(2)}) collective-permute-start(f32[4,6]{1,0:T(4,128)S(1)} %get-tuple-element.67), channel_id=1, source_target_pairs={{0,4},{1,5},{2,6},{3,7},{4,0},{5,1},{6,2},{7,3},{8,12},{9,13},{10,... | collective-permute-start | bytes 296 | tf_op jit(solution)/shard_map/ppermute | solution.py:558
  284.8 4.5 %collective-permute-start.30 = (f32[4,6]{1,0:T(4,128)S(1)}, f32[4,6]{1,0:T(4,128)S(1)}, u32[]{:S(2)}, u32[]{:S(2)}) collective-permute-start(f32[4,6]{1,0:T(4,128)S(1)} %get-tuple-element.66), channel_id=1, source_target_pairs={{0,6},{1,7},{2,4},{3,5},{4,2},{5,3},{6,0},{7,1},{8,14},{9,15},{10,... | collective-permute-start | bytes 296 | tf_op jit(solution)/shard_map/ppermute | solution.py:558
